TPU v7x, 32 devices: a whole 2x2x4 slice. The times are simulated.
32 devices in a mesh: groups: 2 (over y), ctx: 4 (over z), section: 2 (over x), mp: 2 (over core).
Axes of the slice: x: 2, y: 2, z: 4, core: 2. Of those that a mesh axis runs over, the one named last changes fastest.
Arguments:
- spans: bfloat16 [2, 1024, 6144], P('section', ('groups', 'ctx'), 'mp'), parts along dimension 1, may hold values from -6 to 6
- norm_gain: float32 [2, 6144], P('section', 'mp'), may hold values from 0.25 to 1.75
- w_in: bfloat16 [2, 6144, 3, 4096], P('section', 'mp', None, 'ctx'), may hold values from -0.078125 to 0.078125
- filters: bfloat16 [2, 4096, 128], P('section', 'ctx'), may hold values from -0.5 to 0.5
- w_out: bfloat16 [2, 4096, 6144], P('section', 'ctx', 'mp'), may hold values from -0.09375 to 0.09375
- prompt_len: int32 [4], P(('groups', 'section')), parts along dimension 0, may hold values from 128 to 512
- needles: int32 [2, 128], P('section', 'groups'), parts along dimension 1, may hold values from 0 to 511
Outputs:
- advanced: bfloat16 [2, 1024, 6144], P('section', ('groups', 'ctx'), 'mp'), parts along dimension 1
- needle_states: bfloat16 [2, 128, 4096], P('section', 'groups', 'ctx'), parts along dimension 1
There are 2 independent parts, one for each index of `groups`. A program takes and returns all parts, laid end to end along the dimension named above; an argument that names none is the same for every part. Nothing has to cross between parts.
All inputs are finite; a program needn't handle non-finite values.
Results may differ from a plain program's by a relative error of at most 0.02.
Values may be sent and summed in bfloat16 or wider, within the bound.
No kernel may reach another device: no remote copies, remote signals or barrier semaphores. Data moves between devices by JAX's collectives and lax.ppermute only.
A program may use at most 256 MiB of HBM per device.

v0:
```python
import functools

import jax
import jax.numpy as jnp
import ml_dtypes
import numpy as np
from jax import lax
from jax.experimental import pallas as pl
from jax.experimental.pallas import tpu as pltpu
from jax.sharding import PartitionSpec as P


norm_eps = 1e-06
lanes = 128
halves = 2
vmem_limit = 40 * 1024 * 1024


def tile_of(extent, most):
    tile = min(extent, most)
    while extent % tile:
        tile //= 2
    return tile


def smem():
    return pl.BlockSpec(memory_space=pltpu.SMEM)


def params():
    return pltpu.CompilerParams(vmem_limit_bytes=vmem_limit)


def project_kernel(merged, parts, line, first, final, table_ref, gain_ref, *refs):
    step = pl.program_id(0)
    x_refs = refs[:parts]
    carry_ref = None if first else refs[parts]
    w_ref, _, out_ref, scaled, stat = refs[parts + (0 if first else 1) :]
    tile = out_ref.shape[1]
    busy = table_ref[line, 4] > 0
    last = step == pl.num_programs(0) - 1

    @pl.when(busy & (step == 0))
    def _():
        streams = parts // 2 if merged else parts
        chunk = x_refs[0].shape[0]
        for index in range(streams):
            x = x_refs[index][...].astype(jnp.float32)
            if merged:
                x = x + x_refs[streams + index][...].astype(jnp.float32)
            place = slice(index * chunk, (index + 1) * chunk)
            scaled[place, :] = (x * gain_ref[...]).astype(jnp.bfloat16)
            stat[place, :] = jnp.broadcast_to(jnp.sum(x * x, axis=1, keepdims=True), (chunk, lanes))

    @pl.when(busy & jnp.logical_not(last))
    def _():
        total = jnp.dot(scaled[...], w_ref[0], preferred_element_type=jnp.float32)
        if not first:
            total = total + carry_ref[...]
        out_ref[...] = total.astype(out_ref.dtype)

    @pl.when(busy & last)
    def _():
        squares = stat[...]
        if not first:
            squares = squares + carry_ref[:, :lanes]
        if final:
            high = squares.astype(jnp.bfloat16).astype(jnp.float32)
            column = lax.broadcasted_iota(jnp.int32, squares.shape, 1)
            squares = jnp.where(column == 0, high, jnp.where(column == 1, squares - high, 0.0))
        out_ref[:, :lanes] = squares.astype(out_ref.dtype)
        if tile > lanes:
            out_ref[:, lanes:] = jnp.zeros((out_ref.shape[0], tile - lanes), out_ref.dtype)

    @pl.when(jnp.logical_not(busy))
    def _():
        out_ref[...] = jnp.zeros_like(out_ref)


def project(pieces, merged, table, line, gain, w, part, carry, final, after):
    streams, _, channels = w.shape
    rows_each, depth = pieces[0].shape
    rows = rows_each * (len(pieces) // 2 if merged else len(pieces))
    tile = tile_of(channels, 1024)
    per = channels // tile
    steps = streams * per
    first = carry is None

    def weights(i):
        j = jnp.minimum(i, steps - 1)
        return (j // per, part, j % per)

    column = pl.BlockSpec((rows, tile), lambda i: (0, i))
    return pl.pallas_call(
        functools.partial(project_kernel, merged, len(pieces), line, first, final),
        grid=(steps + 1,),
        in_specs=[smem(), pl.BlockSpec((1, depth), lambda i: (0, part))]
        + [pl.BlockSpec((rows_each, depth), lambda i: (0, 0))] * len(pieces)
        + ([] if first else [column])
        + [pl.BlockSpec((1, depth, tile), weights), pl.BlockSpec(memory_space=pl.ANY)],
        out_specs=column,
        out_shape=jax.ShapeDtypeStruct(
            (rows, streams * channels + lanes), jnp.bfloat16 if final else jnp.float32
        ),
        scratch_shapes=[pltpu.VMEM((rows, depth), jnp.bfloat16), pltpu.VMEM((rows, lanes), jnp.float32)],
        compiler_params=params(),
        cost_estimate=pl.CostEstimate(
            flops=2 * rows * depth * streams * channels,
            bytes_accessed=2 * streams * depth * channels,
            transcendentals=0,
        ),
        name="project",
    )(table, gain, *pieces, *(() if first else (carry,)), w, after)


def wave_tables(rows):
    window = 2 * rows
    angle = np.pi / window * (2 * np.arange(rows)[:, None] + 1) * np.arange(window)[None, :]
    forward = np.concatenate([np.cos(angle), np.sin(angle)], axis=0)
    inverse = forward[:, rows:].T * (2.0 / window)

    def pair(matrix):
        exact = jnp.asarray(matrix, jnp.float32)
        high = jnp.asarray(np.asarray(matrix, ml_dtypes.bfloat16))
        low = jnp.asarray(np.asarray(matrix - np.asarray(matrix, ml_dtypes.bfloat16).astype(np.float64), ml_dtypes.bfloat16))
        return high, low

    high, low = pair(forward)
    inverse_high, inverse_low = pair(inverse)
    return jnp.concatenate([high, low], axis=0), jnp.concatenate([inverse_high, inverse_low], axis=0)


def spectrum_kernel(taps_ref, forward_ref, _, out_ref):
    taps = taps_ref.shape[1]
    both = lax.dot_general(
        forward_ref[:, :taps], taps_ref[...], (((1,), (1,)), ((), ())), preferred_element_type=jnp.float32
    )
    half = out_ref.shape[0]
    out_ref[...] = both[:half, :] + both[half:, :]


def spectrum(taps, forward, after):
    channels = taps.shape[0]
    tile = tile_of(channels, 256)
    window = forward.shape[1]
    return pl.pallas_call(
        spectrum_kernel,
        grid=(channels // tile,),
        in_specs=[
            pl.BlockSpec((tile, taps.shape[1]), lambda i: (i, 0)),
            pl.BlockSpec(forward.shape, lambda i: (0, 0)),
            pl.BlockSpec(memory_space=pl.ANY),
        ],
        out_specs=pl.BlockSpec((window, tile), lambda i: (0, i)),
        out_shape=jax.ShapeDtypeStruct((window, channels), jnp.float32),
        compiler_params=params(),
        name="spectrum",
    )(taps, forward, after)


def mix_kernel(full_width, line, table_ref, *refs):
    q0, k0, v0, s0, q1, k1, v1, s1, pk0, pv0, ps0, pk1, pv1, ps1, f_ref, forward_ref, inverse_ref, _, out_ref, window = refs
    rows = out_ref.shape[0]
    block = table_ref[line, 0]
    length = table_ref[line, 1]
    work = table_ref[line, 2] > 0

    def joined(a_ref, b_ref):
        return a_ref[...].astype(jnp.float32) + b_ref[...].astype(jnp.float32)

    def inverse_norm(a_ref, b_ref):
        mean = jnp.sum(joined(a_ref, b_ref), axis=1, keepdims=True) / full_width
        return lax.rsqrt(mean + norm_eps)

    @pl.when(work)
    def _():
        row = lax.broadcasted_iota(jnp.int32, (rows, 1), 0)
        scale = inverse_norm(s0, s1)
        live = (row + block * rows < length).astype(jnp.float32)
        here = joined(k0, k1) * scale * (joined(v0, v1) * scale) * live
        window[rows:, :] = here.astype(jnp.bfloat16)

        @pl.when(table_ref[line, 3] > 0)
        def _():
            scale = inverse_norm(ps0, ps1)
            live = (row + (block - 1) * rows < length).astype(jnp.float32)
            before = joined(pk0, pk1) * scale * (joined(pv0, pv1) * scale) * live
            window[:rows, :] = before.astype(jnp.bfloat16)

        @pl.when(table_ref[line, 3] == 0)
        def _():
            window[:rows, :] = jnp.zeros((rows, window.shape[1]), jnp.bfloat16)

        both = jnp.dot(forward_ref[...], window[...], preferred_element_type=jnp.float32)
        cosine = both[:rows, :] + both[2 * rows : 3 * rows, :]
        sine = both[rows : 2 * rows, :] + both[3 * rows :, :]
        f_cosine = f_ref[:rows, :]
        f_sine = f_ref[rows:, :]
        product = jnp.concatenate(
            [cosine * f_cosine - sine * f_sine, cosine * f_sine + sine * f_cosine], axis=0
        )
        high = product.astype(jnp.bfloat16)
        low = (product - high.astype(jnp.float32)).astype(jnp.bfloat16)
        back = jnp.dot(inverse_ref[...], high, preferred_element_type=jnp.float32)
        conv = back[:rows, :] + back[rows:, :]
        conv = conv + jnp.dot(inverse_ref[:rows, :], low, preferred_element_type=jnp.float32)
        out_ref[...] = (joined(q0, q1) * scale * conv * live).astype(jnp.bfloat16)

    @pl.when(jnp.logical_not(work))
    def _():
        out_ref[...] = jnp.zeros_like(out_ref)


def mix(table, line, here, before, rows, waves, filter_waves, full_width, after):
    own, got, at = here
    own_before, got_before, at_before = before
    forward, inverse = waves
    channels = filter_waves.shape[1]
    tile = tile_of(channels, 256)
    per = channels // tile
    streams = 3

    def spec(at, stream):
        return pl.BlockSpec((rows, tile), lambda i: (at, stream * per + i))

    def stat(at):
        return pl.BlockSpec((rows, lanes), lambda i: (at, streams * (channels // lanes)))

    whole = [pl.BlockSpec(wave.shape, lambda i: (0, 0)) for wave in waves]
    return pl.pallas_call(
        functools.partial(mix_kernel, full_width, line),
        grid=(per,),
        in_specs=[smem()]
        + [spec(at, 0), spec(at, 1), spec(at, 2), stat(at)] * 2
        + [spec(at_before, 1), spec(at_before, 2), stat(at_before)] * 2
        + [pl.BlockSpec((2 * rows, tile), lambda i: (0, i))]
        + whole
        + [pl.BlockSpec(memory_space=pl.ANY)],
        out_specs=pl.BlockSpec((rows, tile), lambda i: (0, i)),
        out_shape=jax.ShapeDtypeStruct((rows, channels), jnp.bfloat16),
        scratch_shapes=[pltpu.VMEM((2 * rows, tile), jnp.bfloat16)],
        compiler_params=params(),
        cost_estimate=pl.CostEstimate(
            flops=16 * rows * rows * channels, bytes_accessed=32 * rows * channels, transcendentals=0
        ),
        name="mix",
    )(
        table, own, own, own, own, got, got, got, got,
        own_before, own_before, own_before, got_before, got_before, got_before,
        filter_waves, forward, inverse, after,
    )


def emit_kernel(line, table_ref, gated_ref, w_ref, _, *out_refs):
    work = table_ref[line, 2] > 0
    chunk = out_refs[0].shape[0]

    @pl.when(work)
    def _():
        product = jnp.dot(gated_ref[...], w_ref[...], preferred_element_type=jnp.float32).astype(jnp.bfloat16)
        for index, out_ref in enumerate(out_refs):
            out_ref[...] = product[index * chunk : (index + 1) * chunk, :]

    @pl.when(jnp.logical_not(work))
    def _():
        for out_ref in out_refs:
            out_ref[...] = jnp.zeros_like(out_ref)


def emit(table, line, gated, w, after):
    rows, channels = gated.shape
    width = w.shape[1]
    tile = tile_of(width, 1024)
    chunk = rows // halves
    return pl.pallas_call(
        functools.partial(emit_kernel, line),
        grid=(width // tile,),
        in_specs=[
            smem(),
            pl.BlockSpec((rows, channels), lambda i: (0, 0)),
            pl.BlockSpec((channels, tile), lambda i: (0, i)),
            pl.BlockSpec(memory_space=pl.ANY),
        ],
        out_specs=[pl.BlockSpec((chunk, tile), lambda i: (0, i))] * halves,
        out_shape=[jax.ShapeDtypeStruct((chunk, width), jnp.bfloat16)] * halves,
        compiler_params=params(),
        cost_estimate=pl.CostEstimate(
            flops=2 * rows * channels * width, bytes_accessed=2 * channels * width, transcendentals=0
        ),
        name="emit",
    )(table, gated, w, after)


def added(*terms):
    total = terms[0].astype(jnp.float32)
    for term in terms[1:]:
        total = total + term.astype(jnp.float32)
    return total.astype(jnp.bfloat16)


def layer(spans, norm_gain, w_in, filters, w_out, prompt_len, needles):
    count = lax.axis_size("ctx")
    place = lax.axis_index("ctx")
    x_local = spans[0]
    rows, half_width = x_local.shape
    chunk = rows // halves
    full_width = half_width * lax.axis_size("mp")
    weights = jnp.swapaxes(w_in[0], 0, 1)
    gain = norm_gain
    up = [(source, source + 1) for source in range(count - 1)]
    down = [(source + 1, source) for source in range(count - 1)]
    partner = [(0, 1), (1, 0)] if lax.axis_size("mp") == 2 else None

    far = count - 1
    order = [("d", 0)] + [(kind, k) for k in range(1, far) for kind in "du"] + [("m", far)]
    line = {slot: index for index, slot in enumerate(order)}
    z = place.astype(jnp.int32)
    reach = jnp.array([k for _, k in order], jnp.int32)
    kinds = jnp.array(["dum".index(kind) for kind, _ in order], jnp.int32)
    downward = (kinds == 0) | ((kinds == 2) & (z == 0))
    blocks = jnp.where(downward, z + reach, z - reach)
    work = (blocks >= 0) & (blocks < count)
    busy = (z - reach >= 0) | (z + reach < count)
    table = jnp.stack(
        [blocks, jnp.broadcast_to(prompt_len[0], blocks.shape), work, (blocks >= 1) & work, busy], axis=1
    ).astype(jnp.int32)

    part = half_width // halves
    waves = wave_tables(rows)
    pieces = [x_local[:, i * part : (i + 1) * part] for i in range(halves)]
    gathered = {("d", 0): pieces, ("u", 0): pieces}
    for k in range(1, count):
        gathered["u", k] = []
        gathered["d", k] = []
        for i in range(halves):
            value = lax.ppermute(gathered["u", k - 1][i], "ctx", [(a, b) for a, b in up if a >= k - 1])
            gathered["u", k].append(value)
            value = lax.ppermute(gathered["d", k - 1][i], "ctx", [(a, b) for a, b in down if a <= count - k])
            gathered["d", k].append(value)

    after = x_local
    held = {}

    def offer(k, own):
        merged = 2 * k >= count
        got = lax.ppermute(own, "mp", partner)
        held["u", k] = (own, got, 0)
        held["d", k] = (own, got, 0 if merged or k == 0 else 1)

    gated = {}
    sums = {}

    def blend(kind, k, after):
        before = ("u", k + 1) if kind == "u" or k == 0 else ("d", k - 1)
        gated[kind, k] = mix(
            table, line[kind, k], held["d" if kind == "m" else kind, k], held[before],
            rows, waves, filter_waves, full_width, after,
        )
        sums[kind, k] = emit(table, line[kind, k], gated[kind, k], w_out[0], gated[kind, k])
        return sums[kind, k][0]

    after = project([x_local], False, table, 0, gain, weights, 0, None, True, after)
    offer(0, after)
    filter_waves = spectrum(filters[0], waves[0], after)
    after = filter_waves
    for k in range(1, count):
        slot = ("d", k) if k < far else ("m", far)
        carry = None
        for i in range(halves):
            after = project(
                [gathered["u", k][i], gathered["d", k][i]],
                2 * k >= count, table, line[slot], gain, weights, i, carry, i == halves - 1, after,
            )
            carry = after
        offer(k, after)
    after = blend("m", far, after)
    for k in range(far - 1, 0, -1):
        after = blend("u", k, after)
        after = blend("d", k, after)
    after = blend("d", 0, after)

    def reduce_step(values, pairs):
        moved = []
        for value in values:
            moved.append(lax.ppermute(value, "ctx", pairs))
        return moved

    terms = [sums["d", 0]]
    for k in range(far, 0, -1):
        to_up = [(a, b) for a, b in up if a + k <= far]
        to_down = [(a, b) for a, b in down if a >= k]
        if k == far and far != 2:
            arrived = [reduce_step(sums["m", far], to_up + to_down)] * 2
        else:
            from_up, from_down = ("m", "m") if k == far else ("d", "u")
            arrived = [reduce_step(sums[from_up, k], to_up), reduce_step(sums[from_down, k], to_down)]
        if k > 1:
            for kind, moved in zip("du", arrived):
                sums[kind, k - 1] = [added(a, b) for a, b in zip(sums[kind, k - 1], moved)]
        else:
            terms += arrived if far > 1 else arrived[:1]
    pieces = [x_local[i * chunk : (i + 1) * chunk] for i in range(halves)]
    sections = lax.axis_size("section")
    turn = [(source, (source + 1) % sections) for source in range(sections)]
    final = [added(*parts) for parts in zip(pieces, *terms)]
    advanced = jnp.concatenate([lax.ppermute(v, "section", turn) for v in final], axis=0)[None]

    row = jnp.arange(rows, dtype=jnp.int32)
    picked = None
    for slot in order:
        one_hot = (needles[0][:, None] == (row + blocks[line[slot]] * rows)[None, :]).astype(jnp.bfloat16)
        term = jnp.dot(one_hot, gated[slot], preferred_element_type=jnp.float32)
        picked = term if picked is None else picked + term
    return (advanced, picked.astype(jnp.bfloat16)[None])


def solution(mesh):
    return jax.shard_map(
        layer,
        mesh=mesh,
        in_specs=(
            P("section", ("groups", "ctx"), "mp"),
            P("section", "mp"),
            P("section", "mp", None, "ctx"),
            P("section", "ctx", None),
            P("section", "ctx", "mp"),
            P(("groups", "section")),
            P("section", "groups"),
        ),
        out_specs=(P("section", ("groups", "ctx"), "mp"), P("section", "groups", "ctx")),
        check_vma=False,
    )
```

profile of v0, /device:TPU:0, one launch (start us, length us, event | category | flops | bytes accessed | tf_op | source)
XLA Modules:
  0.0 174.7 jit_solution(14049352838391253930)
XLA Ops:
  0.6 1.2 fusion.41
  1.9 5.0 %collective-permute-start.1 = (bf16[128,1536]{1,0:T(8,128)(2,1)S(1)}, bf16[128,1536]{1,0:T(8,128)(2,1)S(1)}, u32[]{:S(2)}, u32[]{:S(2)}) collective-permute-start(bf16[128,1536]{1,0:T(8,128)(2,1)S(1)} %get-tuple-element.31), channel_id=1, source_target_pairs={{0,4},{4,8},{8,12},{1,5},{5,9},{9,13},{2,6},{6,10},{10,14},{3,7},{... | collective-permute-start | bytes 1179656 | tf_op jit(solution)/shard_map/ppermute | solution.py:336
  6.9 1.3 collective-permute-start.2
  8.2 4.6 %collective-permute-start.3 = (bf16[128,1536]{1,0:T(8,128)(2,1)S(1)}, bf16[128,1536]{1,0:T(8,128)(2,1)S(1)}, u32[]{:S(2)}, u32[]{:S(2)}) collective-permute-start(bf16[128,1536]{1,0:T(8,128)(2,1)S(1)} %get-tuple-element.30), channel_id=1, source_target_pairs={{0,4},{4,8},{8,12},{1,5},{5,9},{9,13},{2,6},{6,10},{10,14},{3,7},{... | collective-permute-start | bytes 1179656 | tf_op jit(solution)/shard_map/ppermute | solution.py:336
  12.8 1.3 collective-permute-start.4
  17.0 3.7 %collective-permute-done.2.refs_1_ = bf16[128,1536]{1,0:T(8,128)(2,1)S(1)} collective-permute-done((bf16[128,1536]{1,0:T(8,128)(2,1)S(1)}, bf16[128,1536]{1,0:T(8,128)(2,1)S(1)}, u32[]{:S(2)}, u32[]{:S(2)}) %collective-permute-start.2) | collective-permute-done | bytes 393248 | tf_op jit(solution)/shard_map/ppermute | solution.py:338
  20.8 1.3 collective-permute-start.7
  22.0 1.6 collective-permute-done.3.refs_0_
  24.3 4.9 %collective-permute-done.4.refs_1_ = bf16[128,1536]{1,0:T(8,128)(2,1)S(1)} collective-permute-done((bf16[128,1536]{1,0:T(8,128)(2,1)S(1)}, bf16[128,1536]{1,0:T(8,128)(2,1)S(1)}, u32[]{:S(2)}, u32[]{:S(2)}) %collective-permute-start.4) | collective-permute-done | bytes 393248 | tf_op jit(solution)/shard_map/ppermute | solution.py:338
  29.2 1.3 collective-permute-start.9
  30.5 8.3 %project.7._.refs_8_.refs_9_.refs_10_.refs_0_.refs_1_.refs_2_.refs_3_ = bf16[128,3200]{1,0:T(8,128)(2,1)S(1)} custom-call(s32[6,5]{1,0:T(8,128)S(1)} %stack.31.table_ref, f32[1,3072]{1,0:T(1,128)S(1)} %copy-done.3, bf16[128,3072]{1,0:T(8,128)(2,1)S(1)} %bitcast.47, bf16[3,3072,1024]{2,1,0:T(8,128)(2,1)} %bitcast.50, bf16[128,3072]{1,0:T(8,128)(2,1)S(1)} %bitcast.48), custom_call_target="tpu_custom_call" | custom-call | flops 2415919104 | bytes 18874368 | tf_op jit(solution)/shard_map/project/pallas_call | solution.py:94
  38.9 1.0 spectrum.1.refs_3_.refs_14_
  39.9 6.5 %project.8.refs_2_.refs_4_ = f32[256,3200]{1,0:T(8,128)S(1)} custom-call(s32[6,5]{1,0:T(8,128)S(1)} %stack.31.table_ref, f32[1,3072]{1,0:T(1,128)S(1)} %copy-done.3, bf16[128,1536]{1,0:T(8,128)(2,1)S(1)} %collective-permute-done.3.refs_0_, bf16[128,1536]{1,0:T(8,128)(2,1)S(1)} %collective-permute-done.4.refs_1_, bf16[3,3072,1024]{2,1,0:T(8,128)(2,1)} %bitcast.51, ...), custom_call_target="tpu_custom_call" | custom-call | flops 2415919104 | bytes 9437184 | tf_op jit(solution)/shard_map/project/pallas_call | solution.py:94
  47.1 1.3 collective-permute-start.12
  49.1 1.3 collective-permute-start.14
  50.4 6.6 %project.9.refs_3_.refs_8_.refs_9_.refs_10_.refs_0_.refs_1_.refs_2_ = bf16[256,3200]{1,0:T(8,128)(2,1)S(1)} custom-call(s32[6,5]{1,0:T(8,128)S(1)} %stack.31.table_ref, f32[1,3072]{1,0:T(1,128)S(1)} %copy-done.3, bf16[128,1536]{1,0:T(8,128)(2,1)S(1)} %collective-permute-done.1.refs_0_, bf16[128,1536]{1,0:T(8,128)(2,1)S(1)} %collective-permute-done.2.refs_1_, ...), custom_call_target="tpu_custom_call" | custom-call | flops 2415919104 | bytes 9437184 | tf_op jit(solution)/shard_map/project/pallas_call | solution.py:94
  57.1 5.5 %project.10.refs_2_.refs_4_ = f32[128,3200]{1,0:T(8,128)S(1)} custom-call(s32[6,5]{1,0:T(8,128)S(1)} %stack.31.table_ref, f32[1,3072]{1,0:T(1,128)S(1)} %copy-done.3, bf16[128,1536]{1,0:T(8,128)(2,1)S(1)} %collective-permute-done.8.refs_0_, bf16[128,1536]{1,0:T(8,128)(2,1)S(1)} %collective-permute-done.9.refs_1_, bf16[3,3072,1024]{2,1,0:T(8,128)(2,1)} %bitcast.53, ...), custom_call_target="tpu_custom_call" | custom-call | flops 1207959552 | bytes 9437184 | tf_op jit(solution)/shard_map/project/pallas_call | solution.py:94
  62.7 5.6 %project.11.refs_3_.refs_8_.refs_9_.refs_10_.refs_0_.refs_1_.refs_2_ = bf16[128,3200]{1,0:T(8,128)(2,1)S(1)} custom-call(s32[6,5]{1,0:T(8,128)S(1)} %stack.31.table_ref, f32[1,3072]{1,0:T(1,128)S(1)} %copy-done.3, bf16[128,1536]{1,0:T(8,128)(2,1)S(1)} %collective-permute-done.6.refs_0_, bf16[128,1536]{1,0:T(8,128)(2,1)S(1)} %collective-permute-done.7.refs_1_, ...), custom_call_target="tpu_custom_call" | custom-call | flops 1207959552 | bytes 9437184 | tf_op jit(solution)/shard_map/project/pallas_call | solution.py:94
  68.9 5.8 %project.12.refs_2_.refs_4_ = f32[128,3200]{1,0:T(8,128)S(1)} custom-call(s32[6,5]{1,0:T(8,128)S(1)} %stack.31.table_ref, f32[1,3072]{1,0:T(1,128)S(1)} %copy-done.3, bf16[128,1536]{1,0:T(8,128)(2,1)S(1)} %collective-permute-done.13.refs_0_, bf16[128,1536]{1,0:T(8,128)(2,1)S(1)} %collective-permute-done.14.refs_1_, bf16[3,3072,1024]{2,1,0:T(8,128)(2,1)} %bitcast.55, ...), custom_call_target="tpu_custom_call" | custom-call | flops 1207959552 | bytes 9437184 | tf_op jit(solution)/shard_map/project/pallas_call | solution.py:94
  74.7 5.8 %project.13.refs_0_.refs_1_.refs_2_.refs_3_.refs_17_.refs_8_.refs_9_.refs_10_ = bf16[128,3200]{1,0:T(8,128)(2,1)S(1)} custom-call(s32[6,5]{1,0:T(8,128)S(1)} %stack.31.table_ref, f32[1,3072]{1,0:T(1,128)S(1)} %copy-done.3, bf16[128,1536]{1,0:T(8,128)(2,1)S(1)} %collective-permute-done.11.refs_0_, bf16[128,1536]{1,0:T(8,128)(2,1)S(1)} %collective-permute-done.12.refs_1_, ...), custom_call_target="tpu_custom_call" | custom-call | flops 1207959552 | bytes 9437184 | tf_op jit(solution)/shard_map/project/pallas_call | solution.py:94
  85.6 5.0 %mix.6.gated_ref._ = bf16[128,1024]{1,0:T(8,128)(2,1)S(1)} custom-call(s32[6,5]{1,0:T(8,128)S(1)} %stack.31.table_ref, bf16[128,3200]{1,0:T(8,128)(2,1)S(1)} %project.13.refs_0_.refs_1_.refs_2_.refs_3_.refs_17_.refs_8_.refs_9_.refs_10_, bf16[128,3200]{1,0:T(8,128)(2,1)S(1)} %project.13.refs_0_.refs_1_.refs_2_.refs_3_.refs_17_.refs_8_.refs_9_.refs_10_, ...), custom_call_target="tpu_custom_call" | custom-call | flops 268435456 | bytes 4194304 | tf_op jit(solution)/shard_map/mix/pallas_call | solution.py:230
  90.7 2.4 %emit.6 = (bf16[64,3072]{1,0:T(8,128)(2,1)S(1)}, bf16[64,3072]{1,0:T(8,128)(2,1)S(1)}) custom-call(s32[6,5]{1,0:T(8,128)S(1)} %stack.31.table_ref, bf16[128,1024]{1,0:T(8,128)(2,1)S(1)} %mix.6.gated_ref._, bf16[1024,3072]{1,0:T(8,128)(2,1)S(1)} %bitcast.40, bf16[128,1024]{1,0:T(8,128)(2,1)S(1)} %mix.6.gated_ref._), custom_call_target="tpu_custom_call" | custom-call | flops 805306368 | bytes 6291456 | tf_op jit(solution)/shard_map/emit/pallas_call | solution.py:275
  93.1 1.3 collective-permute-start.16
  94.4 1.5 collective-permute-start.22
  95.9 2.0 %mix.7.gated_ref._ = bf16[128,1024]{1,0:T(8,128)(2,1)S(1)} custom-call(s32[6,5]{1,0:T(8,128)S(1)} %stack.31.table_ref, bf16[128,3200]{1,0:T(8,128)(2,1)S(1)} %project.11.refs_3_.refs_8_.refs_9_.refs_10_.refs_0_.refs_1_.refs_2_, bf16[128,3200]{1,0:T(8,128)(2,1)S(1)} %project.11.refs_3_.refs_8_.refs_9_.refs_10_.refs_0_.refs_1_.refs_2_, ...), custom_call_target="tpu_custom_call" | custom-call | flops 268435456 | bytes 4194304 | tf_op jit(solution)/shard_map/mix/pallas_call | solution.py:230
  98.4 1.1 emit.7
  99.5 5.0 %mix.8.gated_ref._ = bf16[128,1024]{1,0:T(8,128)(2,1)S(1)} custom-call(s32[6,5]{1,0:T(8,128)S(1)} %stack.31.table_ref, bf16[128,3200]{1,0:T(8,128)(2,1)S(1)} %project.11.refs_3_.refs_8_.refs_9_.refs_10_.refs_0_.refs_1_.refs_2_, bf16[128,3200]{1,0:T(8,128)(2,1)S(1)} %project.11.refs_3_.refs_8_.refs_9_.refs_10_.refs_0_.refs_1_.refs_2_, ...), custom_call_target="tpu_custom_call" | custom-call | flops 268435456 | bytes 4194304 | tf_op jit(solution)/shard_map/mix/pallas_call | solution.py:230
  104.5 2.4 %emit.8 = (bf16[64,3072]{1,0:T(8,128)(2,1)S(1)}, bf16[64,3072]{1,0:T(8,128)(2,1)S(1)}) custom-call(s32[6,5]{1,0:T(8,128)S(1)} %stack.31.table_ref, bf16[128,1024]{1,0:T(8,128)(2,1)S(1)} %mix.8.gated_ref._, bf16[1024,3072]{1,0:T(8,128)(2,1)S(1)} %bitcast.42, bf16[128,1024]{1,0:T(8,128)(2,1)S(1)} %mix.8.gated_ref._), custom_call_target="tpu_custom_call" | custom-call | flops 805306368 | bytes 6291456 | tf_op jit(solution)/shard_map/emit/pallas_call | solution.py:275
  107.0 2.0 %mix.9.gated_ref._ = bf16[128,1024]{1,0:T(8,128)(2,1)S(1)} custom-call(s32[6,5]{1,0:T(8,128)S(1)} %stack.31.table_ref, bf16[256,3200]{1,0:T(8,128)(2,1)S(1)} %project.9.refs_3_.refs_8_.refs_9_.refs_10_.refs_0_.refs_1_.refs_2_, bf16[256,3200]{1,0:T(8,128)(2,1)S(1)} %project.9.refs_3_.refs_8_.refs_9_.refs_10_.refs_0_.refs_1_.refs_2_, ...), custom_call_target="tpu_custom_call" | custom-call | flops 268435456 | bytes 4194304 | tf_op jit(solution)/shard_map/mix/pallas_call | solution.py:230
  109.0 1.1 emit.9
  110.1 5.0 %mix.10.gated_ref._ = bf16[128,1024]{1,0:T(8,128)(2,1)S(1)} custom-call(s32[6,5]{1,0:T(8,128)S(1)} %stack.31.table_ref, bf16[256,3200]{1,0:T(8,128)(2,1)S(1)} %project.9.refs_3_.refs_8_.refs_9_.refs_10_.refs_0_.refs_1_.refs_2_, bf16[256,3200]{1,0:T(8,128)(2,1)S(1)} %project.9.refs_3_.refs_8_.refs_9_.refs_10_.refs_0_.refs_1_.refs_2_, ...), custom_call_target="tpu_custom_call" | custom-call | flops 268435456 | bytes 4194304 | tf_op jit(solution)/shard_map/mix/pallas_call | solution.py:230
  115.1 2.4 %emit.10 = (bf16[64,3072]{1,0:T(8,128)(2,1)S(1)}, bf16[64,3072]{1,0:T(8,128)(2,1)S(1)}) custom-call(s32[6,5]{1,0:T(8,128)S(1)} %stack.31.table_ref, bf16[128,1024]{1,0:T(8,128)(2,1)S(1)} %mix.10.gated_ref._, bf16[1024,3072]{1,0:T(8,128)(2,1)S(1)} %bitcast.44, bf16[128,1024]{1,0:T(8,128)(2,1)S(1)} %mix.10.gated_ref._), custom_call_target="tpu_custom_call" | custom-call | flops 805306368 | bytes 6291456 | tf_op jit(solution)/shard_map/emit/pallas_call | solution.py:275
  118.4 2.2 %collective-permute-start.17 = (bf16[64,3072]{1,0:T(8,128)(2,1)S(1)}, bf16[64,3072]{1,0:T(8,128)(2,1)S(1)}, u32[]{:S(2)}, u32[]{:S(2)}) collective-permute-start(bf16[64,3072]{1,0:T(8,128)(2,1)S(1)} %get-tuple-element.32), channel_id=1, source_target_pairs={{0,4},{4,8},{1,5},{5,9},{2,6},{6,10},{3,7},{7,11},{16,20},{20,24},... | collective-permute-start | bytes 1179656 | tf_op jit(solution)/shard_map/ppermute | solution.py:385
  121.5 5.2 %collective-permute-start.23 = (bf16[64,3072]{1,0:T(8,128)(2,1)S(1)}, bf16[64,3072]{1,0:T(8,128)(2,1)S(1)}, u32[]{:S(2)}, u32[]{:S(2)}) collective-permute-start(bf16[64,3072]{1,0:T(8,128)(2,1)S(1)} %get-tuple-element.34), channel_id=1, source_target_pairs={{0,4},{4,8},{1,5},{5,9},{2,6},{6,10},{3,7},{7,11},{16,20},{20,24},... | collective-permute-start | bytes 1179656 | tf_op jit(solution)/shard_map/ppermute | solution.py:385
  126.8 1.3 collective-permute-start.20
  128.1 2.0 %collective-permute-done.17 = bf16[64,3072]{1,0:T(8,128)(2,1)S(1)} collective-permute-done((bf16[64,3072]{1,0:T(8,128)(2,1)S(1)}, bf16[64,3072]{1,0:T(8,128)(2,1)S(1)}, u32[]{:S(2)}, u32[]{:S(2)}) %collective-permute-start.17) | collective-permute-done | bytes 393248 | tf_op jit(solution)/shard_map/ppermute | solution.py:385
  130.2 5.2 %collective-permute-start.18 = (bf16[64,3072]{1,0:T(8,128)(2,1)S(1)}, bf16[64,3072]{1,0:T(8,128)(2,1)S(1)}, u32[]{:S(2)}, u32[]{:S(2)}) collective-permute-start(bf16[64,3072]{1,0:T(8,128)(2,1)S(1)} %add_convert_fusion.3), channel_id=1, source_target_pairs={{0,4},{4,8},{8,12},{1,5},{5,9},{9,13},{2,6},{6,10},{10,14},{3,7},{... | collective-permute-start | bytes 1179656 | tf_op jit(solution)/shard_map/ppermute | solution.py:385
  135.5 1.3 collective-permute-start.26
  136.8 1.8 %collective-permute-done.23 = bf16[64,3072]{1,0:T(8,128)(2,1)S(1)} collective-permute-done((bf16[64,3072]{1,0:T(8,128)(2,1)S(1)}, bf16[64,3072]{1,0:T(8,128)(2,1)S(1)}, u32[]{:S(2)}, u32[]{:S(2)}) %collective-permute-start.23) | collective-permute-done | bytes 393248 | tf_op jit(solution)/shard_map/ppermute | solution.py:385
  138.6 5.2 %collective-permute-start.24 = (bf16[64,3072]{1,0:T(8,128)(2,1)S(1)}, bf16[64,3072]{1,0:T(8,128)(2,1)S(1)}, u32[]{:S(2)}, u32[]{:S(2)}) collective-permute-start(bf16[64,3072]{1,0:T(8,128)(2,1)S(1)} %add_convert_fusion.1), channel_id=1, source_target_pairs={{0,4},{4,8},{8,12},{1,5},{5,9},{9,13},{2,6},{6,10},{10,14},{3,7},{... | collective-permute-start | bytes 1179656 | tf_op jit(solution)/shard_map/ppermute | solution.py:385
  144.0 4.6 %mix.11.gated_ref._ = bf16[128,1024]{1,0:T(8,128)(2,1)S(1)} custom-call(s32[6,5]{1,0:T(8,128)S(1)} %stack.31.table_ref, bf16[128,3200]{1,0:T(8,128)(2,1)S(1)} %project.7._.refs_8_.refs_9_.refs_10_.refs_0_.refs_1_.refs_2_.refs_3_, bf16[128,3200]{1,0:T(8,128)(2,1)S(1)} %project.7._.refs_8_.refs_9_.refs_10_.refs_0_.refs_1_.refs_2_.refs_3_, ...), custom_call_target="tpu_custom_call" | custom-call | flops 268435456 | bytes 4194304 | tf_op jit(solution)/shard_map/mix/pallas_call | solution.py:230
  148.6 2.4 %emit.11 = (bf16[64,3072]{1,0:T(8,128)(2,1)S(1)}, bf16[64,3072]{1,0:T(8,128)(2,1)S(1)}) custom-call(s32[6,5]{1,0:T(8,128)S(1)} %stack.31.table_ref, bf16[128,1024]{1,0:T(8,128)(2,1)S(1)} %mix.11.gated_ref._, bf16[1024,3072]{1,0:T(8,128)(2,1)S(1)} %bitcast.45, bf16[128,1024]{1,0:T(8,128)(2,1)S(1)} %mix.11.gated_ref._), custom_call_target="tpu_custom_call" | custom-call | flops 805306368 | bytes 6291456 | tf_op jit(solution)/shard_map/emit/pallas_call | solution.py:275
  151.3 3.2 %collective-permute-done.24 = bf16[64,3072]{1,0:T(8,128)(2,1)S(1)} collective-permute-done((bf16[64,3072]{1,0:T(8,128)(2,1)S(1)}, bf16[64,3072]{1,0:T(8,128)(2,1)S(1)}, u32[]{:S(2)}, u32[]{:S(2)}) %collective-permute-start.24) | collective-permute-done | bytes 393248 | tf_op jit(solution)/shard_map/ppermute | solution.py:385
  155.0 1.6 collective-permute-start.27
  157.3 0.9 fusion.5
  158.2 8.8 %collective-permute-done.27 = bf16[64,3072]{1,0:T(8,128)(2,1)S(1)} collective-permute-done((bf16[64,3072]{1,0:T(8,128)(2,1)S(1)}, bf16[64,3072]{1,0:T(8,128)(2,1)S(1)}, u32[]{:S(2)}, u32[]{:S(2)}) %collective-permute-start.27) | collective-permute-done | bytes 393248 | tf_op jit(solution)/shard_map/ppermute | solution.py:406
  167.0 6.7 %collective-permute-done.21 = bf16[64,3072]{1,0:T(8,128)(2,1)S(1)} collective-permute-done((bf16[64,3072]{1,0:T(8,128)(2,1)S(1)}, bf16[64,3072]{1,0:T(8,128)(2,1)S(1)}, u32[]{:S(2)}, u32[]{:S(2)}) %collective-permute-start.21) | collective-permute-done | bytes 393248 | tf_op jit(solution)/shard_map/ppermute | solution.py:406
  173.7 0.9 maximum_bitcast_fusion
  (75 shorter events, 10.5 us)
Async XLA Ops:
  0.6 29.8 %copy-start.1 = (bf16[1,128,3072]{2,1,0:T(8,128)(2,1)S(1)}, bf16[1,128,3072]{2,1,0:T(8,128)(2,1)}, u32[]{:S(2)}) copy-start(bf16[1,128,3072]{2,1,0:T(8,128)(2,1)} %param.13) | copy-start | bytes 2359300
  0.6 29.8 %copy-start.3 = (f32[1,3072]{1,0:T(1,128)S(1)}, f32[1,3072]{1,0:T(1,128)}, u32[]{:S(2)}) copy-start(f32[1,3072]{1,0:T(1,128)} %gain_ref.13) | copy-start | bytes 36868
  1.9 14.4 %collective-permute-start.1 = (bf16[128,1536]{1,0:T(8,128)(2,1)S(1)}, bf16[128,1536]{1,0:T(8,128)(2,1)S(1)}, u32[]{:S(2)}, u32[]{:S(2)}) collective-permute-start(bf16[128,1536]{1,0:T(8,128)(2,1)S(1)} %get-tuple-element.31), channel_id=1, source_target_pairs={{0,4},{4,8},{8,12},{1,5},{5,9},{9,13},{2,6},{6,10},{10,14},{3,7},{... | collective-permute-start | bytes 1179656 | tf_op jit(solution)/shard_map/ppermute | solution.py:336
  6.9 13.9 %collective-permute-start.2 = (bf16[128,1536]{1,0:T(8,128)(2,1)S(1)}, bf16[128,1536]{1,0:T(8,128)(2,1)S(1)}, u32[]{:S(2)}, u32[]{:S(2)}) collective-permute-start(bf16[128,1536]{1,0:T(8,128)(2,1)S(1)} %get-tuple-element.31), channel_id=1, source_target_pairs={{4,0},{8,4},{12,8},{5,1},{9,5},{13,9},{6,2},{10,6},{14,10},{7,3},{... | collective-permute-start | bytes 1179656 | tf_op jit(solution)/shard_map/ppermute | solution.py:338
  8.2 15.5 %collective-permute-start.3 = (bf16[128,1536]{1,0:T(8,128)(2,1)S(1)}, bf16[128,1536]{1,0:T(8,128)(2,1)S(1)}, u32[]{:S(2)}, u32[]{:S(2)}) collective-permute-start(bf16[128,1536]{1,0:T(8,128)(2,1)S(1)} %get-tuple-element.30), channel_id=1, source_target_pairs={{0,4},{4,8},{8,12},{1,5},{5,9},{9,13},{2,6},{6,10},{10,14},{3,7},{... | collective-permute-start | bytes 1179656 | tf_op jit(solution)/shard_map/ppermute | solution.py:336
  12.8 16.4 %collective-permute-start.4 = (bf16[128,1536]{1,0:T(8,128)(2,1)S(1)}, bf16[128,1536]{1,0:T(8,128)(2,1)S(1)}, u32[]{:S(2)}, u32[]{:S(2)}) collective-permute-start(bf16[128,1536]{1,0:T(8,128)(2,1)S(1)} %get-tuple-element.30), channel_id=1, source_target_pairs={{4,0},{8,4},{12,8},{5,1},{9,5},{13,9},{6,2},{10,6},{14,10},{7,3},{... | collective-permute-start | bytes 1179656 | tf_op jit(solution)/shard_map/ppermute | solution.py:338
  16.3 30.0 %collective-permute-start.6 = (bf16[128,1536]{1,0:T(8,128)(2,1)S(1)}, bf16[128,1536]{1,0:T(8,128)(2,1)S(1)}, u32[]{:S(2)}, u32[]{:S(2)}) collective-permute-start(bf16[128,1536]{1,0:T(8,128)(2,1)S(1)} %collective-permute-done.1.refs_0_), channel_id=1, source_target_pairs={{4,8},{8,12},{5,9},{9,13},{6,10},{10,14},{7,11},{11,15},{20,24},{2... | collective-permute-start | bytes 1179656 | tf_op jit(solution)/shard_map/ppermute | solution.py:336
  20.8 26.3 %collective-permute-start.7 = (bf16[128,1536]{1,0:T(8,128)(2,1)S(1)}, bf16[128,1536]{1,0:T(8,128)(2,1)S(1)}, u32[]{:S(2)}, u32[]{:S(2)}) collective-permute-start(bf16[128,1536]{1,0:T(8,128)(2,1)S(1)} %collective-permute-done.2.refs_1_), channel_id=1, source_target_pairs={{4,0},{8,4},{5,1},{9,5},{6,2},{10,6},{7,3},{11,7},{20,16},{24,20},... | collective-permute-start | bytes 1179656 | tf_op jit(solution)/shard_map/ppermute | solution.py:338
  23.6 24.8 %collective-permute-start.8 = (bf16[128,1536]{1,0:T(8,128)(2,1)S(1)}, bf16[128,1536]{1,0:T(8,128)(2,1)S(1)}, u32[]{:S(2)}, u32[]{:S(2)}) collective-permute-start(bf16[128,1536]{1,0:T(8,128)(2,1)S(1)} %collective-permute-done.3.refs_0_), channel_id=1, source_target_pairs={{4,8},{8,12},{5,9},{9,13},{6,10},{10,14},{7,11},{11,15},{20,24},{2... | collective-permute-start | bytes 1179656 | tf_op jit(solution)/shard_map/ppermute | solution.py:336
  29.2 19.9 %collective-permute-start.9 = (bf16[128,1536]{1,0:T(8,128)(2,1)S(1)}, bf16[128,1536]{1,0:T(8,128)(2,1)S(1)}, u32[]{:S(2)}, u32[]{:S(2)}) collective-permute-start(bf16[128,1536]{1,0:T(8,128)(2,1)S(1)} %collective-permute-done.4.refs_1_), channel_id=1, source_target_pairs={{4,0},{8,4},{5,1},{9,5},{6,2},{10,6},{7,3},{11,7},{20,16},{24,20},... | collective-permute-start | bytes 1179656 | tf_op jit(solution)/shard_map/ppermute | solution.py:338
  30.5 8.3 %copy-start = (bf16[512,256]{1,0:T(8,128)(2,1)S(1)}, bf16[512,256]{1,0:T(8,128)(2,1)}, u32[]{:S(2)}) copy-start(bf16[512,256]{1,0:T(8,128)(2,1)} %constant.50.forward_ref.refs_15_) | copy-start | bytes 786436
  30.5 8.3 %copy-start.4 = (bf16[1,1024,128]{2,1,0:T(8,128)(2,1)S(1)}, bf16[1,1024,128]{2,1,0:T(8,128)(2,1)}, u32[]{:S(2)}) copy-start(bf16[1,1024,128]{2,1,0:T(8,128)(2,1)} %param.16) | copy-start | bytes 786436
  46.4 28.3 %collective-permute-start.11 = (bf16[128,1536]{1,0:T(8,128)(2,1)S(1)}, bf16[128,1536]{1,0:T(8,128)(2,1)S(1)}, u32[]{:S(2)}, u32[]{:S(2)}) collective-permute-start(bf16[128,1536]{1,0:T(8,128)(2,1)S(1)} %collective-permute-done.6.refs_0_), channel_id=1, source_target_pairs={{8,12},{9,13},{10,14},{11,15},{24,28},{25,29},{26,30},{27,31}} | collective-permute-start | bytes 1179656 | tf_op jit(solution)/shard_map/ppermute | solution.py:336
  47.1 27.6 %collective-permute-start.12 = (bf16[128,1536]{1,0:T(8,128)(2,1)S(1)}, bf16[128,1536]{1,0:T(8,128)(2,1)S(1)}, u32[]{:S(2)}, u32[]{:S(2)}) collective-permute-start(bf16[128,1536]{1,0:T(8,128)(2,1)S(1)} %collective-permute-done.7.refs_1_), channel_id=1, source_target_pairs={{4,0},{5,1},{6,2},{7,3},{20,16},{21,17},{22,18},{23,19}} | collective-permute-start | bytes 1179656 | tf_op jit(solution)/shard_map/ppermute | solution.py:338
  48.4 19.9 %collective-permute-start.13 = (bf16[128,1536]{1,0:T(8,128)(2,1)S(1)}, bf16[128,1536]{1,0:T(8,128)(2,1)S(1)}, u32[]{:S(2)}, u32[]{:S(2)}) collective-permute-start(bf16[128,1536]{1,0:T(8,128)(2,1)S(1)} %collective-permute-done.8.refs_0_), channel_id=1, source_target_pairs={{8,12},{9,13},{10,14},{11,15},{24,28},{25,29},{26,30},{27,31}} | collective-permute-start | bytes 1179656 | tf_op jit(solution)/shard_map/ppermute | solution.py:336
  49.1 19.8 %collective-permute-start.14 = (bf16[128,1536]{1,0:T(8,128)(2,1)S(1)}, bf16[128,1536]{1,0:T(8,128)(2,1)S(1)}, u32[]{:S(2)}, u32[]{:S(2)}) collective-permute-start(bf16[128,1536]{1,0:T(8,128)(2,1)S(1)} %collective-permute-done.9.refs_1_), channel_id=1, source_target_pairs={{4,0},{5,1},{6,2},{7,3},{20,16},{21,17},{22,18},{23,19}} | collective-permute-start | bytes 1179656 | tf_op jit(solution)/shard_map/ppermute | solution.py:338
  57.0 42.5 %collective-permute-start.5 = (bf16[256,3200]{1,0:T(8,128)(2,1)S(1)}, bf16[256,3200]{1,0:T(8,128)(2,1)S(1)}, u32[]{:S(2)}, u32[]{:S(2)}) collective-permute-start(bf16[256,3200]{1,0:T(8,128)(2,1)S(1)} %project.9.refs_3_.refs_8_.refs_9_.refs_10_.refs_0_.refs_1_.refs_2_), channel_id=1, source_target_pairs={{0,1},{1,0},{2,3},{3,2},{4,5},{5,4},{6,7},{7,6},{8,9},{9,8},{10,11... | collective-permute-start | bytes 4915208 | tf_op jit(solution)/shard_map/ppermute | solution.py:346
  68.3 17.3 %collective-permute-start.10 = (bf16[128,3200]{1,0:T(8,128)(2,1)S(1)}, bf16[128,3200]{1,0:T(8,128)(2,1)S(1)}, u32[]{:S(2)}, u32[]{:S(2)}) collective-permute-start(bf16[128,3200]{1,0:T(8,128)(2,1)S(1)} %project.11.refs_3_.refs_8_.refs_9_.refs_10_.refs_0_.refs_1_.refs_2_), channel_id=1, source_target_pairs={{0,1},{1,0},{2,3},{3,2},{4,5},{5,4},{6,7},{7,6},{8,9},{9,8},{10,11... | collective-permute-start | bytes 2457608 | tf_op jit(solution)/shard_map/ppermute | solution.py:346
  68.9 21.8 %slice-start = ((s8[6291456]{0:T(1024)(128)(4,1)}), s8[4194304]{0:T(1024)(128)(4,1)S(1)}, s32[]{:S(2)}) async-start(s8[6291456]{0:T(1024)(128)(4,1)} %bitcast.38), calls=%async_computation | async-start | bytes 8388608
  74.7 10.9 %copy-start.2 = (bf16[256,256]{1,0:T(8,128)(2,1)S(1)}, bf16[256,256]{1,0:T(8,128)(2,1)}, u32[]{:S(2)}) copy-start(bf16[256,256]{1,0:T(8,128)(2,1)} %constant.51.refs_16_) | copy-start | bytes 393220
  74.7 15.9 %slice-start.1 = ((s8[6291456]{0:T(1024)(128)(4,1)}), s8[2097152]{0:T(1024)(128)(4,1)S(1)}, s32[]{:S(2)}) async-start(s8[6291456]{0:T(1024)(128)(4,1)} %bitcast.38), calls=%async_computation.1 | async-start | bytes 4194304
  80.5 5.1 %collective-permute-start.15 = (bf16[128,3200]{1,0:T(8,128)(2,1)S(1)}, bf16[128,3200]{1,0:T(8,128)(2,1)S(1)}, u32[]{:S(2)}, u32[]{:S(2)}) collective-permute-start(bf16[128,3200]{1,0:T(8,128)(2,1)S(1)} %project.13.refs_0_.refs_1_.refs_2_.refs_3_.refs_17_.refs_8_.refs_9_.refs_10_), channel_id=1, source_target_pairs={{0,1},{1,0},{2,3},{3,2},{4,5},{5,4},{6,7},{7,6},{8,9},{9,8},{10,11... | collective-permute-start | bytes 2457608 | tf_op jit(solution)/shard_map/ppermute | solution.py:346
  80.6 29.5 %collective-permute-start = (bf16[128,3200]{1,0:T(8,128)(2,1)S(1)}, bf16[128,3200]{1,0:T(8,128)(2,1)S(1)}, u32[]{:S(2)}, u32[]{:S(2)}) collective-permute-start(bf16[128,3200]{1,0:T(8,128)(2,1)S(1)} %project.7._.refs_8_.refs_9_.refs_10_.refs_0_.refs_1_.refs_2_.refs_3_), channel_id=1, source_target_pairs={{0,1},{1,0},{2,3},{3,2},{4,5},{5,4},{6,7},{7,6},{8,9},{9,8},{10,11... | collective-permute-start | bytes 2457608 | tf_op jit(solution)/shard_map/ppermute | solution.py:346
  93.1 24.5 %collective-permute-start.16 = (bf16[64,3072]{1,0:T(8,128)(2,1)S(1)}, bf16[64,3072]{1,0:T(8,128)(2,1)S(1)}, u32[]{:S(2)}, u32[]{:S(2)}) collective-permute-start(bf16[64,3072]{1,0:T(8,128)(2,1)S(1)} %get-tuple-element.14.refs_17_), channel_id=1, source_target_pairs={{0,4},{12,8},{1,5},{13,9},{2,6},{14,10},{3,7},{15,11},{16,20},{28,... | collective-permute-start | bytes 1179656 | tf_op jit(solution)/shard_map/ppermute | solution.py:385
  94.4 3.5 %copy-start.5 = (s32[1,64]{1,0:T(1,128)S(1)}, s32[1,64]{1,0:T(1,128)}, u32[]{:S(2)}) copy-start(s32[1,64]{1,0:T(1,128)} %param.19) | copy-start | bytes 772
  94.4 26.2 %collective-permute-start.22 = (bf16[64,3072]{1,0:T(8,128)(2,1)S(1)}, bf16[64,3072]{1,0:T(8,128)(2,1)S(1)}, u32[]{:S(2)}, u32[]{:S(2)}) collective-permute-start(bf16[64,3072]{1,0:T(8,128)(2,1)S(1)} %get-tuple-element.23), channel_id=1, source_target_pairs={{0,4},{12,8},{1,5},{13,9},{2,6},{14,10},{3,7},{15,11},{16,20},{28,... | collective-permute-start | bytes 1179656 | tf_op jit(solution)/shard_map/ppermute | solution.py:385
  117.7 9.0 %collective-permute-start.19 = (bf16[64,3072]{1,0:T(8,128)(2,1)S(1)}, bf16[64,3072]{1,0:T(8,128)(2,1)S(1)}, u32[]{:S(2)}, u32[]{:S(2)}) collective-permute-start(bf16[64,3072]{1,0:T(8,128)(2,1)S(1)} %get-tuple-element.33), channel_id=1, source_target_pairs={{8,4},{12,8},{9,5},{13,9},{10,6},{14,10},{11,7},{15,11},{24,20},{2... | collective-permute-start | bytes 1179656 | tf_op jit(solution)/shard_map/ppermute | solution.py:385
  118.4 11.7 %collective-permute-start.17 = (bf16[64,3072]{1,0:T(8,128)(2,1)S(1)}, bf16[64,3072]{1,0:T(8,128)(2,1)S(1)}, u32[]{:S(2)}, u32[]{:S(2)}) collective-permute-start(bf16[64,3072]{1,0:T(8,128)(2,1)S(1)} %get-tuple-element.32), channel_id=1, source_target_pairs={{0,4},{4,8},{1,5},{5,9},{2,6},{6,10},{3,7},{7,11},{16,20},{20,24},... | collective-permute-start | bytes 1179656 | tf_op jit(solution)/shard_map/ppermute | solution.py:385
  120.8 14.5 %collective-permute-start.25 = (bf16[64,3072]{1,0:T(8,128)(2,1)S(1)}, bf16[64,3072]{1,0:T(8,128)(2,1)S(1)}, u32[]{:S(2)}, u32[]{:S(2)}) collective-permute-start(bf16[64,3072]{1,0:T(8,128)(2,1)S(1)} %get-tuple-element.35), channel_id=1, source_target_pairs={{8,4},{12,8},{9,5},{13,9},{10,6},{14,10},{11,7},{15,11},{24,20},{2... | collective-permute-start | bytes 1179656 | tf_op jit(solution)/shard_map/ppermute | solution.py:385
  121.5 17.0 %collective-permute-start.23 = (bf16[64,3072]{1,0:T(8,128)(2,1)S(1)}, bf16[64,3072]{1,0:T(8,128)(2,1)S(1)}, u32[]{:S(2)}, u32[]{:S(2)}) collective-permute-start(bf16[64,3072]{1,0:T(8,128)(2,1)S(1)} %get-tuple-element.34), channel_id=1, source_target_pairs={{0,4},{4,8},{1,5},{5,9},{2,6},{6,10},{3,7},{7,11},{16,20},{20,24},... | collective-permute-start | bytes 1179656 | tf_op jit(solution)/shard_map/ppermute | solution.py:385
  126.8 24.4 %collective-permute-start.20 = (bf16[64,3072]{1,0:T(8,128)(2,1)S(1)}, bf16[64,3072]{1,0:T(8,128)(2,1)S(1)}, u32[]{:S(2)}, u32[]{:S(2)}) collective-permute-start(bf16[64,3072]{1,0:T(8,128)(2,1)S(1)} %add_convert_fusion.2), channel_id=1, source_target_pairs={{4,0},{8,4},{12,8},{5,1},{9,5},{13,9},{6,2},{10,6},{14,10},{7,3},{... | collective-permute-start | bytes 1179656 | tf_op jit(solution)/shard_map/ppermute | solution.py:385
  130.2 21.1 %collective-permute-start.18 = (bf16[64,3072]{1,0:T(8,128)(2,1)S(1)}, bf16[64,3072]{1,0:T(8,128)(2,1)S(1)}, u32[]{:S(2)}, u32[]{:S(2)}) collective-permute-start(bf16[64,3072]{1,0:T(8,128)(2,1)S(1)} %add_convert_fusion.3), channel_id=1, source_target_pairs={{0,4},{4,8},{8,12},{1,5},{5,9},{9,13},{2,6},{6,10},{10,14},{3,7},{... | collective-permute-start | bytes 1179656 | tf_op jit(solution)/shard_map/ppermute | solution.py:385
  135.5 15.8 %collective-permute-start.26 = (bf16[64,3072]{1,0:T(8,128)(2,1)S(1)}, bf16[64,3072]{1,0:T(8,128)(2,1)S(1)}, u32[]{:S(2)}, u32[]{:S(2)}) collective-permute-start(bf16[64,3072]{1,0:T(8,128)(2,1)S(1)} %add_convert_fusion), channel_id=1, source_target_pairs={{4,0},{8,4},{12,8},{5,1},{9,5},{13,9},{6,2},{10,6},{14,10},{7,3},{... | collective-permute-start | bytes 1179656 | tf_op jit(solution)/shard_map/ppermute | solution.py:385
  138.6 15.9 %collective-permute-start.24 = (bf16[64,3072]{1,0:T(8,128)(2,1)S(1)}, bf16[64,3072]{1,0:T(8,128)(2,1)S(1)}, u32[]{:S(2)}, u32[]{:S(2)}) collective-permute-start(bf16[64,3072]{1,0:T(8,128)(2,1)S(1)} %add_convert_fusion.1), channel_id=1, source_target_pairs={{0,4},{4,8},{8,12},{1,5},{5,9},{9,13},{2,6},{6,10},{10,14},{3,7},{... | collective-permute-start | bytes 1179656 | tf_op jit(solution)/shard_map/ppermute | solution.py:385
  155.0 12.1 %collective-permute-start.27 = (bf16[64,3072]{1,0:T(8,128)(2,1)S(1)}, bf16[64,3072]{1,0:T(8,128)(2,1)S(1)}, u32[]{:S(2)}, u32[]{:S(2)}) collective-permute-start(bf16[64,3072]{1,0:T(8,128)(2,1)S(1)} %get-tuple-element.29), channel_id=1, source_target_pairs={{0,2},{2,0},{1,3},{3,1},{4,6},{6,4},{5,7},{7,5},{8,10},{10,8},{9,1... | collective-permute-start | bytes 1179656 | tf_op jit(solution)/shard_map/ppermute | solution.py:406
  156.6 17.2 %collective-permute-start.21 = (bf16[64,3072]{1,0:T(8,128)(2,1)S(1)}, bf16[64,3072]{1,0:T(8,128)(2,1)S(1)}, u32[]{:S(2)}, u32[]{:S(2)}) collective-permute-start(bf16[64,3072]{1,0:T(8,128)(2,1)S(1)} %get-tuple-element.28), channel_id=1, source_target_pairs={{0,2},{2,0},{1,3},{3,1},{4,6},{6,4},{5,7},{7,5},{8,10},{10,8},{9,1... | collective-permute-start | bytes 1179656 | tf_op jit(solution)/shard_map/ppermute | solution.py:406
where the time goes:
time: 175 us
  Pallas kernels  80.7 us (46%)
  starting transfers between devices  47.7 us (27%)
  waiting for transfers between devices  33.2 us (19%)
  between operations  5.78 us (3%)
  other arithmetic  2.88 us (2%)
  local copies, waits for them, and re-layouts  2.39 us (1%)
  matrix products  2.04 us (1%)
    pallas_call x7, Pallas kernels, project(): pl.pallas_call(functools.partial(project_kernel, merged, len(pieces), lin...  44.2 us
    ppermute x10, starting transfers between devices, reduce_step(): moved.append(lax.ppermute(value, 'ctx', pairs))  24.5 us
    pallas_call x6, Pallas kernels, mix(): pl.pallas_call(functools.partial(mix_kernel, full_width, line), grid=(per...  23.6 us
    ppermute x2, waiting for transfers between devices, layer(): lax.ppermute(v, 'section', turn)  15.5 us
    ppermute x6, starting transfers between devices, layer(): lax.ppermute(gathered['u', k - 1][i], 'ctx', [(a, b) for a, b in up if a...  12.3 us
    pallas_call x6, Pallas kernels, emit(): pl.pallas_call(functools.partial(emit_kernel, line), grid=(width // tile,...  11.8 us
    ppermute x6, waiting for transfers between devices, layer(): lax.ppermute(gathered['d', k - 1][i], 'ctx', [(a, b) for a, b in down if...  8.61 us
    ppermute x6, starting transfers between devices, layer(): lax.ppermute(gathered['d', k - 1][i], 'ctx', [(a, b) for a, b in down if...  7.73 us
  transfers between devices with their start and end apart: 28, of which 9 were waited for; matrix products, arithmetic and copies ran while one was open for 3% of the time, Pallas kernels for 46%

commit v1 on v0

--- a/solution.py
+++ b/solution.py
@@ -31,86 +31,106 @@
     return pltpu.CompilerParams(vmem_limit_bytes=vmem_limit)
 
 
-def project_kernel(merged, parts, line, first, final, table_ref, gain_ref, *refs):
+def project_kernel(layout, first, final, *refs):
+    refs = refs[1:] if final else refs
+    gain_ref, *refs = refs
+    x_refs = refs[: sum(layout)]
+    refs = refs[sum(layout) :]
+    carry_refs = () if first else refs[:2]
+    refs = refs if first else refs[2:]
+    w_ref, _, out_ref, *more, scaled, stat = refs
     step = pl.program_id(0)
-    x_refs = refs[:parts]
-    carry_ref = None if first else refs[parts]
-    w_ref, _, out_ref, scaled, stat = refs[parts + (0 if first else 1) :]
-    tile = out_ref.shape[1]
-    busy = table_ref[line, 4] > 0
     last = step == pl.num_programs(0) - 1
 
-    @pl.when(busy & (step == 0))
+    @pl.when(step == 0)
     def _():
-        streams = parts // 2 if merged else parts
         chunk = x_refs[0].shape[0]
-        for index in range(streams):
-            x = x_refs[index][...].astype(jnp.float32)
-            if merged:
-                x = x + x_refs[streams + index][...].astype(jnp.float32)
+        source = 0
+        for index, inputs in enumerate(layout):
+            x = x_refs[source][...].astype(jnp.float32)
+            for other in range(1, inputs):
+                x = x + x_refs[source + other][...].astype(jnp.float32)
+            source += inputs
             place = slice(index * chunk, (index + 1) * chunk)
             scaled[place, :] = (x * gain_ref[...]).astype(jnp.bfloat16)
-            stat[place, :] = jnp.broadcast_to(jnp.sum(x * x, axis=1, keepdims=True), (chunk, lanes))
-
-    @pl.when(busy & jnp.logical_not(last))
-    def _():
+            squares = jnp.broadcast_to(jnp.sum(x * x, axis=1, keepdims=True), (chunk, lanes))
+            stat[place, :] = squares if first else squares + carry_refs[1][place, :]
+
+    def product():
         total = jnp.dot(scaled[...], w_ref[0], preferred_element_type=jnp.float32)
         if not first:
-            total = total + carry_ref[...]
+            total = total + carry_refs[0][...]
         out_ref[...] = total.astype(out_ref.dtype)
 
-    @pl.when(busy & last)
+    if not final:
+        product()
+        more[0][...] = stat[...]
+        return
+
+    pl.when(jnp.logical_not(last))(product)
+
+    @pl.when(last)
     def _():
         squares = stat[...]
-        if not first:
-            squares = squares + carry_ref[:, :lanes]
-        if final:
-            high = squares.astype(jnp.bfloat16).astype(jnp.float32)
-            column = lax.broadcasted_iota(jnp.int32, squares.shape, 1)
-            squares = jnp.where(column == 0, high, jnp.where(column == 1, squares - high, 0.0))
+        high = squares.astype(jnp.bfloat16).astype(jnp.float32)
+        column = lax.broadcasted_iota(jnp.int32, squares.shape, 1)
+        squares = jnp.where(column == 0, high, jnp.where(column == 1, squares - high, 0.0))
         out_ref[:, :lanes] = squares.astype(out_ref.dtype)
-        if tile > lanes:
-            out_ref[:, lanes:] = jnp.zeros((out_ref.shape[0], tile - lanes), out_ref.dtype)
-
-    @pl.when(jnp.logical_not(busy))
-    def _():
-        out_ref[...] = jnp.zeros_like(out_ref)
-
-
-def project(pieces, merged, table, line, gain, w, part, carry, final, after):
+        if out_ref.shape[1] > lanes:
+            out_ref[:, lanes:] = jnp.zeros((out_ref.shape[0], out_ref.shape[1] - lanes), out_ref.dtype)
+
+
+def project(pieces, layout, gain, w, part, carry, side, sides, after):
     streams, _, channels = w.shape
-    rows_each, depth = pieces[0].shape
-    rows = rows_each * (len(pieces) // 2 if merged else len(pieces))
-    tile = tile_of(channels, 1024)
-    per = channels // tile
-    steps = streams * per
+    chunk, depth = pieces[0].shape
+    rows = chunk * len(layout)
+    final = side is not None
     first = carry is None
-
-    def weights(i):
-        j = jnp.minimum(i, steps - 1)
-        return (j // per, part, j % per)
-
-    column = pl.BlockSpec((rows, tile), lambda i: (0, i))
-    return pl.pallas_call(
-        functools.partial(project_kernel, merged, len(pieces), line, first, final),
-        grid=(steps + 1,),
-        in_specs=[smem(), pl.BlockSpec((1, depth), lambda i: (0, part))]
-        + [pl.BlockSpec((rows_each, depth), lambda i: (0, 0))] * len(pieces)
-        + ([] if first else [column])
-        + [pl.BlockSpec((1, depth, tile), weights), pl.BlockSpec(memory_space=pl.ANY)],
-        out_specs=column,
-        out_shape=jax.ShapeDtypeStruct(
-            (rows, streams * channels + lanes), jnp.bfloat16 if final else jnp.float32
-        ),
-        scratch_shapes=[pltpu.VMEM((rows, depth), jnp.bfloat16), pltpu.VMEM((rows, lanes), jnp.float32)],
+    tile = channels // 2
+    steps = streams if final else 2 * streams
+
+    def channel(i, held):
+        return (jnp.minimum(i, steps - 1) * 2 + held[side]) if final else i
+
+    def at(index):
+        return lambda i, *held: index(i, held[0] if final else None)
+
+    column = pl.BlockSpec((rows, tile), at(lambda i, held: (0, channel(i, held))))
+    whole_stat = pl.BlockSpec((rows, lanes), at(lambda i, held: (0, 0)))
+    out_specs = [pl.BlockSpec((rows, tile), at(lambda i, held: (0, i)))]
+    out_shape = [jax.ShapeDtypeStruct((rows, streams * tile + lanes), jnp.bfloat16)]
+    if not final:
+        out_specs.append(whole_stat)
+        out_shape = [
+            jax.ShapeDtypeStruct((rows, streams * channels), jnp.float32),
+            jax.ShapeDtypeStruct((rows, lanes), jnp.float32),
+        ]
+    result = pl.pallas_call(
+        functools.partial(project_kernel, layout, first, final),
+        grid_spec=pltpu.PrefetchScalarGridSpec(
+            num_scalar_prefetch=1 if final else 0,
+            grid=(steps + 1 if final else steps,),
+            in_specs=[pl.BlockSpec((1, depth), at(lambda i, held: (0, part)))]
+            + [pl.BlockSpec((chunk, depth), at(lambda i, held: (0, 0)))] * len(pieces)
+            + ([] if first else [column, whole_stat])
+            + [
+                pl.BlockSpec(
+                    (1, depth, tile),
+                    at(lambda i, held: (channel(i, held) // 2, part, channel(i, held) % 2)),
+                ),
+                pl.BlockSpec(memory_space=pl.ANY),
+            ],
+            out_specs=out_specs,
+            scratch_shapes=[pltpu.VMEM((rows, depth), jnp.bfloat16), pltpu.VMEM((rows, lanes), jnp.float32)],
+        ),
+        out_shape=out_shape,
         compiler_params=params(),
         cost_estimate=pl.CostEstimate(
-            flops=2 * rows * depth * streams * channels,
-            bytes_accessed=2 * streams * depth * channels,
-            transcendentals=0,
+            flops=2 * rows * depth * steps * tile, bytes_accessed=2 * depth * steps * tile, transcendentals=0
         ),
         name="project",
-    )(table, gain, *pieces, *(() if first else (carry,)), w, after)
+    )(*((sides,) if final else ()), gain, *pieces, *(() if first else carry), w, after)
+    return result[0] if final else tuple(result)
 
 
 def wave_tables(rows):
@@ -158,7 +178,7 @@
     )(taps, forward, after)
 
 
-def mix_kernel(full_width, line, table_ref, *refs):
+def mix_kernel(full_width, line, sides_ref, table_ref, *refs):
     q0, k0, v0, s0, q1, k1, v1, s1, pk0, pv0, ps0, pk1, pv1, ps1, f_ref, forward_ref, inverse_ref, _, out_ref, window = refs
     rows = out_ref.shape[0]
     block = table_ref[line, 0]
@@ -211,53 +231,57 @@
         out_ref[...] = jnp.zeros_like(out_ref)
 
 
-def mix(table, line, here, before, rows, waves, filter_waves, full_width, after):
+def mix(table, line, here, before, rows, waves, filter_waves, full_width, sides, after):
     own, got, at = here
     own_before, got_before, at_before = before
-    forward, inverse = waves
-    channels = filter_waves.shape[1]
+    channels = filter_waves.shape[1] // 2
     tile = tile_of(channels, 256)
     per = channels // tile
     streams = 3
 
     def spec(at, stream):
-        return pl.BlockSpec((rows, tile), lambda i: (at, stream * per + i))
+        return pl.BlockSpec((rows, tile), lambda i, held: (at, stream * per + i))
 
     def stat(at):
-        return pl.BlockSpec((rows, lanes), lambda i: (at, streams * (channels // lanes)))
-
-    whole = [pl.BlockSpec(wave.shape, lambda i: (0, 0)) for wave in waves]
+        return pl.BlockSpec((rows, lanes), lambda i, held: (at, streams * (channels // lanes)))
+
+    whole = [pl.BlockSpec(wave.shape, lambda i, held: (0, 0)) for wave in waves]
     return pl.pallas_call(
         functools.partial(mix_kernel, full_width, line),
-        grid=(per,),
-        in_specs=[smem()]
-        + [spec(at, 0), spec(at, 1), spec(at, 2), stat(at)] * 2
-        + [spec(at_before, 1), spec(at_before, 2), stat(at_before)] * 2
-        + [pl.BlockSpec((2 * rows, tile), lambda i: (0, i))]
-        + whole
-        + [pl.BlockSpec(memory_space=pl.ANY)],
-        out_specs=pl.BlockSpec((rows, tile), lambda i: (0, i)),
+        grid_spec=pltpu.PrefetchScalarGridSpec(
+            num_scalar_prefetch=1,
+            grid=(per,),
+            in_specs=[smem()]
+            + [spec(at, 0), spec(at, 1), spec(at, 2), stat(at)] * 2
+            + [spec(at_before, 1), spec(at_before, 2), stat(at_before)] * 2
+            + [pl.BlockSpec((2 * rows, tile), lambda i, held: (0, held[0] * per + i))]
+            + whole
+            + [pl.BlockSpec(memory_space=pl.ANY)],
+            out_specs=pl.BlockSpec((rows, tile), lambda i, held: (0, i)),
+            scratch_shapes=[pltpu.VMEM((2 * rows, tile), jnp.bfloat16)],
+        ),
         out_shape=jax.ShapeDtypeStruct((rows, channels), jnp.bfloat16),
-        scratch_shapes=[pltpu.VMEM((2 * rows, tile), jnp.bfloat16)],
         compiler_params=params(),
         cost_estimate=pl.CostEstimate(
             flops=16 * rows * rows * channels, bytes_accessed=32 * rows * channels, transcendentals=0
         ),
         name="mix",
     )(
-        table, own, own, own, own, got, got, got, got,
+        sides, table, own, own, own, own, got, got, got, got,
         own_before, own_before, own_before, got_before, got_before, got_before,
-        filter_waves, forward, inverse, after,
+        filter_waves, *waves, after,
     )
 
 
-def emit_kernel(line, table_ref, gated_ref, w_ref, _, *out_refs):
+def emit_kernel(line, sides_ref, table_ref, mine_ref, theirs_ref, w_mine_ref, w_theirs_ref, _, *out_refs):
     work = table_ref[line, 2] > 0
     chunk = out_refs[0].shape[0]
 
     @pl.when(work)
     def _():
-        product = jnp.dot(gated_ref[...], w_ref[...], preferred_element_type=jnp.float32).astype(jnp.bfloat16)
+        product = jnp.dot(mine_ref[...], w_mine_ref[...], preferred_element_type=jnp.float32)
+        product = product + jnp.dot(theirs_ref[...], w_theirs_ref[...], preferred_element_type=jnp.float32)
+        product = product.astype(jnp.bfloat16)
         for index, out_ref in enumerate(out_refs):
             out_ref[...] = product[index * chunk : (index + 1) * chunk, :]
 
@@ -267,28 +291,59 @@
             out_ref[...] = jnp.zeros_like(out_ref)
 
 
-def emit(table, line, gated, w, after):
-    rows, channels = gated.shape
+def emit(table, line, mine, theirs, w, sides, after):
+    rows, half = mine.shape
     width = w.shape[1]
     tile = tile_of(width, 1024)
     chunk = rows // halves
+    whole = pl.BlockSpec((rows, half), lambda i, held: (0, 0))
     return pl.pallas_call(
         functools.partial(emit_kernel, line),
-        grid=(width // tile,),
-        in_specs=[
-            smem(),
-            pl.BlockSpec((rows, channels), lambda i: (0, 0)),
-            pl.BlockSpec((channels, tile), lambda i: (0, i)),
-            pl.BlockSpec(memory_space=pl.ANY),
-        ],
-        out_specs=[pl.BlockSpec((chunk, tile), lambda i: (0, i))] * halves,
+        grid_spec=pltpu.PrefetchScalarGridSpec(
+            num_scalar_prefetch=1,
+            grid=(width // tile,),
+            in_specs=[
+                smem(),
+                whole,
+                whole,
+                pl.BlockSpec((half, tile), lambda i, held: (held[0], i)),
+                pl.BlockSpec((half, tile), lambda i, held: (held[1], i)),
+                pl.BlockSpec(memory_space=pl.ANY),
+            ],
+            out_specs=[pl.BlockSpec((chunk, tile), lambda i, held: (0, i))] * halves,
+        ),
         out_shape=[jax.ShapeDtypeStruct((chunk, width), jnp.bfloat16)] * halves,
         compiler_params=params(),
         cost_estimate=pl.CostEstimate(
-            flops=2 * rows * channels * width, bytes_accessed=2 * channels * width, transcendentals=0
+            flops=4 * rows * half * width, bytes_accessed=4 * half * width, transcendentals=0
         ),
         name="emit",
-    )(table, gated, w, after)
+    )(sides, table, mine, theirs, w, w, after)
+
+
+def finish_kernel(*refs):
+    total = refs[0][...].astype(jnp.float32)
+    for ref in refs[1:-1]:
+        total = total + ref[...].astype(jnp.float32)
+    refs[-1][...] = total.astype(jnp.bfloat16)
+
+
+def finish(x, index, terms):
+    chunk, width = terms[0].shape
+    tile = tile_of(width, 1024)
+    return pl.pallas_call(
+        finish_kernel,
+        grid=(width // tile,),
+        in_specs=[pl.BlockSpec((chunk, tile), lambda i: (index, i))]
+        + [pl.BlockSpec((chunk, tile), lambda i: (0, i))] * len(terms),
+        out_specs=pl.BlockSpec((chunk, tile), lambda i: (0, i)),
+        out_shape=jax.ShapeDtypeStruct((chunk, width), jnp.bfloat16),
+        compiler_params=params(),
+        cost_estimate=pl.CostEstimate(
+            flops=chunk * width * len(terms), bytes_accessed=2 * chunk * width * (len(terms) + 2), transcendentals=0
+        ),
+        name="finish",
+    )(x, *terms)
 
 
 def added(*terms):
@@ -303,7 +358,6 @@
     place = lax.axis_index("ctx")
     x_local = spans[0]
     rows, half_width = x_local.shape
-    chunk = rows // halves
     full_width = half_width * lax.axis_size("mp")
     weights = jnp.swapaxes(w_in[0], 0, 1)
     gain = norm_gain
@@ -338,46 +392,60 @@
             value = lax.ppermute(gathered["d", k - 1][i], "ctx", [(a, b) for a, b in down if a <= count - k])
             gathered["d", k].append(value)
 
-    after = x_local
+    core = lax.axis_index("mp").astype(jnp.int32)
+    sides = jnp.stack([core, 1 - core])
     held = {}
-
-    def offer(k, own):
-        merged = 2 * k >= count
-        got = lax.ppermute(own, "mp", partner)
-        held["u", k] = (own, got, 0)
-        held["d", k] = (own, got, 0 if merged or k == 0 else 1)
-
     gated = {}
     sums = {}
 
-    def blend(kind, k, after):
+    def combine(kind, k, after):
         before = ("u", k + 1) if kind == "u" or k == 0 else ("d", k - 1)
-        gated[kind, k] = mix(
+        mine = mix(
             table, line[kind, k], held["d" if kind == "m" else kind, k], held[before],
-            rows, waves, filter_waves, full_width, after,
+            rows, waves, filter_waves, full_width, sides, after,
         )
-        sums[kind, k] = emit(table, line[kind, k], gated[kind, k], w_out[0], gated[kind, k])
+        gated[kind, k] = (mine, lax.ppermute(mine, "mp", partner))
+        return mine
+
+    def spread(kind, k, after):
+        sums[kind, k] = emit(table, line[kind, k], *gated[kind, k], w_out[0], sides, after)
         return sums[kind, k][0]
 
-    after = project([x_local], False, table, 0, gain, weights, 0, None, True, after)
-    offer(0, after)
-    filter_waves = spectrum(filters[0], waves[0], after)
+    filter_waves = spectrum(filters[0], waves[0], x_local)
     after = filter_waves
-    for k in range(1, count):
-        slot = ("d", k) if k < far else ("m", far)
+    for group in groups_of(count):
+        layout = []
+        inputs = [[] for _ in range(halves)]
+        for k in group:
+            merged = 2 * k >= count
+            for kind in ("d",) if k == 0 else ("ud",) if merged else ("u", "d"):
+                for way in kind:
+                    held[way, k] = len(layout)
+                    for i in range(halves):
+                        inputs[i].append(gathered[way, k][i])
+                layout.append(len(kind))
         carry = None
-        for i in range(halves):
-            after = project(
-                [gathered["u", k][i], gathered["d", k][i]],
-                2 * k >= count, table, line[slot], gain, weights, i, carry, i == halves - 1, after,
-            )
-            carry = after
-        offer(k, after)
-    after = blend("m", far, after)
-    for k in range(far - 1, 0, -1):
-        after = blend("u", k, after)
-        after = blend("d", k, after)
-    after = blend("d", 0, after)
+        for i in range(halves - 1):
+            carry = project(inputs[i], layout, gain, weights, i, carry, None, sides, after)
+            after = carry[1]
+        theirs = project(inputs[-1], layout, gain, weights, halves - 1, carry, 1, sides, after)
+        got = lax.ppermute(theirs, "mp", partner)
+        mine = project(inputs[-1], layout, gain, weights, halves - 1, carry, 0, sides, theirs)
+        after = mine
+        for k in group:
+            for way in "d" if k == 0 else "ud":
+                held[way, k] = (mine, got, held[way, k])
+        for kind, k in early_slots(count) if group[0] == 0 else ():
+            after = combine(kind, k, after)
+        for kind, k in early_slots(count) if group[0] == 0 else ():
+            after = spread(kind, k, after)
+    rest = [slot for slot in [("m", far)] + [(kind, k) for k in range(far - 1, 0, -1) for kind in "ud"] + [("d", 0)]]
+    rest = [slot for slot in rest if slot not in sums]
+    after = combine(*rest[0], after)
+    for index, slot in enumerate(rest):
+        if index + 1 < len(rest):
+            after = combine(*rest[index + 1], after)
+        after = spread(*slot, after)
 
     def reduce_step(values, pairs):
         moved = []
@@ -399,19 +467,32 @@
                 sums[kind, k - 1] = [added(a, b) for a, b in zip(sums[kind, k - 1], moved)]
         else:
             terms += arrived if far > 1 else arrived[:1]
-    pieces = [x_local[i * chunk : (i + 1) * chunk] for i in range(halves)]
     sections = lax.axis_size("section")
     turn = [(source, (source + 1) % sections) for source in range(sections)]
-    final = [added(*parts) for parts in zip(pieces, *terms)]
-    advanced = jnp.concatenate([lax.ppermute(v, "section", turn) for v in final], axis=0)[None]
+    advanced = []
+    for i in range(halves):
+        final = finish(x_local, i, [term[i] for term in terms])
+        advanced.append(lax.ppermute(final, "section", turn))
+    advanced = jnp.concatenate(advanced, axis=0)[None]
 
     row = jnp.arange(rows, dtype=jnp.int32)
-    picked = None
+    picked = [0.0, 0.0]
     for slot in order:
         one_hot = (needles[0][:, None] == (row + blocks[line[slot]] * rows)[None, :]).astype(jnp.bfloat16)
-        term = jnp.dot(one_hot, gated[slot], preferred_element_type=jnp.float32)
-        picked = term if picked is None else picked + term
-    return (advanced, picked.astype(jnp.bfloat16)[None])
+        for index, part in enumerate(gated[slot]):
+            picked[index] += jnp.dot(one_hot, part, preferred_element_type=jnp.float32)
+    mine, theirs = [value.astype(jnp.bfloat16) for value in picked]
+    lower = jnp.where(core == 0, mine, theirs)
+    upper = jnp.where(core == 0, theirs, mine)
+    return (advanced, jnp.concatenate([lower, upper], axis=1)[None])
+
+
+def groups_of(count):
+    return [list(range(k, min(k + 2, count))) for k in range(0, count, 2)]
+
+
+def early_slots(count):
+    return [("d", 0), ("d", 1)] if count > 2 else []
 
 
 def solution(mesh):

time: 175 us -> 196 us (1.12)
  the two profiles are of different devices: /device:TPU:0 before, /device:TPU:12 now
where the time goes in v1:
time: 196 us; the launch traced here: 194 us
  Pallas kernels  74 us (38%)
  starting transfers between devices  61 us (31%)
  waiting for transfers between devices  27.6 us (14%)
  local copies, waits for them, and re-layouts  17.4 us (9%)
  between operations  6.22 us (3%)
  other arithmetic  4.58 us (2%)
  matrix products  3.43 us (2%)
    pallas_call x6, Pallas kernels, project(): pl.pallas_call(functools.partial(project_kernel, layout, first, final), g...  41 us
    ppermute x10, starting transfers between devices, reduce_step(): moved.append(lax.ppermute(value, 'ctx', pairs))  26.1 us
    ppermute x6, starting transfers between devices, layer(): lax.ppermute(gathered['u', k - 1][i], 'ctx', [(a, b) for a, b in up if a...  16.8 us
    ppermute x10, waiting for transfers between devices, reduce_step(): moved.append(lax.ppermute(value, 'ctx', pairs))  16 us
    pallas_call x6, Pallas kernels, mix(): pl.pallas_call(functools.partial(mix_kernel, full_width, line), grid_spec...  15.9 us
    pallas_call x6, Pallas kernels, emit(): pl.pallas_call(functools.partial(emit_kernel, line), grid_spec=pltpu.Pref...  15.3 us
    unnamed x118, local copies, waits for them, and re-layouts  15 us
    ppermute x6, starting transfers between devices, layer(): lax.ppermute(gathered['d', k - 1][i], 'ctx', [(a, b) for a, b in down if...  13 us
  transfers between devices with their start and end apart: 32, of which 9 were waited for; matrix products, arithmetic and copies ran while one was open for 4% of the time, Pallas kernels for 30%

profile of v1, /device:TPU:12, one launch (start us, length us, event | category | flops | bytes accessed | tf_op | source)
XLA Modules:
  0.0 194.2 jit_solution(13622445805055443090)
XLA Ops:
  1.9 3.5 %collective-permute-start.2 = (bf16[128,1536]{1,0:T(8,128)(2,1)S(1)}, bf16[128,1536]{1,0:T(8,128)(2,1)}, u32[]{:S(2)}, u32[]{:S(2)}) collective-permute-start(bf16[128,1536]{1,0:T(8,128)(2,1)S(1)} %get-tuple-element.36.refs_1_), channel_id=1, source_target_pairs={{0,4},{4,8},{8,12},{1,5},{5,9},{9,13},{2,6},{6,10},{10,14},{3,7},{... | collective-permute-start | bytes 1179656 | tf_op jit(solution)/shard_map/ppermute | solution.py:390
  5.4 3.1 %collective-permute-start.3 = (bf16[128,1536]{1,0:T(8,128)(2,1)S(1)}, bf16[128,1536]{1,0:T(8,128)(2,1)}, u32[]{:S(2)}, u32[]{:S(2)}) collective-permute-start(bf16[128,1536]{1,0:T(8,128)(2,1)S(1)} %get-tuple-element.36.refs_1_), channel_id=1, source_target_pairs={{4,0},{8,4},{12,8},{5,1},{9,5},{13,9},{6,2},{10,6},{14,10},{7,3},{... | collective-permute-start | bytes 1179656 | tf_op jit(solution)/shard_map/ppermute | solution.py:392
  8.5 2.8 %collective-permute-start = (bf16[128,1536]{1,0:T(8,128)(2,1)S(1)}, bf16[128,1536]{1,0:T(8,128)(2,1)S(1)}, u32[]{:S(2)}, u32[]{:S(2)}) collective-permute-start(bf16[128,1536]{1,0:T(8,128)(2,1)S(1)} %get-tuple-element.37.refs_2_), channel_id=1, source_target_pairs={{0,4},{4,8},{8,12},{1,5},{5,9},{9,13},{2,6},{6,10},{10,14},{3,7},{... | collective-permute-start | bytes 1179656 | tf_op jit(solution)/shard_map/ppermute | solution.py:390
  11.3 3.1 %collective-permute-start.1 = (bf16[128,1536]{1,0:T(8,128)(2,1)S(1)}, bf16[128,1536]{1,0:T(8,128)(2,1)S(1)}, u32[]{:S(2)}, u32[]{:S(2)}) collective-permute-start(bf16[128,1536]{1,0:T(8,128)(2,1)S(1)} %get-tuple-element.37.refs_2_), channel_id=1, source_target_pairs={{4,0},{8,4},{12,8},{5,1},{9,5},{13,9},{6,2},{10,6},{14,10},{7,3},{... | collective-permute-start | bytes 1179656 | tf_op jit(solution)/shard_map/ppermute | solution.py:392
  15.9 3.5 %collective-permute-done.3.refs_3_ = bf16[128,1536]{1,0:T(8,128)(2,1)} collective-permute-done((bf16[128,1536]{1,0:T(8,128)(2,1)S(1)}, bf16[128,1536]{1,0:T(8,128)(2,1)}, u32[]{:S(2)}, u32[]{:S(2)}) %collective-permute-start.3) | collective-permute-done | bytes 393248 | tf_op jit(solution)/shard_map/ppermute | solution.py:392
  19.4 8.4 %project.6 = (f32[384,3072]{1,0:T(8,128)S(1)}, f32[384,128]{1,0:T(8,128)S(1)}) custom-call(f32[1,3072]{1,0:T(1,128)S(1)} %copy-done.37, bf16[128,1536]{1,0:T(8,128)(2,1)S(1)} %get-tuple-element.36.refs_1_, bf16[128,1536]{1,0:T(8,128)(2,1)} %collective-permute-done.2.refs_2_, bf16[128,1536]{1,0:T(8,128)(2,1)} %collective-permute-done.3.refs_3_, ...), custom_call_target="tpu_custom_call" | custom-call | flops 3623878656 | bytes 9437184 | tf_op jit(solution)/shard_map/project/pallas_call | solution.py:108
  28.8 6.7 %project.7.refs_8_ = bf16[384,1664]{1,0:T(8,128)(2,1)} custom-call(s32[2]{0:T(128)S(1)} %pad_add_fusion.refs_0_.sides_ref, f32[1,3072]{1,0:T(1,128)S(1)} %copy-done.37, bf16[128,1536]{1,0:T(8,128)(2,1)S(1)} %get-tuple-element.37.refs_2_, bf16[128,1536]{1,0:T(8,128)(2,1)S(1)} %collective-permute-done.refs_3_, ...), custom_call_target="tpu_custom_call" | custom-call | flops 1811939328 | bytes 4718592 | tf_op jit(solution)/shard_map/project/pallas_call | solution.py:108
  35.6 4.3 %collective-permute-start.11 = (bf16[128,1536]{1,0:T(8,128)(2,1)}, bf16[128,1536]{1,0:T(8,128)(2,1)}, u32[]{:S(2)}, u32[]{:S(2)}) collective-permute-start(bf16[128,1536]{1,0:T(8,128)(2,1)} %collective-permute-done.2.refs_2_), channel_id=1, source_target_pairs={{4,8},{8,12},{5,9},{9,13},{6,10},{10,14},{7,11},{11,15},{20,24},{2... | collective-permute-start | bytes 1179656 | tf_op jit(solution)/shard_map/ppermute | solution.py:390
  39.9 1.9 collective-permute-start.12
  44.3 4.8 %collective-permute-start.7 = (bf16[128,1536]{1,0:T(8,128)(2,1)}, bf16[128,1536]{1,0:T(8,128)(2,1)S(1)}, u32[]{:S(2)}, u32[]{:S(2)}) collective-permute-start(bf16[128,1536]{1,0:T(8,128)(2,1)} %copy-done.21), channel_id=1, source_target_pairs={{4,8},{8,12},{5,9},{9,13},{6,10},{10,14},{7,11},{11,15},{20,24},{2... | collective-permute-start | bytes 1179656 | tf_op jit(solution)/shard_map/ppermute | solution.py:390
  49.1 1.9 collective-permute-start.8
  51.1 2.3 %copy-done.4 = f32[384,3072]{1,0:T(8,128)S(1)} copy-done((f32[384,3072]{1,0:T(8,128)S(1)}, f32[384,3072]{1,0:T(8,128)}, u32[]{:S(2)}) %copy-start.4) | copy-done | bytes 4718616
  56.1 5.8 %project.8.refs_0_.refs_1_.refs_2_.refs_3_.refs_8_.refs_9_.refs_10_.refs_17_ = bf16[384,1664]{1,0:T(8,128)(2,1)S(1)} custom-call(s32[2]{0:T(128)S(1)} %copy-done.44, f32[1,3072]{1,0:T(1,128)S(1)} %copy-done.37, bf16[128,1536]{1,0:T(8,128)(2,1)S(1)} %get-tuple-element.37.refs_2_, bf16[128,1536]{1,0:T(8,128)(2,1)S(1)} %copy-done.22, ...), custom_call_target="tpu_custom_call" | custom-call | flops 1811939328 | bytes 4718592 | tf_op jit(solution)/shard_map/project/pallas_call | solution.py:108
  62.6 1.3 collective-permute-start.14
  63.9 3.2 %mix.6.refs_17_.mine_ref = bf16[128,512]{1,0:T(8,128)(2,1)S(1)} custom-call(s32[2]{0:T(128)S(1)} %copy-done.44, s32[6,5]{1,0:T(8,128)S(1)} %stack.43.table_ref, bf16[384,1664]{1,0:T(8,128)(2,1)S(1)} %project.8.refs_0_.refs_1_.refs_2_.refs_3_.refs_8_.refs_9_.refs_10_.refs_17_, ...), custom_call_target="tpu_custom_call" | custom-call | flops 134217728 | bytes 2097152 | tf_op jit(solution)/shard_map/mix/pallas_call | solution.py:249
  70.4 1.6 collective-permute-start.10
  72.0 3.2 %mix.7._.mine_ref = bf16[128,512]{1,0:T(8,128)(2,1)S(1)} custom-call(s32[2]{0:T(128)S(1)} %copy-done.44, s32[6,5]{1,0:T(8,128)S(1)} %stack.43.table_ref, bf16[384,1664]{1,0:T(8,128)(2,1)S(1)} %project.8.refs_0_.refs_1_.refs_2_.refs_3_.refs_8_.refs_9_.refs_10_.refs_17_, ...), custom_call_target="tpu_custom_call" | custom-call | flops 134217728 | bytes 2097152 | tf_op jit(solution)/shard_map/mix/pallas_call | solution.py:249
  77.0 3.0 %emit.6 = (bf16[64,3072]{1,0:T(8,128)(2,1)S(1)}, bf16[64,3072]{1,0:T(8,128)(2,1)S(1)}) custom-call(s32[2]{0:T(128)S(1)} %copy-done.44, s32[6,5]{1,0:T(8,128)S(1)} %stack.43.table_ref, bf16[128,512]{1,0:T(8,128)(2,1)S(1)} %mix.6.refs_17_.mine_ref, bf16[128,512]{1,0:T(8,128)(2,1)S(1)} %collective-permute-done.5.theirs_ref, bf16[1024,3072]{1,0:T(8,128)(2,1)S(1)} %bitcast.42, ...), custom_call_target="tpu_custom_call" | custom-call | flops 805306368 | bytes 6291456 | tf_op jit(solution)/shard_map/emit/pallas_call | solution.py:300
  80.8 3.0 %emit.7 = (bf16[64,3072]{1,0:T(8,128)(2,1)S(1)}, bf16[64,3072]{1,0:T(8,128)(2,1)S(1)}) custom-call(s32[2]{0:T(128)S(1)} %copy-done.44, s32[6,5]{1,0:T(8,128)S(1)} %stack.43.table_ref, bf16[128,512]{1,0:T(8,128)(2,1)S(1)} %mix.7._.mine_ref, bf16[128,512]{1,0:T(8,128)(2,1)S(1)} %collective-permute-done.6.theirs_ref, bf16[1024,3072]{1,0:T(8,128)(2,1)S(1)} %bitcast.44, ...), custom_call_target="tpu_custom_call" | custom-call | flops 805306368 | bytes 6291456 | tf_op jit(solution)/shard_map/emit/pallas_call | solution.py:300
  84.5 7.7 %project.9 = (f32[256,3072]{1,0:T(8,128)S(1)}, f32[256,128]{1,0:T(8,128)S(1)}) custom-call(f32[1,3072]{1,0:T(1,128)S(1)} %copy-done.37, bf16[128,1536]{1,0:T(8,128)(2,1)} %collective-permute-done.11.refs_1_, bf16[128,1536]{1,0:T(8,128)(2,1)} %collective-permute-done.12.refs_2_, bf16[128,1536]{1,0:T(8,128)(2,1)S(1)} %collective-permute-done.13.refs_3_, ...), custom_call_target="tpu_custom_call" | custom-call | flops 2415919104 | bytes 9437184 | tf_op jit(solution)/shard_map/project/pallas_call | solution.py:108
  92.4 6.6 %project.10.refs_9_ = bf16[256,1664]{1,0:T(8,128)(2,1)} custom-call(s32[2]{0:T(128)S(1)} %copy-done.44, f32[1,3072]{1,0:T(1,128)S(1)} %copy-done.37, bf16[128,1536]{1,0:T(8,128)(2,1)S(1)} %collective-permute-done.7.refs_2_, bf16[128,1536]{1,0:T(8,128)(2,1)S(1)} %collective-permute-done.8.refs_3_, bf16[128,1536]{1,0:T(8,128)(2,1)S(1)} %collective-permute-done.9.refs_4_, ...), custom_call_target="tpu_custom_call" | custom-call | flops 1207959552 | bytes 4718592 | tf_op jit(solution)/shard_map/project/pallas_call | solution.py:108
  102.1 1.9 copy-done.10
  109.5 5.7 %project.11.refs_0_.refs_1_.refs_2_.refs_3_.refs_8_.refs_9_.refs_10_.refs_17_ = bf16[256,1664]{1,0:T(8,128)(2,1)S(1)} custom-call(s32[2]{0:T(128)S(1)} %copy-done.45, f32[1,3072]{1,0:T(1,128)S(1)} %copy-done.37, bf16[128,1536]{1,0:T(8,128)(2,1)S(1)} %copy-done.24, bf16[128,1536]{1,0:T(8,128)(2,1)S(1)} %copy-done.26, bf16[128,1536]{1,0:T(8,128)(2,1)S(1)} %copy-done.28, ...), custom_call_target="tpu_custom_call" | custom-call | flops 1207959552 | bytes 4718592 | tf_op jit(solution)/shard_map/project/pallas_call | solution.py:108
  115.5 1.7 mix.8.refs_17_.mine_ref
  117.7 1.7 mix.9._.mine_ref
  120.0 1.7 emit.8
  123.0 1.5 collective-permute-start.19
  124.5 3.2 %mix.10._.mine_ref = bf16[128,512]{1,0:T(8,128)(2,1)S(1)} custom-call(s32[2]{0:T(128)S(1)} %copy-done.45, s32[6,5]{1,0:T(8,128)S(1)} %stack.43.table_ref, bf16[256,1664]{1,0:T(8,128)(2,1)S(1)} %project.11.refs_0_.refs_1_.refs_2_.refs_3_.refs_8_.refs_9_.refs_10_.refs_17_, ...), custom_call_target="tpu_custom_call" | custom-call | flops 134217728 | bytes 2097152 | tf_op jit(solution)/shard_map/mix/pallas_call | solution.py:249
  128.3 1.7 emit.9
  130.0 3.0 %mix.11._.mine_ref = bf16[128,512]{1,0:T(8,128)(2,1)S(1)} custom-call(s32[2]{0:T(128)S(1)} %copy-done.45, s32[6,5]{1,0:T(8,128)S(1)} %stack.43.table_ref, bf16[384,1664]{1,0:T(8,128)(2,1)S(1)} %project.8.refs_0_.refs_1_.refs_2_.refs_3_.refs_8_.refs_9_.refs_10_.refs_17_, ...), custom_call_target="tpu_custom_call" | custom-call | flops 134217728 | bytes 2097152 | tf_op jit(solution)/shard_map/mix/pallas_call | solution.py:249
  133.9 3.0 %emit.10 = (bf16[64,3072]{1,0:T(8,128)(2,1)S(1)}, bf16[64,3072]{1,0:T(8,128)(2,1)S(1)}) custom-call(s32[2]{0:T(128)S(1)} %copy-done.45, s32[6,5]{1,0:T(8,128)S(1)} %stack.43.table_ref, bf16[128,512]{1,0:T(8,128)(2,1)S(1)} %mix.10._.mine_ref, bf16[128,512]{1,0:T(8,128)(2,1)S(1)} %collective-permute-done.17.theirs_ref, bf16[1024,3072]{1,0:T(8,128)(2,1)S(1)} %bitcast.52, ...), custom_call_target="tpu_custom_call" | custom-call | flops 805306368 | bytes 6291456 | tf_op jit(solution)/shard_map/emit/pallas_call | solution.py:300
  136.9 3.0 %emit.11 = (bf16[64,3072]{1,0:T(8,128)(2,1)S(1)}, bf16[64,3072]{1,0:T(8,128)(2,1)S(1)}) custom-call(s32[2]{0:T(128)S(1)} %copy-done.45, s32[6,5]{1,0:T(8,128)S(1)} %stack.43.table_ref, bf16[128,512]{1,0:T(8,128)(2,1)S(1)} %mix.11._.mine_ref, bf16[128,512]{1,0:T(8,128)(2,1)S(1)} %collective-permute-done.22.theirs_ref, bf16[1024,3072]{1,0:T(8,128)(2,1)S(1)} %bitcast.54, ...), custom_call_target="tpu_custom_call" | custom-call | flops 805306368 | bytes 6291456 | tf_op jit(solution)/shard_map/emit/pallas_call | solution.py:300
  140.1 4.0 %collective-permute-start.27 = (bf16[64,3072]{1,0:T(8,128)(2,1)S(1)}, bf16[64,3072]{1,0:T(8,128)(2,1)S(1)}, u32[]{:S(2)}, u32[]{:S(2)}) collective-permute-start(bf16[64,3072]{1,0:T(8,128)(2,1)S(1)} %get-tuple-element.41), channel_id=1, source_target_pairs={{0,4},{4,8},{1,5},{5,9},{2,6},{6,10},{3,7},{7,11},{16,20},{20,24},... | collective-permute-start | bytes 1179656 | tf_op jit(solution)/shard_map/ppermute | solution.py:453
  144.1 1.3 collective-permute-start.29
  145.5 4.7 %collective-permute-start.20 = (bf16[64,3072]{1,0:T(8,128)(2,1)S(1)}, bf16[64,3072]{1,0:T(8,128)(2,1)S(1)}, u32[]{:S(2)}, u32[]{:S(2)}) collective-permute-start(bf16[64,3072]{1,0:T(8,128)(2,1)S(1)} %get-tuple-element.39), channel_id=1, source_target_pairs={{0,4},{4,8},{1,5},{5,9},{2,6},{6,10},{3,7},{7,11},{16,20},{20,24},... | collective-permute-start | bytes 1179656 | tf_op jit(solution)/shard_map/ppermute | solution.py:453
  151.5 2.4 %collective-permute-done.27 = bf16[64,3072]{1,0:T(8,128)(2,1)S(1)} collective-permute-done((bf16[64,3072]{1,0:T(8,128)(2,1)S(1)}, bf16[64,3072]{1,0:T(8,128)(2,1)S(1)}, u32[]{:S(2)}, u32[]{:S(2)}) %collective-permute-start.27) | collective-permute-done | bytes 393248 | tf_op jit(solution)/shard_map/ppermute | solution.py:453
  154.1 4.0 %collective-permute-start.28 = (bf16[64,3072]{1,0:T(8,128)(2,1)S(1)}, bf16[64,3072]{1,0:T(8,128)(2,1)S(1)}, u32[]{:S(2)}, u32[]{:S(2)}) collective-permute-start(bf16[64,3072]{1,0:T(8,128)(2,1)S(1)} %add_convert_fusion.1), channel_id=1, source_target_pairs={{0,4},{4,8},{8,12},{1,5},{5,9},{9,13},{2,6},{6,10},{10,14},{3,7},{... | collective-permute-start | bytes 1179656 | tf_op jit(solution)/shard_map/ppermute | solution.py:453
  158.2 2.1 %collective-permute-start.30 = (bf16[64,3072]{1,0:T(8,128)(2,1)S(1)}, bf16[64,3072]{1,0:T(8,128)(2,1)S(1)}, u32[]{:S(2)}, u32[]{:S(2)}) collective-permute-start(bf16[64,3072]{1,0:T(8,128)(2,1)S(1)} %add_convert_fusion), channel_id=1, source_target_pairs={{4,0},{8,4},{12,8},{5,1},{9,5},{13,9},{6,2},{10,6},{14,10},{7,3},{... | collective-permute-start | bytes 1179656 | tf_op jit(solution)/shard_map/ppermute | solution.py:453
  160.2 2.1 %collective-permute-done.20 = bf16[64,3072]{1,0:T(8,128)(2,1)S(1)} collective-permute-done((bf16[64,3072]{1,0:T(8,128)(2,1)S(1)}, bf16[64,3072]{1,0:T(8,128)(2,1)S(1)}, u32[]{:S(2)}, u32[]{:S(2)}) %collective-permute-start.20) | collective-permute-done | bytes 393248 | tf_op jit(solution)/shard_map/ppermute | solution.py:453
  162.5 4.0 %collective-permute-start.21 = (bf16[64,3072]{1,0:T(8,128)(2,1)S(1)}, bf16[64,3072]{1,0:T(8,128)(2,1)S(1)}, u32[]{:S(2)}, u32[]{:S(2)}) collective-permute-start(bf16[64,3072]{1,0:T(8,128)(2,1)S(1)} %add_convert_fusion.3), channel_id=1, source_target_pairs={{0,4},{4,8},{8,12},{1,5},{5,9},{9,13},{2,6},{6,10},{10,14},{3,7},{... | collective-permute-start | bytes 1179656 | tf_op jit(solution)/shard_map/ppermute | solution.py:453
  166.6 2.1 %collective-permute-start.24 = (bf16[64,3072]{1,0:T(8,128)(2,1)S(1)}, bf16[64,3072]{1,0:T(8,128)(2,1)S(1)}, u32[]{:S(2)}, u32[]{:S(2)}) collective-permute-start(bf16[64,3072]{1,0:T(8,128)(2,1)S(1)} %add_convert_fusion.2), channel_id=1, source_target_pairs={{4,0},{8,4},{12,8},{5,1},{9,5},{13,9},{6,2},{10,6},{14,10},{7,3},{... | collective-permute-start | bytes 1179656 | tf_op jit(solution)/shard_map/ppermute | solution.py:453
  169.1 1.7 collective-permute-done.28.refs_2_
  170.8 4.0 %collective-permute-done.30.refs_3_ = bf16[64,3072]{1,0:T(8,128)(2,1)S(1)} collective-permute-done((bf16[64,3072]{1,0:T(8,128)(2,1)S(1)}, bf16[64,3072]{1,0:T(8,128)(2,1)S(1)}, u32[]{:S(2)}, u32[]{:S(2)}) %collective-permute-start.30) | collective-permute-done | bytes 393248 | tf_op jit(solution)/shard_map/ppermute | solution.py:453
  175.2 1.6 collective-permute-start.31
  176.8 2.0 %collective-permute-done.21.refs_2_ = bf16[64,3072]{1,0:T(8,128)(2,1)S(1)} collective-permute-done((bf16[64,3072]{1,0:T(8,128)(2,1)S(1)}, bf16[64,3072]{1,0:T(8,128)(2,1)S(1)}, u32[]{:S(2)}, u32[]{:S(2)}) %collective-permute-start.21) | collective-permute-done | bytes 393248 | tf_op jit(solution)/shard_map/ppermute | solution.py:453
  178.8 3.7 %collective-permute-done.24.refs_3_ = bf16[64,3072]{1,0:T(8,128)(2,1)S(1)} collective-permute-done((bf16[64,3072]{1,0:T(8,128)(2,1)S(1)}, bf16[64,3072]{1,0:T(8,128)(2,1)S(1)}, u32[]{:S(2)}, u32[]{:S(2)}) %collective-permute-start.24) | collective-permute-done | bytes 393248 | tf_op jit(solution)/shard_map/ppermute | solution.py:453
  182.8 1.6 collective-permute-start.25
  185.5 7.7 %collective-permute-done.25 = bf16[64,3072]{1,0:T(8,128)(2,1)S(1)} collective-permute-done((bf16[64,3072]{1,0:T(8,128)(2,1)S(1)}, bf16[64,3072]{1,0:T(8,128)(2,1)S(1)}, u32[]{:S(2)}, u32[]{:S(2)}) %collective-permute-start.25) | collective-permute-done | bytes 393248 | tf_op jit(solution)/shard_map/ppermute | solution.py:475
  (194 shorter events, 29.5 us)
Async XLA Ops:
  0.6 13.9 %copy-start.5 = (bf16[512,256]{1,0:T(8,128)(2,1)S(1)}, bf16[512,256]{1,0:T(8,128)(2,1)}, u32[]{:S(2)}) copy-start(bf16[512,256]{1,0:T(8,128)(2,1)} %constant.55.forward_ref.refs_15_) | copy-start | bytes 786436
  0.6 13.9 %copy-start.7 = (bf16[1,128,3072]{2,1,0:T(8,128)(2,1)S(1)}, bf16[1,128,3072]{2,1,0:T(8,128)(2,1)}, u32[]{:S(2)}) copy-start(bf16[1,128,3072]{2,1,0:T(8,128)(2,1)} %param.13) | copy-start | bytes 2359300
  0.7 13.9 %copy-start.42 = (bf16[1,1024,128]{2,1,0:T(8,128)(2,1)S(1)}, bf16[1,1024,128]{2,1,0:T(8,128)(2,1)}, u32[]{:S(2)}) copy-start(bf16[1,1024,128]{2,1,0:T(8,128)(2,1)} %param.16) | copy-start | bytes 786436
  1.9 17.5 %copy-start.37 = (f32[1,3072]{1,0:T(1,128)S(1)}, f32[1,3072]{1,0:T(1,128)}, u32[]{:S(2)}) copy-start(f32[1,3072]{1,0:T(1,128)} %refs_1_.7) | copy-start | bytes 36868
  1.9 14.0 %collective-permute-start.2 = (bf16[128,1536]{1,0:T(8,128)(2,1)S(1)}, bf16[128,1536]{1,0:T(8,128)(2,1)}, u32[]{:S(2)}, u32[]{:S(2)}) collective-permute-start(bf16[128,1536]{1,0:T(8,128)(2,1)S(1)} %get-tuple-element.36.refs_1_), channel_id=1, source_target_pairs={{0,4},{4,8},{8,12},{1,5},{5,9},{9,13},{2,6},{6,10},{10,14},{3,7},{... | collective-permute-start | bytes 1179656 | tf_op jit(solution)/shard_map/ppermute | solution.py:390
  5.4 14.0 %collective-permute-start.3 = (bf16[128,1536]{1,0:T(8,128)(2,1)S(1)}, bf16[128,1536]{1,0:T(8,128)(2,1)}, u32[]{:S(2)}, u32[]{:S(2)}) collective-permute-start(bf16[128,1536]{1,0:T(8,128)(2,1)S(1)} %get-tuple-element.36.refs_1_), channel_id=1, source_target_pairs={{4,0},{8,4},{12,8},{5,1},{9,5},{13,9},{6,2},{10,6},{14,10},{7,3},{... | collective-permute-start | bytes 1179656 | tf_op jit(solution)/shard_map/ppermute | solution.py:392
  8.5 19.4 %collective-permute-start = (bf16[128,1536]{1,0:T(8,128)(2,1)S(1)}, bf16[128,1536]{1,0:T(8,128)(2,1)S(1)}, u32[]{:S(2)}, u32[]{:S(2)}) collective-permute-start(bf16[128,1536]{1,0:T(8,128)(2,1)S(1)} %get-tuple-element.37.refs_2_), channel_id=1, source_target_pairs={{0,4},{4,8},{8,12},{1,5},{5,9},{9,13},{2,6},{6,10},{10,14},{3,7},{... | collective-permute-start | bytes 1179656 | tf_op jit(solution)/shard_map/ppermute | solution.py:390
  11.3 16.6 %collective-permute-start.1 = (bf16[128,1536]{1,0:T(8,128)(2,1)S(1)}, bf16[128,1536]{1,0:T(8,128)(2,1)S(1)}, u32[]{:S(2)}, u32[]{:S(2)}) collective-permute-start(bf16[128,1536]{1,0:T(8,128)(2,1)S(1)} %get-tuple-element.37.refs_2_), channel_id=1, source_target_pairs={{4,0},{8,4},{12,8},{5,1},{9,5},{13,9},{6,2},{10,6},{14,10},{7,3},{... | collective-permute-start | bytes 1179656 | tf_op jit(solution)/shard_map/ppermute | solution.py:392
  14.5 13.4 %copy-start.43 = (s32[2]{0:T(128)}, s32[2]{0:T(128)S(1)}, u32[]{:S(2)}) copy-start(s32[2]{0:T(128)S(1)} %pad_add_fusion.refs_0_.sides_ref) | copy-start | bytes 28
  15.5 12.3 %copy-start = (f32[256,1024]{1,0:T(8,128)}, f32[256,1024]{1,0:T(8,128)S(1)}, u32[]{:S(2)}) copy-start(f32[256,1024]{1,0:T(8,128)S(1)} %spectrum.1.refs_5_.refs_14_) | copy-start | bytes 3145732
  35.6 28.3 %collective-permute-start.4 = (bf16[384,1664]{1,0:T(8,128)(2,1)}, bf16[384,1664]{1,0:T(8,128)(2,1)S(1)}, u32[]{:S(2)}, u32[]{:S(2)}) collective-permute-start(bf16[384,1664]{1,0:T(8,128)(2,1)} %project.7.refs_8_), channel_id=1, source_target_pairs={{0,1},{1,0},{2,3},{3,2},{4,5},{5,4},{6,7},{7,6},{8,9},{9,8},{10,11... | collective-permute-start | bytes 3833864 | tf_op jit(solution)/shard_map/ppermute | solution.py:432
  35.6 26.2 %collective-permute-start.11 = (bf16[128,1536]{1,0:T(8,128)(2,1)}, bf16[128,1536]{1,0:T(8,128)(2,1)}, u32[]{:S(2)}, u32[]{:S(2)}) collective-permute-start(bf16[128,1536]{1,0:T(8,128)(2,1)} %collective-permute-done.2.refs_2_), channel_id=1, source_target_pairs={{4,8},{8,12},{5,9},{9,13},{6,10},{10,14},{7,11},{11,15},{20,24},{2... | collective-permute-start | bytes 1179656 | tf_op jit(solution)/shard_map/ppermute | solution.py:390
  39.9 22.7 %collective-permute-start.12 = (bf16[128,1536]{1,0:T(8,128)(2,1)}, bf16[128,1536]{1,0:T(8,128)(2,1)}, u32[]{:S(2)}, u32[]{:S(2)}) collective-permute-start(bf16[128,1536]{1,0:T(8,128)(2,1)} %collective-permute-done.3.refs_3_), channel_id=1, source_target_pairs={{4,0},{8,4},{5,1},{9,5},{6,2},{10,6},{7,3},{11,7},{20,16},{24,20},... | collective-permute-start | bytes 1179656 | tf_op jit(solution)/shard_map/ppermute | solution.py:392
  44.3 19.6 %copy-start.1 = (f32[256,1024]{1,0:T(8,128)S(1)}, f32[256,1024]{1,0:T(8,128)}, u32[]{:S(2)}) copy-start(f32[256,1024]{1,0:T(8,128)} %copy-done) | copy-start | bytes 3145732
  44.3 25.2 %collective-permute-start.7 = (bf16[128,1536]{1,0:T(8,128)(2,1)}, bf16[128,1536]{1,0:T(8,128)(2,1)S(1)}, u32[]{:S(2)}, u32[]{:S(2)}) collective-permute-start(bf16[128,1536]{1,0:T(8,128)(2,1)} %copy-done.21), channel_id=1, source_target_pairs={{4,8},{8,12},{5,9},{9,13},{6,10},{10,14},{7,11},{11,15},{20,24},{2... | collective-permute-start | bytes 1179656 | tf_op jit(solution)/shard_map/ppermute | solution.py:390
  49.1 21.2 %collective-permute-start.8 = (bf16[128,1536]{1,0:T(8,128)(2,1)}, bf16[128,1536]{1,0:T(8,128)(2,1)S(1)}, u32[]{:S(2)}, u32[]{:S(2)}) collective-permute-start(bf16[128,1536]{1,0:T(8,128)(2,1)} %copy-done.19), channel_id=1, source_target_pairs={{4,0},{8,4},{5,1},{9,5},{6,2},{10,6},{7,3},{11,7},{20,16},{24,20},... | collective-permute-start | bytes 1179656 | tf_op jit(solution)/shard_map/ppermute | solution.py:392
  61.9 22.6 %collective-permute-start.13 = (bf16[128,1536]{1,0:T(8,128)(2,1)}, bf16[128,1536]{1,0:T(8,128)(2,1)S(1)}, u32[]{:S(2)}, u32[]{:S(2)}) collective-permute-start(bf16[128,1536]{1,0:T(8,128)(2,1)} %collective-permute-done.11.refs_1_), channel_id=1, source_target_pairs={{8,12},{9,13},{10,14},{11,15},{24,28},{25,29},{26,30},{27,31}} | collective-permute-start | bytes 1179656 | tf_op jit(solution)/shard_map/ppermute | solution.py:390
  62.6 21.9 %collective-permute-start.14 = (bf16[128,1536]{1,0:T(8,128)(2,1)}, bf16[128,1536]{1,0:T(8,128)(2,1)S(1)}, u32[]{:S(2)}, u32[]{:S(2)}) collective-permute-start(bf16[128,1536]{1,0:T(8,128)(2,1)} %collective-permute-done.12.refs_2_), channel_id=1, source_target_pairs={{4,0},{5,1},{6,2},{7,3},{20,16},{21,17},{22,18},{23,19}} | collective-permute-start | bytes 1179656 | tf_op jit(solution)/shard_map/ppermute | solution.py:392
  67.1 9.8 %copy-start.12 = (bf16[128,512]{1,0:T(8,128)(2,1)}, bf16[128,512]{1,0:T(8,128)(2,1)S(1)}, u32[]{:S(2)}) copy-start(bf16[128,512]{1,0:T(8,128)(2,1)S(1)} %mix.6.refs_17_.mine_ref) | copy-start | bytes 393220
  67.2 8.1 %collective-permute-start.5 = (bf16[128,512]{1,0:T(8,128)(2,1)S(1)}, bf16[128,512]{1,0:T(8,128)(2,1)S(1)}, u32[]{:S(2)}, u32[]{:S(2)}) collective-permute-start(bf16[128,512]{1,0:T(8,128)(2,1)S(1)} %mix.6.refs_17_.mine_ref), channel_id=1, source_target_pairs={{0,1},{1,0},{2,3},{3,2},{4,5},{5,4},{6,7},{7,6},{8,9},{9,8},{10,11... | collective-permute-start | bytes 393224 | tf_op jit(solution)/shard_map/ppermute | solution.py:407
  69.5 22.8 %copy-start.23 = (bf16[128,1536]{1,0:T(8,128)(2,1)}, bf16[128,1536]{1,0:T(8,128)(2,1)S(1)}, u32[]{:S(2)}) copy-start(bf16[128,1536]{1,0:T(8,128)(2,1)S(1)} %collective-permute-done.7.refs_2_) | copy-start | bytes 1179652
  69.5 22.8 %collective-permute-start.9 = (bf16[128,1536]{1,0:T(8,128)(2,1)S(1)}, bf16[128,1536]{1,0:T(8,128)(2,1)S(1)}, u32[]{:S(2)}, u32[]{:S(2)}) collective-permute-start(bf16[128,1536]{1,0:T(8,128)(2,1)S(1)} %collective-permute-done.7.refs_2_), channel_id=1, source_target_pairs={{8,12},{9,13},{10,14},{11,15},{24,28},{25,29},{26,30},{27,31}} | collective-permute-start | bytes 1179656 | tf_op jit(solution)/shard_map/ppermute | solution.py:390
  70.4 22.0 %copy-start.25 = (bf16[128,1536]{1,0:T(8,128)(2,1)}, bf16[128,1536]{1,0:T(8,128)(2,1)S(1)}, u32[]{:S(2)}) copy-start(bf16[128,1536]{1,0:T(8,128)(2,1)S(1)} %collective-permute-done.8.refs_3_) | copy-start | bytes 1179652
  70.4 21.9 %collective-permute-start.10 = (bf16[128,1536]{1,0:T(8,128)(2,1)S(1)}, bf16[128,1536]{1,0:T(8,128)(2,1)S(1)}, u32[]{:S(2)}, u32[]{:S(2)}) collective-permute-start(bf16[128,1536]{1,0:T(8,128)(2,1)S(1)} %collective-permute-done.8.refs_3_), channel_id=1, source_target_pairs={{4,0},{5,1},{6,2},{7,3},{20,16},{21,17},{22,18},{23,19}} | collective-permute-start | bytes 1179656 | tf_op jit(solution)/shard_map/ppermute | solution.py:392
  75.2 5.5 %collective-permute-start.6 = (bf16[128,512]{1,0:T(8,128)(2,1)S(1)}, bf16[128,512]{1,0:T(8,128)(2,1)S(1)}, u32[]{:S(2)}, u32[]{:S(2)}) collective-permute-start(bf16[128,512]{1,0:T(8,128)(2,1)S(1)} %mix.7._.mine_ref), channel_id=1, source_target_pairs={{0,1},{1,0},{2,3},{3,2},{4,5},{5,4},{6,7},{7,6},{8,9},{9,8},{10,11... | collective-permute-start | bytes 393224 | tf_op jit(solution)/shard_map/ppermute | solution.py:407
  98.9 16.5 %collective-permute-start.15 = (bf16[256,1664]{1,0:T(8,128)(2,1)}, bf16[256,1664]{1,0:T(8,128)(2,1)S(1)}, u32[]{:S(2)}, u32[]{:S(2)}) collective-permute-start(bf16[256,1664]{1,0:T(8,128)(2,1)} %project.10.refs_9_), channel_id=1, source_target_pairs={{0,1},{1,0},{2,3},{3,2},{4,5},{5,4},{6,7},{7,6},{8,9},{9,8},{10,11... | collective-permute-start | bytes 2555912 | tf_op jit(solution)/shard_map/ppermute | solution.py:432
  109.5 10.5 %slice-start.2 = ((s8[6291456]{0:T(1024)(128)(4,1)}), s8[4194304]{0:T(1024)(128)(4,1)S(1)}, s32[]{:S(2)}) async-start(s8[6291456]{0:T(1024)(128)(4,1)} %bitcast.46), calls=%async_computation.2 | async-start | bytes 8388608
  117.2 2.8 %collective-permute-start.16 = (bf16[128,512]{1,0:T(8,128)(2,1)S(1)}, bf16[128,512]{1,0:T(8,128)(2,1)S(1)}, u32[]{:S(2)}, u32[]{:S(2)}) collective-permute-start(bf16[128,512]{1,0:T(8,128)(2,1)S(1)} %mix.8.refs_17_.mine_ref), channel_id=1, source_target_pairs={{0,1},{1,0},{2,3},{3,2},{4,5},{5,4},{6,7},{7,6},{8,9},{9,8},{10,11... | collective-permute-start | bytes 393224 | tf_op jit(solution)/shard_map/ppermute | solution.py:407
  119.4 8.8 %collective-permute-start.18 = (bf16[128,512]{1,0:T(8,128)(2,1)S(1)}, bf16[128,512]{1,0:T(8,128)(2,1)S(1)}, u32[]{:S(2)}, u32[]{:S(2)}) collective-permute-start(bf16[128,512]{1,0:T(8,128)(2,1)S(1)} %mix.9._.mine_ref), channel_id=1, source_target_pairs={{0,1},{1,0},{2,3},{3,2},{4,5},{5,4},{6,7},{7,6},{8,9},{9,8},{10,11... | collective-permute-start | bytes 393224 | tf_op jit(solution)/shard_map/ppermute | solution.py:407
  121.7 18.2 %collective-permute-start.26 = (bf16[64,3072]{1,0:T(8,128)(2,1)S(1)}, bf16[64,3072]{1,0:T(8,128)(2,1)S(1)}, u32[]{:S(2)}, u32[]{:S(2)}) collective-permute-start(bf16[64,3072]{1,0:T(8,128)(2,1)S(1)} %get-tuple-element.31), channel_id=1, source_target_pairs={{0,4},{12,8},{1,5},{13,9},{2,6},{14,10},{3,7},{15,11},{16,20},{28,... | collective-permute-start | bytes 1179656 | tf_op jit(solution)/shard_map/ppermute | solution.py:453
  123.0 22.4 %collective-permute-start.19 = (bf16[64,3072]{1,0:T(8,128)(2,1)S(1)}, bf16[64,3072]{1,0:T(8,128)(2,1)S(1)}, u32[]{:S(2)}, u32[]{:S(2)}) collective-permute-start(bf16[64,3072]{1,0:T(8,128)(2,1)S(1)} %get-tuple-element.24.refs_17_), channel_id=1, source_target_pairs={{0,4},{12,8},{1,5},{13,9},{2,6},{14,10},{3,7},{15,11},{16,20},{28,... | collective-permute-start | bytes 1179656 | tf_op jit(solution)/shard_map/ppermute | solution.py:453
  127.7 6.2 %collective-permute-start.17 = (bf16[128,512]{1,0:T(8,128)(2,1)S(1)}, bf16[128,512]{1,0:T(8,128)(2,1)S(1)}, u32[]{:S(2)}, u32[]{:S(2)}) collective-permute-start(bf16[128,512]{1,0:T(8,128)(2,1)S(1)} %mix.10._.mine_ref), channel_id=1, source_target_pairs={{0,1},{1,0},{2,3},{3,2},{4,5},{5,4},{6,7},{7,6},{8,9},{9,8},{10,11... | collective-permute-start | bytes 393224 | tf_op jit(solution)/shard_map/ppermute | solution.py:407
  133.0 3.9 %collective-permute-start.22 = (bf16[128,512]{1,0:T(8,128)(2,1)S(1)}, bf16[128,512]{1,0:T(8,128)(2,1)S(1)}, u32[]{:S(2)}, u32[]{:S(2)}) collective-permute-start(bf16[128,512]{1,0:T(8,128)(2,1)S(1)} %mix.11._.mine_ref), channel_id=1, source_target_pairs={{0,1},{1,0},{2,3},{3,2},{4,5},{5,4},{6,7},{7,6},{8,9},{9,8},{10,11... | collective-permute-start | bytes 393224 | tf_op jit(solution)/shard_map/ppermute | solution.py:407
  139.9 14.1 %copy-start.41 = (bf16[64,3072]{1,0:T(8,128)(2,1)S(1)}, bf16[64,3072]{1,0:T(8,128)(2,1)}, u32[]{:S(2)}) copy-start(bf16[64,3072]{1,0:T(8,128)(2,1)} %copy-done.40) | copy-start | bytes 1179652
  140.1 13.9 %collective-permute-start.27 = (bf16[64,3072]{1,0:T(8,128)(2,1)S(1)}, bf16[64,3072]{1,0:T(8,128)(2,1)S(1)}, u32[]{:S(2)}, u32[]{:S(2)}) collective-permute-start(bf16[64,3072]{1,0:T(8,128)(2,1)S(1)} %get-tuple-element.41), channel_id=1, source_target_pairs={{0,4},{4,8},{1,5},{5,9},{2,6},{6,10},{3,7},{7,11},{16,20},{20,24},... | collective-permute-start | bytes 1179656 | tf_op jit(solution)/shard_map/ppermute | solution.py:453
  144.1 14.0 %collective-permute-start.29 = (bf16[64,3072]{1,0:T(8,128)(2,1)S(1)}, bf16[64,3072]{1,0:T(8,128)(2,1)S(1)}, u32[]{:S(2)}, u32[]{:S(2)}) collective-permute-start(bf16[64,3072]{1,0:T(8,128)(2,1)S(1)} %get-tuple-element.40), channel_id=1, source_target_pairs={{8,4},{12,8},{9,5},{13,9},{10,6},{14,10},{11,7},{15,11},{24,20},{2... | collective-permute-start | bytes 1179656 | tf_op jit(solution)/shard_map/ppermute | solution.py:453
  145.5 16.9 %copy-start.18 = (bf16[64,3072]{1,0:T(8,128)(2,1)S(1)}, bf16[64,3072]{1,0:T(8,128)(2,1)}, u32[]{:S(2)}) copy-start(bf16[64,3072]{1,0:T(8,128)(2,1)} %copy-done.17) | copy-start | bytes 1179652
  145.5 16.8 %collective-permute-start.20 = (bf16[64,3072]{1,0:T(8,128)(2,1)S(1)}, bf16[64,3072]{1,0:T(8,128)(2,1)S(1)}, u32[]{:S(2)}, u32[]{:S(2)}) collective-permute-start(bf16[64,3072]{1,0:T(8,128)(2,1)S(1)} %get-tuple-element.39), channel_id=1, source_target_pairs={{0,4},{4,8},{1,5},{5,9},{2,6},{6,10},{3,7},{7,11},{16,20},{20,24},... | collective-permute-start | bytes 1179656 | tf_op jit(solution)/shard_map/ppermute | solution.py:453
  150.2 16.2 %collective-permute-start.23 = (bf16[64,3072]{1,0:T(8,128)(2,1)S(1)}, bf16[64,3072]{1,0:T(8,128)(2,1)S(1)}, u32[]{:S(2)}, u32[]{:S(2)}) collective-permute-start(bf16[64,3072]{1,0:T(8,128)(2,1)S(1)} %get-tuple-element.38), channel_id=1, source_target_pairs={{8,4},{12,8},{9,5},{13,9},{10,6},{14,10},{11,7},{15,11},{24,20},{2... | collective-permute-start | bytes 1179656 | tf_op jit(solution)/shard_map/ppermute | solution.py:453
  154.1 16.8 %collective-permute-start.28 = (bf16[64,3072]{1,0:T(8,128)(2,1)S(1)}, bf16[64,3072]{1,0:T(8,128)(2,1)S(1)}, u32[]{:S(2)}, u32[]{:S(2)}) collective-permute-start(bf16[64,3072]{1,0:T(8,128)(2,1)S(1)} %add_convert_fusion.1), channel_id=1, source_target_pairs={{0,4},{4,8},{8,12},{1,5},{5,9},{9,13},{2,6},{6,10},{10,14},{3,7},{... | collective-permute-start | bytes 1179656 | tf_op jit(solution)/shard_map/ppermute | solution.py:453
  158.2 16.6 %copy-start.8 = (bf16[1,128,3072]{2,1,0:T(8,128)(2,1)S(1)}, bf16[1,128,3072]{2,1,0:T(8,128)(2,1)}, u32[]{:S(2)}) copy-start(bf16[1,128,3072]{2,1,0:T(8,128)(2,1)} %param.13) | copy-start | bytes 2359300
  158.2 16.6 %copy-start.39 = (bf16[64,3072]{1,0:T(8,128)(2,1)S(1)}, bf16[64,3072]{1,0:T(8,128)(2,1)}, u32[]{:S(2)}) copy-start(bf16[64,3072]{1,0:T(8,128)(2,1)} %copy-done.38) | copy-start | bytes 1179652
  158.2 16.6 %collective-permute-start.30 = (bf16[64,3072]{1,0:T(8,128)(2,1)S(1)}, bf16[64,3072]{1,0:T(8,128)(2,1)S(1)}, u32[]{:S(2)}, u32[]{:S(2)}) collective-permute-start(bf16[64,3072]{1,0:T(8,128)(2,1)S(1)} %add_convert_fusion), channel_id=1, source_target_pairs={{4,0},{8,4},{12,8},{5,1},{9,5},{13,9},{6,2},{10,6},{14,10},{7,3},{... | collective-permute-start | bytes 1179656 | tf_op jit(solution)/shard_map/ppermute | solution.py:453
  162.5 16.3 %collective-permute-start.21 = (bf16[64,3072]{1,0:T(8,128)(2,1)S(1)}, bf16[64,3072]{1,0:T(8,128)(2,1)S(1)}, u32[]{:S(2)}, u32[]{:S(2)}) collective-permute-start(bf16[64,3072]{1,0:T(8,128)(2,1)S(1)} %add_convert_fusion.3), channel_id=1, source_target_pairs={{0,4},{4,8},{8,12},{1,5},{5,9},{9,13},{2,6},{6,10},{10,14},{3,7},{... | collective-permute-start | bytes 1179656 | tf_op jit(solution)/shard_map/ppermute | solution.py:453
  166.6 15.8 %copy-start.16 = (bf16[64,3072]{1,0:T(8,128)(2,1)S(1)}, bf16[64,3072]{1,0:T(8,128)(2,1)}, u32[]{:S(2)}) copy-start(bf16[64,3072]{1,0:T(8,128)(2,1)} %copy-done.15) | copy-start | bytes 1179652
  166.6 15.8 %collective-permute-start.24 = (bf16[64,3072]{1,0:T(8,128)(2,1)S(1)}, bf16[64,3072]{1,0:T(8,128)(2,1)S(1)}, u32[]{:S(2)}, u32[]{:S(2)}) collective-permute-start(bf16[64,3072]{1,0:T(8,128)(2,1)S(1)} %add_convert_fusion.2), channel_id=1, source_target_pairs={{4,0},{8,4},{12,8},{5,1},{9,5},{13,9},{6,2},{10,6},{14,10},{7,3},{... | collective-permute-start | bytes 1179656 | tf_op jit(solution)/shard_map/ppermute | solution.py:453
  175.2 10.3 %collective-permute-start.31 = (bf16[64,3072]{1,0:T(8,128)(2,1)S(1)}, bf16[64,3072]{1,0:T(8,128)(2,1)S(1)}, u32[]{:S(2)}, u32[]{:S(2)}) collective-permute-start(bf16[64,3072]{1,0:T(8,128)(2,1)S(1)} %finish.3), channel_id=1, source_target_pairs={{0,2},{2,0},{1,3},{3,1},{4,6},{6,4},{5,7},{7,5},{8,10},{10,8},{9,1... | collective-permute-start | bytes 1179656 | tf_op jit(solution)/shard_map/ppermute | solution.py:475
  182.8 10.4 %collective-permute-start.25 = (bf16[64,3072]{1,0:T(8,128)(2,1)S(1)}, bf16[64,3072]{1,0:T(8,128)(2,1)S(1)}, u32[]{:S(2)}, u32[]{:S(2)}) collective-permute-start(bf16[64,3072]{1,0:T(8,128)(2,1)S(1)} %finish.2), channel_id=1, source_target_pairs={{0,2},{2,0},{1,3},{3,1},{4,6},{6,4},{5,7},{7,5},{8,10},{10,8},{9,1... | collective-permute-start | bytes 1179656 | tf_op jit(solution)/shard_map/ppermute | solution.py:475
  (43 other events, 182.1 us)

commit v2 on v1

v2 whole, which is shorter than its diff:
```python
import functools

import jax
import jax.numpy as jnp
import ml_dtypes
import numpy as np
from jax import lax
from jax.experimental import pallas as pl
from jax.experimental.pallas import tpu as pltpu
from jax.sharding import PartitionSpec as P


norm_eps = 1e-06
lanes = 128
halves = 2
vmem_limit = 60 * 1024 * 1024


def tile_of(extent, most):
    tile = min(extent, most)
    while extent % tile:
        tile //= 2
    return tile


def block_of(slot, z):
    kind, k = slot[:2]
    below = z - k
    return z + k if kind == "d" else jnp.where(z == 0, k, below) if kind == "m" else below


def params():
    return pltpu.CompilerParams(vmem_limit_bytes=vmem_limit)


def prepare_kernel(x_ref, gain_ref, *refs):
    part = refs[0].shape[1]
    total = jnp.zeros((x_ref.shape[0], 1), jnp.float32)
    for index, out_ref in enumerate(refs[:-1]):
        place = slice(index * part, (index + 1) * part)
        x = x_ref[:, place].astype(jnp.float32)
        out_ref[...] = (x * gain_ref[:, place]).astype(jnp.bfloat16)
        total = total + jnp.sum(x * x, axis=1, keepdims=True)
    refs[-1][...] = jnp.broadcast_to(total, refs[-1].shape)


def prepare(x, gain):
    rows, width = x.shape
    return pl.pallas_call(
        prepare_kernel,
        out_shape=[jax.ShapeDtypeStruct((rows, width // halves), jnp.bfloat16)] * halves
        + [jax.ShapeDtypeStruct((rows, lanes), jnp.float32)],
        compiler_params=params(),
        name="prepare",
    )(x, gain)


def project_kernel(layout, parts, first, *refs):
    x_refs = refs[1 : 1 + sum(layout) * parts]
    refs = refs[1 + sum(layout) * parts :]
    carry_ref = None if first else refs[0]
    w_ref, _, out_ref, joined = refs if first else refs[1:]

    @pl.when(pl.program_id(0) == 0)
    def _():
        chunk, depth = x_refs[0].shape
        source = 0
        for part in range(parts):
            for index, inputs in enumerate(layout):
                x = x_refs[source][...]
                for other in range(1, inputs):
                    x = x + x_refs[source + other][...]
                source += inputs
                joined[index * chunk : (index + 1) * chunk, part * depth : (part + 1) * depth] = x

    total = jnp.dot(joined[...], w_ref[0], preferred_element_type=jnp.float32)
    if not first:
        total = total + carry_ref[...]
    out_ref[...] = total.astype(out_ref.dtype)


def project(pieces, layout, w, part, carry, side, info, after):
    streams, _, channels = w.shape
    chunk, depth = pieces[0][0].shape
    rows = chunk * len(layout)
    deep = depth * len(pieces)
    final = side is not None
    first = carry is None
    tile = channels // 2
    steps = streams if final else 2 * streams

    def channel(i, held):
        return i * 2 + held[side] if final else i

    column = pl.BlockSpec((rows, tile), lambda i, held: (0, channel(i, held)))
    flat = [piece for group in pieces for piece in group]
    return pl.pallas_call(
        functools.partial(project_kernel, layout, len(pieces), first),
        grid_spec=pltpu.PrefetchScalarGridSpec(
            num_scalar_prefetch=1,
            grid=(steps,),
            in_specs=[pl.BlockSpec((chunk, depth), lambda i, held: (0, 0))] * len(flat)
            + ([] if first else [column])
            + [
                pl.BlockSpec(
                    (1, deep, tile), lambda i, held: (channel(i, held) // 2, part, channel(i, held) % 2)
                ),
                pl.BlockSpec(memory_space=pl.ANY),
            ],
            out_specs=pl.BlockSpec((rows, tile), lambda i, held: (0, i)),
            scratch_shapes=[pltpu.VMEM((rows, deep), jnp.bfloat16)],
        ),
        out_shape=jax.ShapeDtypeStruct((rows, steps * tile), jnp.bfloat16 if final else jnp.float32),
        compiler_params=params(),
        cost_estimate=pl.CostEstimate(
            flops=2 * rows * deep * steps * tile, bytes_accessed=2 * deep * steps * tile, transcendentals=0
        ),
        name="project",
    )(info, *flat, *(() if first else (carry,)), w, after)


def wave_tables(rows):
    window = 2 * rows
    angle = np.pi / window * (2 * np.arange(rows)[:, None] + 1) * np.arange(window)[None, :]
    forward = np.concatenate([np.cos(angle), np.sin(angle)], axis=0)
    inverse = forward[:, rows:].T * (2.0 / window)

    def pair(matrix):
        exact = jnp.asarray(matrix, jnp.float32)
        high = jnp.asarray(np.asarray(matrix, ml_dtypes.bfloat16))
        low = jnp.asarray(np.asarray(matrix - np.asarray(matrix, ml_dtypes.bfloat16).astype(np.float64), ml_dtypes.bfloat16))
        return high, low

    high, low = pair(forward)
    inverse_high, inverse_low = pair(inverse)
    return jnp.concatenate([high, low], axis=0), jnp.concatenate([inverse_high, inverse_low], axis=0)


def spectrum_kernel(taps_ref, forward_ref, _, out_ref):
    taps = taps_ref.shape[1]
    both = lax.dot_general(
        forward_ref[:, :taps], taps_ref[...], (((1,), (1,)), ((), ())), preferred_element_type=jnp.float32
    )
    half = out_ref.shape[0]
    out_ref[...] = both[:half, :] + both[half:, :]


def spectrum(taps, forward, after):
    channels = taps.shape[0]
    tile = tile_of(channels, 256)
    window = forward.shape[1]
    return pl.pallas_call(
        spectrum_kernel,
        grid=(channels // tile,),
        in_specs=[
            pl.BlockSpec((tile, taps.shape[1]), lambda i: (i, 0)),
            pl.BlockSpec(forward.shape, lambda i: (0, 0)),
            pl.BlockSpec(memory_space=pl.ANY),
        ],
        out_specs=pl.BlockSpec((window, tile), lambda i: (0, i)),
        out_shape=jax.ShapeDtypeStruct((window, channels), jnp.float32),
        compiler_params=params(),
        name="spectrum",
    )(taps, forward, after)


def mix_kernel(slot, info_ref, *refs):
    q0, k0, v0, q1, k1, v1, pk0, pv0, pk1, pv1, scale_ref, before_ref, f_ref, forward_ref, inverse_ref, _, out_ref, window = refs
    rows = out_ref.shape[0]
    block = block_of(slot, info_ref[2])
    length = info_ref[3]
    work = (block >= 0) & (block < slot[2])

    def joined(a_ref, b_ref):
        return a_ref[...].astype(jnp.float32) + b_ref[...].astype(jnp.float32)

    def wide(ref):
        return jnp.concatenate([ref[...]] * (out_ref.shape[1] // lanes), axis=1)

    @pl.when(work)
    def _():
        row = lax.broadcasted_iota(jnp.int32, (rows, 1), 0)
        scale = wide(scale_ref)
        live = (row + block * rows < length).astype(jnp.float32)
        here = joined(k0, k1) * scale * (joined(v0, v1) * scale) * live
        window[rows:, :] = here.astype(jnp.bfloat16)

        @pl.when(block > 0)
        def _():
            scale = wide(before_ref)
            live = (row + (block - 1) * rows < length).astype(jnp.float32)
            before = joined(pk0, pk1) * scale * (joined(pv0, pv1) * scale) * live
            window[:rows, :] = before.astype(jnp.bfloat16)

        @pl.when(block == 0)
        def _():
            window[:rows, :] = jnp.zeros((rows, window.shape[1]), jnp.bfloat16)

        both = jnp.dot(forward_ref[...], window[...], preferred_element_type=jnp.float32)
        cosine = both[:rows, :] + both[2 * rows : 3 * rows, :]
        sine = both[rows : 2 * rows, :] + both[3 * rows :, :]
        f_cosine = f_ref[:rows, :]
        f_sine = f_ref[rows:, :]
        product = jnp.concatenate(
            [cosine * f_cosine - sine * f_sine, cosine * f_sine + sine * f_cosine], axis=0
        )
        high = product.astype(jnp.bfloat16)
        low = (product - high.astype(jnp.float32)).astype(jnp.bfloat16)
        back = jnp.dot(inverse_ref[...], high, preferred_element_type=jnp.float32)
        conv = back[:rows, :] + back[rows:, :]
        conv = conv + jnp.dot(inverse_ref[:rows, :], low, preferred_element_type=jnp.float32)
        out_ref[...] = (joined(q0, q1) * scale * conv * live).astype(jnp.bfloat16)

    @pl.when(jnp.logical_not(work))
    def _():
        out_ref[...] = jnp.zeros_like(out_ref)


def mix(slot, here, before, rows, waves, filter_waves, scales, info, after):
    own, got, at = here
    own_before, got_before, at_before = before
    channels = filter_waves.shape[1] // 2
    tile = tile_of(channels, 256)
    per = channels // tile

    def spec(at, stream):
        return pl.BlockSpec((rows, tile), lambda i, held: (at, stream * per + i))

    def scale(offset):
        def index(i, held):
            return (jnp.clip(block_of(slot, held[2]) - offset, 0, slot[2] - 1), 0)

        return pl.BlockSpec((rows, lanes), index)

    whole = [pl.BlockSpec(wave.shape, lambda i, held: (0, 0)) for wave in waves]
    return pl.pallas_call(
        functools.partial(mix_kernel, slot),
        grid_spec=pltpu.PrefetchScalarGridSpec(
            num_scalar_prefetch=1,
            grid=(per,),
            in_specs=[spec(at, 0), spec(at, 1), spec(at, 2)] * 2
            + [spec(at_before, 1), spec(at_before, 2)] * 2
            + [scale(0), scale(1), pl.BlockSpec((2 * rows, tile), lambda i, held: (0, held[0] * per + i))]
            + whole
            + [pl.BlockSpec(memory_space=pl.ANY)],
            out_specs=pl.BlockSpec((rows, tile), lambda i, held: (0, i)),
            scratch_shapes=[pltpu.VMEM((2 * rows, tile), jnp.bfloat16)],
        ),
        out_shape=jax.ShapeDtypeStruct((rows, channels), jnp.bfloat16),
        compiler_params=params(),
        cost_estimate=pl.CostEstimate(
            flops=16 * rows * rows * channels, bytes_accessed=32 * rows * channels, transcendentals=0
        ),
        name="mix",
    )(
        info, own, own, own, got, got, got, own_before, own_before, got_before, got_before,
        scales, scales, filter_waves, *waves, after,
    )


def emit_kernel(slot, info_ref, mine_ref, theirs_ref, w_mine_ref, w_theirs_ref, _, *out_refs):
    block = block_of(slot, info_ref[2])
    work = (block >= 0) & (block < slot[2])
    chunk = out_refs[0].shape[0]

    @pl.when(work)
    def _():
        product = jnp.dot(mine_ref[...], w_mine_ref[...], preferred_element_type=jnp.float32)
        product = product + jnp.dot(theirs_ref[...], w_theirs_ref[...], preferred_element_type=jnp.float32)
        product = product.astype(jnp.bfloat16)
        for index, out_ref in enumerate(out_refs):
            out_ref[...] = product[index * chunk : (index + 1) * chunk, :]

    @pl.when(jnp.logical_not(work))
    def _():
        for out_ref in out_refs:
            out_ref[...] = jnp.zeros_like(out_ref)


def emit(slot, mine, theirs, w, info, after):
    rows, half = mine.shape
    width = w.shape[1]
    tile = tile_of(width, 1024)
    chunk = rows // halves
    whole = pl.BlockSpec((rows, half), lambda i, held: (0, 0))
    return pl.pallas_call(
        functools.partial(emit_kernel, slot),
        grid_spec=pltpu.PrefetchScalarGridSpec(
            num_scalar_prefetch=1,
            grid=(width // tile,),
            in_specs=[
                whole,
                whole,
                pl.BlockSpec((half, tile), lambda i, held: (held[0], i)),
                pl.BlockSpec((half, tile), lambda i, held: (held[1], i)),
                pl.BlockSpec(memory_space=pl.ANY),
            ],
            out_specs=[pl.BlockSpec((chunk, tile), lambda i, held: (0, i))] * halves,
        ),
        out_shape=[jax.ShapeDtypeStruct((chunk, width), jnp.bfloat16)] * halves,
        compiler_params=params(),
        cost_estimate=pl.CostEstimate(
            flops=4 * rows * half * width, bytes_accessed=4 * half * width, transcendentals=0
        ),
        name="emit",
    )(info, mine, theirs, w, w, after)


def finish_kernel(*refs):
    total = refs[0][...].astype(jnp.float32)
    for ref in refs[1:-1]:
        total = total + ref[...].astype(jnp.float32)
    refs[-1][...] = total.astype(jnp.bfloat16)


def finish(x, index, terms):
    chunk, width = terms[0].shape
    tile = tile_of(width, 1024)
    return pl.pallas_call(
        finish_kernel,
        grid=(width // tile,),
        in_specs=[pl.BlockSpec((chunk, tile), lambda i: (index, i))]
        + [pl.BlockSpec((chunk, tile), lambda i: (0, i))] * len(terms),
        out_specs=pl.BlockSpec((chunk, tile), lambda i: (0, i)),
        out_shape=jax.ShapeDtypeStruct((chunk, width), jnp.bfloat16),
        compiler_params=params(),
        cost_estimate=pl.CostEstimate(
            flops=chunk * width * len(terms), bytes_accessed=2 * chunk * width * (len(terms) + 2), transcendentals=0
        ),
        name="finish",
    )(x, *terms)


def added(*terms):
    total = terms[0].astype(jnp.float32)
    for term in terms[1:]:
        total = total + term.astype(jnp.float32)
    return total.astype(jnp.bfloat16)


def layer(spans, norm_gain, w_in, filters, w_out, prompt_len, needles):
    count = lax.axis_size("ctx")
    place = lax.axis_index("ctx")
    x_local = spans[0]
    rows, half_width = x_local.shape
    full_width = half_width * lax.axis_size("mp")
    weights = jnp.swapaxes(w_in[0], 0, 1)
    up = [(source, source + 1) for source in range(count - 1)]
    down = [(source + 1, source) for source in range(count - 1)]
    partner = [(0, 1), (1, 0)] if lax.axis_size("mp") == 2 else None

    far = count - 1
    order = [("d", 0)] + [(kind, k) for k in range(1, far) for kind in "du"] + [("m", far)]
    z = place.astype(jnp.int32)

    core = lax.axis_index("mp").astype(jnp.int32)
    info = jnp.concatenate([jnp.stack([core, 1 - core, z]), prompt_len])
    waves = wave_tables(rows)
    *pieces, squares = prepare(x_local, norm_gain)
    mine = (jnp.arange(count)[:, None] == z).astype(jnp.float32) * squares[:, 0][None, :]
    total = lax.psum(mine.reshape(-1), ("ctx", "mp"))
    scales = jnp.broadcast_to(lax.rsqrt(total / full_width + norm_eps)[:, None], (count * rows, lanes))
    gathered = {("d", 0): pieces, ("u", 0): pieces}
    for k in range(1, count):
        gathered["u", k] = []
        gathered["d", k] = []
        for i in range(halves):
            value = lax.ppermute(gathered["u", k - 1][i], "ctx", [(a, b) for a, b in up if a >= k - 1])
            gathered["u", k].append(value)
            value = lax.ppermute(gathered["d", k - 1][i], "ctx", [(a, b) for a, b in down if a <= count - k])
            gathered["d", k].append(value)

    held = {}
    gated = {}
    sums = {}

    def combine(kind, k, after):
        before = ("u", k + 1) if kind == "u" or k == 0 else ("d", k - 1)
        mine = mix(
            (kind, k, count), held["d" if kind == "m" else kind, k], held[before],
            rows, waves, filter_waves, scales, info, after,
        )
        gated[kind, k] = (mine, lax.ppermute(mine, "mp", partner))
        return mine

    def spread(kind, k, after):
        sums[kind, k] = emit((kind, k, count), *gated[kind, k], w_out[0], info, after)
        return sums[kind, k][0]

    filter_waves = spectrum(filters[0], waves[0], scales)
    after = filter_waves
    for group in groups_of(count):
        name = group[0]
        layout = []
        inputs = [[] for _ in range(halves)]
        for k in group:
            merged = 2 * k >= count
            for kind in ("d",) if k == 0 else ("ud",) if merged else ("u", "d"):
                for way in kind:
                    held[way, k] = len(layout)
                    for i in range(halves):
                        inputs[i].append(gathered[way, k][i])
                layout.append(len(kind))
        carry = None
        for i in range(halves - 1 if name else 0):
            carry = project(inputs[i : i + 1], layout, weights, i, carry, None, info, after)
            after = carry
        inputs, part = (inputs[-1:], halves - 1) if name else (inputs, 0)
        theirs = project(inputs, layout, weights, part, carry, 1, info, after)
        got = lax.ppermute(theirs, "mp", partner)
        mine = project(inputs, layout, weights, part, carry, 0, info, theirs)
        after = mine
        for k in group:
            for way in "d" if k == 0 else "ud":
                held[way, k] = (mine, got, held[way, k])
        for kind, k in early_slots(count) if name == 1 else ():
            after = combine(kind, k, after)
        for kind, k in early_slots(count) if name == 1 else ():
            after = spread(kind, k, after)
    rest = [slot for slot in [("m", far)] + [(kind, k) for k in range(far - 1, 0, -1) for kind in "ud"] + [("d", 0)]]
    rest = [slot for slot in rest if slot not in sums]
    after = combine(*rest[0], after)
    for index, slot in enumerate(rest):
        if index + 1 < len(rest):
            after = combine(*rest[index + 1], after)
        after = spread(*slot, after)

    def reduce_step(values, pairs):
        moved = []
        for value in values:
            moved.append(lax.ppermute(value, "ctx", pairs))
        return moved

    terms = [sums["d", 0]]
    for k in range(far, 0, -1):
        to_up = [(a, b) for a, b in up if a + k <= far]
        to_down = [(a, b) for a, b in down if a >= k]
        if k == far and far != 2:
            arrived = [reduce_step(sums["m", far], to_up + to_down)] * 2
        else:
            from_up, from_down = ("m", "m") if k == far else ("d", "u")
            arrived = [reduce_step(sums[from_up, k], to_up), reduce_step(sums[from_down, k], to_down)]
        if k > 1:
            for kind, moved in zip("du", arrived):
                sums[kind, k - 1] = [added(a, b) for a, b in zip(sums[kind, k - 1], moved)]
        else:
            terms += arrived if far > 1 else arrived[:1]
    sections = lax.axis_size("section")
    turn = [(source, (source + 1) % sections) for source in range(sections)]
    advanced = []
    for i in range(halves):
        final = finish(x_local, i, [term[i] for term in terms])
        advanced.append(lax.ppermute(final, "section", turn))
    advanced = jnp.concatenate(advanced, axis=0)[None]

    row = jnp.arange(rows, dtype=jnp.int32)
    picked = [0.0, 0.0]
    for slot in order:
        one_hot = (needles[0][:, None] == (row + block_of(slot, z) * rows)[None, :]).astype(jnp.bfloat16)
        for index, part in enumerate(gated[slot]):
            picked[index] += jnp.dot(one_hot, part, preferred_element_type=jnp.float32)
    mine, theirs = [value.astype(jnp.bfloat16) for value in picked]
    lower = jnp.where(core == 0, mine, theirs)
    upper = jnp.where(core == 0, theirs, mine)
    return (advanced, jnp.concatenate([lower, upper], axis=1)[None])


def groups_of(count):
    return [[0], [1]] + [list(range(k, min(k + 2, count))) for k in range(2, count, 2)]


def early_slots(count):
    return [("d", 0), ("d", 1)] if count > 2 else []


def solution(mesh):
    return jax.shard_map(
        layer,
        mesh=mesh,
        in_specs=(
            P("section", ("groups", "ctx"), "mp"),
            P("section", "mp"),
            P("section", "mp", None, "ctx"),
            P("section", "ctx", None),
            P("section", "ctx", "mp"),
            P(("groups", "section")),
            P("section", "groups"),
        ),
        out_specs=(P("section", ("groups", "ctx"), "mp"), P("section", "groups", "ctx")),
        check_vma=False,
    )
```

time: 196 us -> 248 us (1.27)
  the two profiles are of different devices: /device:TPU:12 before, /device:TPU:0 now
where the time goes in v2:
time: 248 us; the launch traced here: 244 us
  Pallas kernels  125 us (50%)
  starting transfers between devices  50.2 us (20%)
  waiting for transfers between devices  23 us (9%)
  blocking collectives  20.6 us (8%)
  local copies, waits for them, and re-layouts  15.1 us (6%)
  matrix products  4.31 us (2%)
  other arithmetic  3.09 us (1%)
    pallas_call x8, Pallas kernels, project(): pl.pallas_call(functools.partial(project_kernel, layout, len(pieces), fir...  57.2 us
    pallas_call x6, Pallas kernels, emit(): pl.pallas_call(functools.partial(emit_kernel, slot), grid_spec=pltpu.Pref...  32.8 us
    ppermute x10, starting transfers between devices, reduce_step(): moved.append(lax.ppermute(value, 'ctx', pairs))  25.3 us
    pallas_call x6, Pallas kernels, mix(): pl.pallas_call(functools.partial(mix_kernel, slot), grid_spec=pltpu.Prefe...  23.3 us
    psum x1, blocking collectives, layer(): total = lax.psum(mine.reshape(-1), ('ctx', 'mp'))  20.6 us
    unnamed x92, local copies, waits for them, and re-layouts  13.3 us
    ppermute x6, starting transfers between devices, layer(): lax.ppermute(gathered['u', k - 1][i], 'ctx', [(a, b) for a, b in up if a...  12.3 us
    ppermute x10, waiting for transfers between devices, reduce_step(): moved.append(lax.ppermute(value, 'ctx', pairs))  9.7 us
  transfers between devices with their start and end apart: 33, of which 7 were waited for; matrix products, arithmetic and copies ran while one was open for 3% of the time, Pallas kernels for 44%

profile of v2, /device:TPU:0, one launch (start us, length us, event | category | flops | bytes accessed | tf_op | source)
XLA Modules:
  0.0 243.7 jit_solution(9762105916850190142)
XLA Ops:
  0.6 2.1 prepare.1
  2.8 5.0 %collective-permute-start.1 = (bf16[128,1536]{1,0:T(8,128)(2,1)}, bf16[128,1536]{1,0:T(8,128)(2,1)S(1)}, u32[]{:S(2)}, u32[]{:S(2)}) collective-permute-start(bf16[128,1536]{1,0:T(8,128)(2,1)} %get-tuple-element.18.refs_2_), channel_id=1, source_target_pairs={{0,4},{4,8},{8,12},{1,5},{5,9},{9,13},{2,6},{6,10},{10,14},{3,7},{... | collective-permute-start | bytes 1179656 | tf_op jit(solution)/shard_map/ppermute | solution.py:368
  7.7 1.3 collective-permute-start.2
  9.0 4.6 %collective-permute-start.3 = (bf16[128,1536]{1,0:T(8,128)(2,1)}, bf16[128,1536]{1,0:T(8,128)(2,1)S(1)}, u32[]{:S(2)}, u32[]{:S(2)}) collective-permute-start(bf16[128,1536]{1,0:T(8,128)(2,1)} %get-tuple-element.17.refs_1_), channel_id=1, source_target_pairs={{0,4},{4,8},{8,12},{1,5},{5,9},{9,13},{2,6},{6,10},{10,14},{3,7},{... | collective-permute-start | bytes 1179656 | tf_op jit(solution)/shard_map/ppermute | solution.py:368
  13.6 1.3 collective-permute-start.4
  16.0 20.6 %psum.7 = f32[512]{0:T(512)S(1)} all-reduce(f32[512]{0:T(512)S(1)} %multiply_bitcast_fusion), channel_id=1, replica_groups=mesh['groups'=2,'ctx'=4,'section'=2,'mp'=2] {'ctx','mp'}, use_global_device_ids=true, to_apply=%region_0.0 | all-reduce | flops 512 | bytes 4096 | tf_op jit(solution)/shard_map/psum | solution.py:361
  38.0 3.7 %spectrum.1.refs_4_.refs_12_ = f32[256,1024]{1,0:T(8,128)} custom-call(bf16[1024,128]{1,0:T(8,128)(2,1)} %bitcast.51, bf16[512,256]{1,0:T(8,128)(2,1)} %constant.49.forward_ref.refs_13_, f32[512,128]{1,0:T(8,128)} %broadcast_in_dim.6._.refs_10_.refs_11_), custom_call_target="tpu_custom_call" | custom-call | tf_op jit(solution)/shard_map/spectrum/pallas_call | solution.py:152
  42.4 6.8 %project.8.refs_4_ = bf16[128,1536]{1,0:T(8,128)(2,1)} custom-call(s32[4]{0:T(128)} %pad_add_fusion.refs_0_.info_ref, bf16[128,1536]{1,0:T(8,128)(2,1)} %get-tuple-element.17.refs_1_, bf16[128,1536]{1,0:T(8,128)(2,1)} %get-tuple-element.18.refs_2_, bf16[3,3072,1024]{2,1,0:T(8,128)(2,1)} %bitcast.28, f32[256,1024]{1,0:T(8,128)} %spectrum.1.refs_4_.refs_12_), custom_call_target="tpu_custom_call" | custom-call | flops 1207959552 | bytes 9437184 | tf_op jit(solution)/shard_map/project/pallas_call | solution.py:97
  49.3 6.8 %project.9.refs_4_.refs_0_.refs_1_.refs_2_.refs_6_.refs_7_ = bf16[128,1536]{1,0:T(8,128)(2,1)} custom-call(s32[4]{0:T(128)} %pad_add_fusion.refs_0_.info_ref, bf16[128,1536]{1,0:T(8,128)(2,1)} %get-tuple-element.17.refs_1_, bf16[128,1536]{1,0:T(8,128)(2,1)} %get-tuple-element.18.refs_2_, bf16[3,3072,1024]{2,1,0:T(8,128)(2,1)} %bitcast.29, ...), custom_call_target="tpu_custom_call" | custom-call | flops 1207959552 | bytes 9437184 | tf_op jit(solution)/shard_map/project/pallas_call | solution.py:97
  57.5 9.0 %project.10.refs_3_.refs_5_ = f32[256,3072]{1,0:T(8,128)} custom-call(s32[4]{0:T(128)} %pad_add_fusion.refs_0_.info_ref, bf16[128,1536]{1,0:T(8,128)(2,1)} %copy-done.40, bf16[128,1536]{1,0:T(8,128)(2,1)} %copy-done.38, bf16[3,3072,1024]{2,1,0:T(8,128)(2,1)} %bitcast.30, bf16[128,1536]{1,0:T(8,128)(2,1)} %project.9.refs_4_.refs_0_.refs_1_.refs_2_.refs_6_.refs_7_), custom_call_target="tpu_custom_call" | custom-call | flops 2415919104 | bytes 9437184 | tf_op jit(solution)/shard_map/project/pallas_call | solution.py:97
  68.0 6.1 %project.11.refs_5_ = bf16[256,1536]{1,0:T(8,128)(2,1)} custom-call(s32[4]{0:T(128)} %pad_add_fusion.refs_0_.info_ref, bf16[128,1536]{1,0:T(8,128)(2,1)} %copy-done.10, bf16[128,1536]{1,0:T(8,128)(2,1)} %copy-done.9, f32[256,3072]{1,0:T(8,128)} %project.10.refs_3_.refs_5_, bf16[3,3072,1024]{2,1,0:T(8,128)(2,1)} %bitcast.31, f32[256,3072]{1,0:T(8,128)} %project.10.refs_3_.refs_5_), custom_call_target="tpu_custom_call" | custom-call | flops 1207959552 | bytes 4718592 | tf_op jit(solution)/shard_map/project/pallas_call | solution.py:97
  75.4 1.3 collective-permute-start.13
  77.4 1.3 collective-permute-start.9
  78.7 6.2 %project.12.refs_6_.refs_7_.refs_15_.refs_0_.refs_1_.refs_2_ = bf16[256,1536]{1,0:T(8,128)(2,1)} custom-call(s32[4]{0:T(128)} %pad_add_fusion.refs_0_.info_ref, bf16[128,1536]{1,0:T(8,128)(2,1)} %copy-done.10, bf16[128,1536]{1,0:T(8,128)(2,1)} %copy-done.9, f32[256,3072]{1,0:T(8,128)} %project.10.refs_3_.refs_5_, bf16[3,3072,1024]{2,1,0:T(8,128)(2,1)} %bitcast.32, ...), custom_call_target="tpu_custom_call" | custom-call | flops 1207959552 | bytes 4718592 | tf_op jit(solution)/shard_map/project/pallas_call | solution.py:97
  85.6 4.3 %collective-permute-done.13.refs_2_ = bf16[128,1536]{1,0:T(8,128)(2,1)} collective-permute-done((bf16[128,1536]{1,0:T(8,128)(2,1)S(1)}, bf16[128,1536]{1,0:T(8,128)(2,1)}, u32[]{:S(2)}, u32[]{:S(2)}) %collective-permute-start.13) | collective-permute-done | bytes 393248 | tf_op jit(solution)/shard_map/ppermute | solution.py:370
  89.9 1.3 collective-permute-start.15
  92.1 4.2 %mix.6.refs_15_.mine_ref = bf16[128,512]{1,0:T(8,128)(2,1)} custom-call(s32[4]{0:T(128)} %pad_add_fusion.refs_0_.info_ref, bf16[128,1536]{1,0:T(8,128)(2,1)} %project.9.refs_4_.refs_0_.refs_1_.refs_2_.refs_6_.refs_7_, bf16[128,1536]{1,0:T(8,128)(2,1)} %project.9.refs_4_.refs_0_.refs_1_.refs_2_.refs_6_.refs_7_, ...), custom_call_target="tpu_custom_call" | custom-call | flops 134217728 | bytes 2097152 | tf_op jit(solution)/shard_map/mix/pallas_call | solution.py:236
  99.5 4.3 %mix.7._.mine_ref = bf16[128,512]{1,0:T(8,128)(2,1)} custom-call(s32[4]{0:T(128)} %pad_add_fusion.refs_0_.info_ref, bf16[256,1536]{1,0:T(8,128)(2,1)} %project.12.refs_6_.refs_7_.refs_15_.refs_0_.refs_1_.refs_2_, bf16[256,1536]{1,0:T(8,128)(2,1)} %project.12.refs_6_.refs_7_.refs_15_.refs_0_.refs_1_.refs_2_, ...), custom_call_target="tpu_custom_call" | custom-call | flops 134217728 | bytes 2097152 | tf_op jit(solution)/shard_map/mix/pallas_call | solution.py:236
  104.5 5.7 %emit.6 = (bf16[64,3072]{1,0:T(8,128)(2,1)}, bf16[64,3072]{1,0:T(8,128)(2,1)}) custom-call(s32[4]{0:T(128)} %pad_add_fusion.refs_0_.info_ref, bf16[128,512]{1,0:T(8,128)(2,1)} %mix.6.refs_15_.mine_ref, bf16[128,512]{1,0:T(8,128)(2,1)} %copy-done.27, bf16[1024,3072]{1,0:T(8,128)(2,1)} %bitcast.36, bf16[1024,3072]{1,0:T(8,128)(2,1)} %bitcast.37, ...), custom_call_target="tpu_custom_call" | custom-call | flops 805306368 | bytes 6291456 | tf_op jit(solution)/shard_map/emit/pallas_call | solution.py:286
  110.9 5.7 %emit.7 = (bf16[64,3072]{1,0:T(8,128)(2,1)}, bf16[64,3072]{1,0:T(8,128)(2,1)}) custom-call(s32[4]{0:T(128)} %pad_add_fusion.refs_0_.info_ref, bf16[128,512]{1,0:T(8,128)(2,1)} %mix.7._.mine_ref, bf16[128,512]{1,0:T(8,128)(2,1)} %copy-done.21, bf16[1024,3072]{1,0:T(8,128)(2,1)} %bitcast.38, bf16[1024,3072]{1,0:T(8,128)(2,1)} %bitcast.39, ...), custom_call_target="tpu_custom_call" | custom-call | flops 805306368 | bytes 6291456 | tf_op jit(solution)/shard_map/emit/pallas_call | solution.py:286
  117.5 9.3 %project.13.refs_5_.refs_7_ = f32[256,3072]{1,0:T(8,128)} custom-call(s32[4]{0:T(128)} %pad_add_fusion.refs_0_.info_ref, bf16[128,1536]{1,0:T(8,128)(2,1)} %copy-done.42, bf16[128,1536]{1,0:T(8,128)(2,1)} %collective-permute-done.13.refs_2_, bf16[128,1536]{1,0:T(8,128)(2,1)} %copy-done.43, bf16[128,1536]{1,0:T(8,128)(2,1)} %copy-done.44, ...), custom_call_target="tpu_custom_call" | custom-call | flops 2415919104 | bytes 9437184 | tf_op jit(solution)/shard_map/project/pallas_call | solution.py:97
  128.3 6.4 %project.14.refs_7_ = bf16[256,1536]{1,0:T(8,128)(2,1)} custom-call(s32[4]{0:T(128)} %pad_add_fusion.refs_0_.info_ref, bf16[128,1536]{1,0:T(8,128)(2,1)} %copy-done.11, bf16[128,1536]{1,0:T(8,128)(2,1)} %copy-done.12, bf16[128,1536]{1,0:T(8,128)(2,1)} %copy-done.13, bf16[128,1536]{1,0:T(8,128)(2,1)} %copy-done.14, f32[256,3072]{1,0:T(8,128)} %project.13.refs_5_.refs_7_, ...), custom_call_target="tpu_custom_call" | custom-call | flops 1207959552 | bytes 4718592 | tf_op jit(solution)/shard_map/project/pallas_call | solution.py:97
  134.9 6.5 %project.15.refs_0_.refs_1_.refs_2_.refs_6_.refs_7_.refs_15_ = bf16[256,1536]{1,0:T(8,128)(2,1)} custom-call(s32[4]{0:T(128)} %pad_add_fusion.refs_0_.info_ref, bf16[128,1536]{1,0:T(8,128)(2,1)} %copy-done.11, bf16[128,1536]{1,0:T(8,128)(2,1)} %copy-done.12, bf16[128,1536]{1,0:T(8,128)(2,1)} %copy-done.13, bf16[128,1536]{1,0:T(8,128)(2,1)} %copy-done.14, ...), custom_call_target="tpu_custom_call" | custom-call | flops 1207959552 | bytes 4718592 | tf_op jit(solution)/shard_map/project/pallas_call | solution.py:97
  142.6 4.3 %mix.8.refs_15_.mine_ref = bf16[128,512]{1,0:T(8,128)(2,1)} custom-call(s32[4]{0:T(128)} %pad_add_fusion.refs_0_.info_ref, bf16[256,1536]{1,0:T(8,128)(2,1)} %project.15.refs_0_.refs_1_.refs_2_.refs_6_.refs_7_.refs_15_, bf16[256,1536]{1,0:T(8,128)(2,1)} %project.15.refs_0_.refs_1_.refs_2_.refs_6_.refs_7_.refs_15_, ...), custom_call_target="tpu_custom_call" | custom-call | flops 134217728 | bytes 2097152 | tf_op jit(solution)/shard_map/mix/pallas_call | solution.py:236
  147.4 3.1 %mix.9._.mine_ref = bf16[128,512]{1,0:T(8,128)(2,1)} custom-call(s32[4]{0:T(128)} %pad_add_fusion.refs_0_.info_ref, bf16[256,1536]{1,0:T(8,128)(2,1)} %project.15.refs_0_.refs_1_.refs_2_.refs_6_.refs_7_.refs_15_, bf16[256,1536]{1,0:T(8,128)(2,1)} %project.15.refs_0_.refs_1_.refs_2_.refs_6_.refs_7_.refs_15_, ...), custom_call_target="tpu_custom_call" | custom-call | flops 134217728 | bytes 2097152 | tf_op jit(solution)/shard_map/mix/pallas_call | solution.py:236
  152.6 5.7 %emit.8 = (bf16[64,3072]{1,0:T(8,128)(2,1)}, bf16[64,3072]{1,0:T(8,128)(2,1)}) custom-call(s32[4]{0:T(128)} %pad_add_fusion.refs_0_.info_ref, bf16[128,512]{1,0:T(8,128)(2,1)} %mix.8.refs_15_.mine_ref, bf16[128,512]{1,0:T(8,128)(2,1)} %copy-done.23, bf16[1024,3072]{1,0:T(8,128)(2,1)} %bitcast.40, bf16[1024,3072]{1,0:T(8,128)(2,1)} %bitcast.41, ...), custom_call_target="tpu_custom_call" | custom-call | flops 805306368 | bytes 6291456 | tf_op jit(solution)/shard_map/emit/pallas_call | solution.py:286
  158.3 3.0 %collective-permute-start.27 = (bf16[64,3072]{1,0:T(8,128)(2,1)}, bf16[64,3072]{1,0:T(8,128)(2,1)S(1)}, u32[]{:S(2)}, u32[]{:S(2)}) collective-permute-start(bf16[64,3072]{1,0:T(8,128)(2,1)} %get-tuple-element.29), channel_id=1, source_target_pairs={{0,4},{12,8},{1,5},{13,9},{2,6},{14,10},{3,7},{15,11},{16,20},{28,... | collective-permute-start | bytes 1179656 | tf_op jit(solution)/shard_map/ppermute | solution.py:431
  161.2 1.5 collective-permute-start.20
  162.7 4.3 %mix.10._.mine_ref = bf16[128,512]{1,0:T(8,128)(2,1)} custom-call(s32[4]{0:T(128)} %pad_add_fusion.refs_0_.info_ref, bf16[256,1536]{1,0:T(8,128)(2,1)} %project.15.refs_0_.refs_1_.refs_2_.refs_6_.refs_7_.refs_15_, bf16[256,1536]{1,0:T(8,128)(2,1)} %project.15.refs_0_.refs_1_.refs_2_.refs_6_.refs_7_.refs_15_, ...), custom_call_target="tpu_custom_call" | custom-call | flops 134217728 | bytes 2097152 | tf_op jit(solution)/shard_map/mix/pallas_call | solution.py:236
  167.8 4.9 %emit.9 = (bf16[64,3072]{1,0:T(8,128)(2,1)}, bf16[64,3072]{1,0:T(8,128)(2,1)}) custom-call(s32[4]{0:T(128)} %pad_add_fusion.refs_0_.info_ref, bf16[128,512]{1,0:T(8,128)(2,1)} %mix.9._.mine_ref, bf16[128,512]{1,0:T(8,128)(2,1)} %copy-done.25, bf16[1024,3072]{1,0:T(8,128)(2,1)} %bitcast.42, bf16[1024,3072]{1,0:T(8,128)(2,1)} %bitcast.43, ...), custom_call_target="tpu_custom_call" | custom-call | flops 805306368 | bytes 6291456 | tf_op jit(solution)/shard_map/emit/pallas_call | solution.py:286
  172.7 3.2 %mix.11._.mine_ref = bf16[128,512]{1,0:T(8,128)(2,1)} custom-call(s32[4]{0:T(128)} %pad_add_fusion.refs_0_.info_ref, bf16[256,1536]{1,0:T(8,128)(2,1)} %project.12.refs_6_.refs_7_.refs_15_.refs_0_.refs_1_.refs_2_, bf16[256,1536]{1,0:T(8,128)(2,1)} %project.12.refs_6_.refs_7_.refs_15_.refs_0_.refs_1_.refs_2_, ...), custom_call_target="tpu_custom_call" | custom-call | flops 134217728 | bytes 2097152 | tf_op jit(solution)/shard_map/mix/pallas_call | solution.py:236
  178.9 5.7 %emit.10 = (bf16[64,3072]{1,0:T(8,128)(2,1)}, bf16[64,3072]{1,0:T(8,128)(2,1)}) custom-call(s32[4]{0:T(128)} %pad_add_fusion.refs_0_.info_ref, bf16[128,512]{1,0:T(8,128)(2,1)} %mix.10._.mine_ref, bf16[128,512]{1,0:T(8,128)(2,1)} %copy-done.17, bf16[1024,3072]{1,0:T(8,128)(2,1)} %bitcast.44, bf16[1024,3072]{1,0:T(8,128)(2,1)} %bitcast.45, ...), custom_call_target="tpu_custom_call" | custom-call | flops 805306368 | bytes 6291456 | tf_op jit(solution)/shard_map/emit/pallas_call | solution.py:286
  185.2 5.1 %emit.11 = (bf16[64,3072]{1,0:T(8,128)(2,1)}, bf16[64,3072]{1,0:T(8,128)(2,1)}) custom-call(s32[4]{0:T(128)} %pad_add_fusion.refs_0_.info_ref, bf16[128,512]{1,0:T(8,128)(2,1)} %mix.11._.mine_ref, bf16[128,512]{1,0:T(8,128)(2,1)} %copy-done.19, bf16[1024,3072]{1,0:T(8,128)(2,1)} %bitcast.46, bf16[1024,3072]{1,0:T(8,128)(2,1)} %bitcast.47, ...), custom_call_target="tpu_custom_call" | custom-call | flops 805306368 | bytes 6291456 | tf_op jit(solution)/shard_map/emit/pallas_call | solution.py:286
  190.5 3.3 %collective-permute-start.28 = (bf16[64,3072]{1,0:T(8,128)(2,1)S(1)}, bf16[64,3072]{1,0:T(8,128)(2,1)S(1)}, u32[]{:S(2)}, u32[]{:S(2)}) collective-permute-start(bf16[64,3072]{1,0:T(8,128)(2,1)S(1)} %get-tuple-element.35), channel_id=1, source_target_pairs={{0,4},{4,8},{1,5},{5,9},{2,6},{6,10},{3,7},{7,11},{16,20},{20,24},... | collective-permute-start | bytes 1179656 | tf_op jit(solution)/shard_map/ppermute | solution.py:431
  194.9 4.5 %collective-permute-start.21 = (bf16[64,3072]{1,0:T(8,128)(2,1)S(1)}, bf16[64,3072]{1,0:T(8,128)(2,1)S(1)}, u32[]{:S(2)}, u32[]{:S(2)}) collective-permute-start(bf16[64,3072]{1,0:T(8,128)(2,1)S(1)} %get-tuple-element.33), channel_id=1, source_target_pairs={{0,4},{4,8},{1,5},{5,9},{2,6},{6,10},{3,7},{7,11},{16,20},{20,24},... | collective-permute-start | bytes 1179656 | tf_op jit(solution)/shard_map/ppermute | solution.py:431
  200.1 3.2 %collective-permute-done.28 = bf16[64,3072]{1,0:T(8,128)(2,1)S(1)} collective-permute-done((bf16[64,3072]{1,0:T(8,128)(2,1)S(1)}, bf16[64,3072]{1,0:T(8,128)(2,1)S(1)}, u32[]{:S(2)}, u32[]{:S(2)}) %collective-permute-start.28) | collective-permute-done | bytes 393248 | tf_op jit(solution)/shard_map/ppermute | solution.py:431
  203.4 4.4 %collective-permute-start.29 = (bf16[64,3072]{1,0:T(8,128)(2,1)S(1)}, bf16[64,3072]{1,0:T(8,128)(2,1)S(1)}, u32[]{:S(2)}, u32[]{:S(2)}) collective-permute-start(bf16[64,3072]{1,0:T(8,128)(2,1)S(1)} %add_convert_fusion.1), channel_id=1, source_target_pairs={{0,4},{4,8},{8,12},{1,5},{5,9},{9,13},{2,6},{6,10},{10,14},{3,7},{... | collective-permute-start | bytes 1179656 | tf_op jit(solution)/shard_map/ppermute | solution.py:431
  207.9 1.3 collective-permute-start.31
  209.2 2.5 %collective-permute-done.21 = bf16[64,3072]{1,0:T(8,128)(2,1)S(1)} collective-permute-done((bf16[64,3072]{1,0:T(8,128)(2,1)S(1)}, bf16[64,3072]{1,0:T(8,128)(2,1)S(1)}, u32[]{:S(2)}, u32[]{:S(2)}) %collective-permute-start.21) | collective-permute-done | bytes 393248 | tf_op jit(solution)/shard_map/ppermute | solution.py:431
  211.8 4.4 %collective-permute-start.22 = (bf16[64,3072]{1,0:T(8,128)(2,1)S(1)}, bf16[64,3072]{1,0:T(8,128)(2,1)S(1)}, u32[]{:S(2)}, u32[]{:S(2)}) collective-permute-start(bf16[64,3072]{1,0:T(8,128)(2,1)S(1)} %add_convert_fusion.3), channel_id=1, source_target_pairs={{0,4},{4,8},{8,12},{1,5},{5,9},{9,13},{2,6},{6,10},{10,14},{3,7},{... | collective-permute-start | bytes 1179656 | tf_op jit(solution)/shard_map/ppermute | solution.py:431
  216.4 1.4 collective-permute-start.25
  218.2 1.9 collective-permute-done.29.refs_2_
  221.0 3.1 %finish.3 = bf16[64,3072]{1,0:T(8,128)(2,1)} custom-call(bf16[128,3072]{1,0:T(8,128)(2,1)} %bitcast.49, bf16[64,3072]{1,0:T(8,128)(2,1)} %get-tuple-element.26.refs_1_, bf16[64,3072]{1,0:T(8,128)(2,1)} %copy-done.29, bf16[64,3072]{1,0:T(8,128)(2,1)} %copy-done.31), custom_call_target="tpu_custom_call" | custom-call | flops 589824 | bytes 1966080 | tf_op jit(solution)/shard_map/finish/pallas_call | solution.py:319
  224.1 1.5 collective-permute-start.32
  225.6 2.1 collective-permute-done.22.refs_2_
  229.2 3.1 %finish.2 = bf16[64,3072]{1,0:T(8,128)(2,1)} custom-call(bf16[128,3072]{1,0:T(8,128)(2,1)} %bitcast.50, bf16[64,3072]{1,0:T(8,128)(2,1)} %get-tuple-element.20._.refs_1_, bf16[64,3072]{1,0:T(8,128)(2,1)} %copy-done.30, bf16[64,3072]{1,0:T(8,128)(2,1)} %copy-done.32), custom_call_target="tpu_custom_call" | custom-call | flops 589824 | bytes 1966080 | tf_op jit(solution)/shard_map/finish/pallas_call | solution.py:319
  232.3 1.5 collective-permute-start.26
  234.9 7.8 %collective-permute-done.26 = bf16[64,3072]{1,0:T(8,128)(2,1)S(1)} collective-permute-done((bf16[64,3072]{1,0:T(8,128)(2,1)}, bf16[64,3072]{1,0:T(8,128)(2,1)S(1)}, u32[]{:S(2)}, u32[]{:S(2)}) %collective-permute-start.26) | collective-permute-done | bytes 393248 | tf_op jit(solution)/shard_map/ppermute | solution.py:453
  (167 shorter events, 31.1 us)
Async XLA Ops:
  2.8 63.8 %collective-permute-start.1 = (bf16[128,1536]{1,0:T(8,128)(2,1)}, bf16[128,1536]{1,0:T(8,128)(2,1)S(1)}, u32[]{:S(2)}, u32[]{:S(2)}) collective-permute-start(bf16[128,1536]{1,0:T(8,128)(2,1)} %get-tuple-element.18.refs_2_), channel_id=1, source_target_pairs={{0,4},{4,8},{8,12},{1,5},{5,9},{9,13},{2,6},{6,10},{10,14},{3,7},{... | collective-permute-start | bytes 1179656 | tf_op jit(solution)/shard_map/ppermute | solution.py:368
  7.7 58.8 %collective-permute-start.2 = (bf16[128,1536]{1,0:T(8,128)(2,1)}, bf16[128,1536]{1,0:T(8,128)(2,1)S(1)}, u32[]{:S(2)}, u32[]{:S(2)}) collective-permute-start(bf16[128,1536]{1,0:T(8,128)(2,1)} %get-tuple-element.18.refs_2_), channel_id=1, source_target_pairs={{4,0},{8,4},{12,8},{5,1},{9,5},{13,9},{6,2},{10,6},{14,10},{7,3},{... | collective-permute-start | bytes 1179656 | tf_op jit(solution)/shard_map/ppermute | solution.py:370
  9.0 47.0 %collective-permute-start.3 = (bf16[128,1536]{1,0:T(8,128)(2,1)}, bf16[128,1536]{1,0:T(8,128)(2,1)S(1)}, u32[]{:S(2)}, u32[]{:S(2)}) collective-permute-start(bf16[128,1536]{1,0:T(8,128)(2,1)} %get-tuple-element.17.refs_1_), channel_id=1, source_target_pairs={{0,4},{4,8},{8,12},{1,5},{5,9},{9,13},{2,6},{6,10},{10,14},{3,7},{... | collective-permute-start | bytes 1179656 | tf_op jit(solution)/shard_map/ppermute | solution.py:368
  13.6 42.4 %collective-permute-start.4 = (bf16[128,1536]{1,0:T(8,128)(2,1)}, bf16[128,1536]{1,0:T(8,128)(2,1)S(1)}, u32[]{:S(2)}, u32[]{:S(2)}) collective-permute-start(bf16[128,1536]{1,0:T(8,128)(2,1)} %get-tuple-element.17.refs_1_), channel_id=1, source_target_pairs={{4,0},{8,4},{12,8},{5,1},{9,5},{13,9},{6,2},{10,6},{14,10},{7,3},{... | collective-permute-start | bytes 1179656 | tf_op jit(solution)/shard_map/ppermute | solution.py:370
  66.5 8.0 %copy-start.15 = (bf16[128,1536]{1,0:T(8,128)(2,1)S(1)}, bf16[128,1536]{1,0:T(8,128)(2,1)}, u32[]{:S(2)}) copy-start(bf16[128,1536]{1,0:T(8,128)(2,1)} %project.8.refs_4_) | copy-start | bytes 1179652
  66.5 8.2 %copy-start.41 = (bf16[128,1536]{1,0:T(8,128)(2,1)S(1)}, bf16[128,1536]{1,0:T(8,128)(2,1)}, u32[]{:S(2)}) copy-start(bf16[128,1536]{1,0:T(8,128)(2,1)} %copy-done.40) | copy-start | bytes 1179652
  66.5 8.8 %copy-start.39 = (bf16[128,1536]{1,0:T(8,128)(2,1)S(1)}, bf16[128,1536]{1,0:T(8,128)(2,1)}, u32[]{:S(2)}) copy-start(bf16[128,1536]{1,0:T(8,128)(2,1)} %copy-done.38) | copy-start | bytes 1179652
  74.2 17.1 %collective-permute-start.5 = (bf16[256,1536]{1,0:T(8,128)(2,1)}, bf16[256,1536]{1,0:T(8,128)(2,1)S(1)}, u32[]{:S(2)}, u32[]{:S(2)}) collective-permute-start(bf16[256,1536]{1,0:T(8,128)(2,1)} %project.11.refs_5_), channel_id=1, source_target_pairs={{0,1},{1,0},{2,3},{3,2},{4,5},{5,4},{6,7},{7,6},{8,9},{9,8},{10,11... | collective-permute-start | bytes 2359304 | tf_op jit(solution)/shard_map/ppermute | solution.py:410
  74.5 2.9 %collective-permute-start = (bf16[128,1536]{1,0:T(8,128)(2,1)S(1)}, bf16[128,1536]{1,0:T(8,128)(2,1)S(1)}, u32[]{:S(2)}, u32[]{:S(2)}) collective-permute-start(bf16[128,1536]{1,0:T(8,128)(2,1)S(1)} %copy-done.15), channel_id=1, source_target_pairs={{0,1},{1,0},{2,3},{3,2},{4,5},{5,4},{6,7},{7,6},{8,9},{9,8},{10,11... | collective-permute-start | bytes 1179656 | tf_op jit(solution)/shard_map/ppermute | solution.py:410
  74.7 10.3 %collective-permute-start.12 = (bf16[128,1536]{1,0:T(8,128)(2,1)S(1)}, bf16[128,1536]{1,0:T(8,128)(2,1)S(1)}, u32[]{:S(2)}, u32[]{:S(2)}) collective-permute-start(bf16[128,1536]{1,0:T(8,128)(2,1)S(1)} %copy-done.41), channel_id=1, source_target_pairs={{4,8},{8,12},{5,9},{9,13},{6,10},{10,14},{7,11},{11,15},{20,24},{2... | collective-permute-start | bytes 1179656 | tf_op jit(solution)/shard_map/ppermute | solution.py:368
  75.4 14.6 %collective-permute-start.13 = (bf16[128,1536]{1,0:T(8,128)(2,1)S(1)}, bf16[128,1536]{1,0:T(8,128)(2,1)}, u32[]{:S(2)}, u32[]{:S(2)}) collective-permute-start(bf16[128,1536]{1,0:T(8,128)(2,1)S(1)} %copy-done.39), channel_id=1, source_target_pairs={{4,0},{8,4},{5,1},{9,5},{6,2},{10,6},{7,3},{11,7},{20,16},{24,20},... | collective-permute-start | bytes 1179656 | tf_op jit(solution)/shard_map/ppermute | solution.py:370
  76.7 19.8 %collective-permute-start.8 = (bf16[128,1536]{1,0:T(8,128)(2,1)}, bf16[128,1536]{1,0:T(8,128)(2,1)S(1)}, u32[]{:S(2)}, u32[]{:S(2)}) collective-permute-start(bf16[128,1536]{1,0:T(8,128)(2,1)} %copy-done.10), channel_id=1, source_target_pairs={{4,8},{8,12},{5,9},{9,13},{6,10},{10,14},{7,11},{11,15},{20,24},{2... | collective-permute-start | bytes 1179656 | tf_op jit(solution)/shard_map/ppermute | solution.py:368
  77.4 20.9 %collective-permute-start.9 = (bf16[128,1536]{1,0:T(8,128)(2,1)}, bf16[128,1536]{1,0:T(8,128)(2,1)S(1)}, u32[]{:S(2)}, u32[]{:S(2)}) collective-permute-start(bf16[128,1536]{1,0:T(8,128)(2,1)} %copy-done.9), channel_id=1, source_target_pairs={{4,0},{8,4},{5,1},{9,5},{6,2},{10,6},{7,3},{11,7},{20,16},{24,20},... | collective-permute-start | bytes 1179656 | tf_op jit(solution)/shard_map/ppermute | solution.py:370
  84.9 25.3 %copy-start.42 = (bf16[128,1536]{1,0:T(8,128)(2,1)}, bf16[128,1536]{1,0:T(8,128)(2,1)S(1)}, u32[]{:S(2)}) copy-start(bf16[128,1536]{1,0:T(8,128)(2,1)S(1)} %collective-permute-done.12.refs_1_) | copy-start | bytes 1179652
  84.9 31.6 %collective-permute-start.14 = (bf16[128,1536]{1,0:T(8,128)(2,1)S(1)}, bf16[128,1536]{1,0:T(8,128)(2,1)S(1)}, u32[]{:S(2)}, u32[]{:S(2)}) collective-permute-start(bf16[128,1536]{1,0:T(8,128)(2,1)S(1)} %collective-permute-done.12.refs_1_), channel_id=1, source_target_pairs={{8,12},{9,13},{10,14},{11,15},{24,28},{25,29},{26,30},{27,31}} | collective-permute-start | bytes 1179656 | tf_op jit(solution)/shard_map/ppermute | solution.py:368
  89.9 26.7 %collective-permute-start.15 = (bf16[128,1536]{1,0:T(8,128)(2,1)}, bf16[128,1536]{1,0:T(8,128)(2,1)S(1)}, u32[]{:S(2)}, u32[]{:S(2)}) collective-permute-start(bf16[128,1536]{1,0:T(8,128)(2,1)} %collective-permute-done.13.refs_2_), channel_id=1, source_target_pairs={{4,0},{5,1},{6,2},{7,3},{20,16},{21,17},{22,18},{23,19}} | collective-permute-start | bytes 1179656 | tf_op jit(solution)/shard_map/ppermute | solution.py:370
  96.3 7.5 %collective-permute-start.6 = (bf16[128,512]{1,0:T(8,128)(2,1)}, bf16[128,512]{1,0:T(8,128)(2,1)S(1)}, u32[]{:S(2)}, u32[]{:S(2)}) collective-permute-start(bf16[128,512]{1,0:T(8,128)(2,1)} %mix.6.refs_15_.mine_ref), channel_id=1, source_target_pairs={{0,1},{1,0},{2,3},{3,2},{4,5},{5,4},{6,7},{7,6},{8,9},{9,8},{10,11... | collective-permute-start | bytes 393224 | tf_op jit(solution)/shard_map/ppermute | solution.py:383
  96.5 30.3 %collective-permute-start.10 = (bf16[128,1536]{1,0:T(8,128)(2,1)S(1)}, bf16[128,1536]{1,0:T(8,128)(2,1)S(1)}, u32[]{:S(2)}, u32[]{:S(2)}) collective-permute-start(bf16[128,1536]{1,0:T(8,128)(2,1)S(1)} %collective-permute-done.8.refs_1_), channel_id=1, source_target_pairs={{8,12},{9,13},{10,14},{11,15},{24,28},{25,29},{26,30},{27,31}} | collective-permute-start | bytes 1179656 | tf_op jit(solution)/shard_map/ppermute | solution.py:368
  98.3 28.5 %collective-permute-start.11 = (bf16[128,1536]{1,0:T(8,128)(2,1)S(1)}, bf16[128,1536]{1,0:T(8,128)(2,1)S(1)}, u32[]{:S(2)}, u32[]{:S(2)}) collective-permute-start(bf16[128,1536]{1,0:T(8,128)(2,1)S(1)} %collective-permute-done.9.refs_2_), channel_id=1, source_target_pairs={{4,0},{5,1},{6,2},{7,3},{20,16},{21,17},{22,18},{23,19}} | collective-permute-start | bytes 1179656 | tf_op jit(solution)/shard_map/ppermute | solution.py:370
  103.9 6.3 %collective-permute-start.7 = (bf16[128,512]{1,0:T(8,128)(2,1)}, bf16[128,512]{1,0:T(8,128)(2,1)S(1)}, u32[]{:S(2)}, u32[]{:S(2)}) collective-permute-start(bf16[128,512]{1,0:T(8,128)(2,1)} %mix.7._.mine_ref), channel_id=1, source_target_pairs={{0,1},{1,0},{2,3},{3,2},{4,5},{5,4},{6,7},{7,6},{8,9},{9,8},{10,11... | collective-permute-start | bytes 393224 | tf_op jit(solution)/shard_map/ppermute | solution.py:383
  126.7 8.0 %copy-start.45 = (s32[1,64]{1,0:T(1,128)S(1)}, s32[1,64]{1,0:T(1,128)}, u32[]{:S(2)}) copy-start(s32[1,64]{1,0:T(1,128)} %param.17) | copy-start | bytes 772
  134.7 7.0 %collective-permute-start.16 = (bf16[256,1536]{1,0:T(8,128)(2,1)}, bf16[256,1536]{1,0:T(8,128)(2,1)S(1)}, u32[]{:S(2)}, u32[]{:S(2)}) collective-permute-start(bf16[256,1536]{1,0:T(8,128)(2,1)} %project.14.refs_7_), channel_id=1, source_target_pairs={{0,1},{1,0},{2,3},{3,2},{4,5},{5,4},{6,7},{7,6},{8,9},{9,8},{10,11... | collective-permute-start | bytes 2359304 | tf_op jit(solution)/shard_map/ppermute | solution.py:410
  146.9 5.0 %collective-permute-start.17 = (bf16[128,512]{1,0:T(8,128)(2,1)}, bf16[128,512]{1,0:T(8,128)(2,1)S(1)}, u32[]{:S(2)}, u32[]{:S(2)}) collective-permute-start(bf16[128,512]{1,0:T(8,128)(2,1)} %mix.8.refs_15_.mine_ref), channel_id=1, source_target_pairs={{0,1},{1,0},{2,3},{3,2},{4,5},{5,4},{6,7},{7,6},{8,9},{9,8},{10,11... | collective-permute-start | bytes 393224 | tf_op jit(solution)/shard_map/ppermute | solution.py:383
  150.5 16.6 %collective-permute-start.19 = (bf16[128,512]{1,0:T(8,128)(2,1)}, bf16[128,512]{1,0:T(8,128)(2,1)S(1)}, u32[]{:S(2)}, u32[]{:S(2)}) collective-permute-start(bf16[128,512]{1,0:T(8,128)(2,1)} %mix.9._.mine_ref), channel_id=1, source_target_pairs={{0,1},{1,0},{2,3},{3,2},{4,5},{5,4},{6,7},{7,6},{8,9},{9,8},{10,11... | collective-permute-start | bytes 393224 | tf_op jit(solution)/shard_map/ppermute | solution.py:383
  158.3 32.1 %collective-permute-start.27 = (bf16[64,3072]{1,0:T(8,128)(2,1)}, bf16[64,3072]{1,0:T(8,128)(2,1)S(1)}, u32[]{:S(2)}, u32[]{:S(2)}) collective-permute-start(bf16[64,3072]{1,0:T(8,128)(2,1)} %get-tuple-element.29), channel_id=1, source_target_pairs={{0,4},{12,8},{1,5},{13,9},{2,6},{14,10},{3,7},{15,11},{16,20},{28,... | collective-permute-start | bytes 1179656 | tf_op jit(solution)/shard_map/ppermute | solution.py:431
  161.2 33.4 %collective-permute-start.20 = (bf16[64,3072]{1,0:T(8,128)(2,1)}, bf16[64,3072]{1,0:T(8,128)(2,1)S(1)}, u32[]{:S(2)}, u32[]{:S(2)}) collective-permute-start(bf16[64,3072]{1,0:T(8,128)(2,1)} %get-tuple-element.22.refs_15_), channel_id=1, source_target_pairs={{0,4},{12,8},{1,5},{13,9},{2,6},{14,10},{3,7},{15,11},{16,20},{28,... | collective-permute-start | bytes 1179656 | tf_op jit(solution)/shard_map/ppermute | solution.py:431
  167.0 11.2 %collective-permute-start.18 = (bf16[128,512]{1,0:T(8,128)(2,1)}, bf16[128,512]{1,0:T(8,128)(2,1)S(1)}, u32[]{:S(2)}, u32[]{:S(2)}) collective-permute-start(bf16[128,512]{1,0:T(8,128)(2,1)} %mix.10._.mine_ref), channel_id=1, source_target_pairs={{0,1},{1,0},{2,3},{3,2},{4,5},{5,4},{6,7},{7,6},{8,9},{9,8},{10,11... | collective-permute-start | bytes 393224 | tf_op jit(solution)/shard_map/ppermute | solution.py:383
  175.9 8.7 %collective-permute-start.23 = (bf16[128,512]{1,0:T(8,128)(2,1)}, bf16[128,512]{1,0:T(8,128)(2,1)S(1)}, u32[]{:S(2)}, u32[]{:S(2)}) collective-permute-start(bf16[128,512]{1,0:T(8,128)(2,1)} %mix.11._.mine_ref), channel_id=1, source_target_pairs={{0,1},{1,0},{2,3},{3,2},{4,5},{5,4},{6,7},{7,6},{8,9},{9,8},{10,11... | collective-permute-start | bytes 393224 | tf_op jit(solution)/shard_map/ppermute | solution.py:383
  185.2 9.4 %copy-start.7 = (bf16[64,3072]{1,0:T(8,128)(2,1)S(1)}, bf16[64,3072]{1,0:T(8,128)(2,1)}, u32[]{:S(2)}) copy-start(bf16[64,3072]{1,0:T(8,128)(2,1)} %get-tuple-element.24._) | copy-start | bytes 1179652
  185.2 9.5 %copy-start.8 = (bf16[64,3072]{1,0:T(8,128)(2,1)S(1)}, bf16[64,3072]{1,0:T(8,128)(2,1)}, u32[]{:S(2)}) copy-start(bf16[64,3072]{1,0:T(8,128)(2,1)} %get-tuple-element.23.refs_15_) | copy-start | bytes 1179652
  190.3 13.0 %copy-start.33 = (bf16[64,3072]{1,0:T(8,128)(2,1)S(1)}, bf16[64,3072]{1,0:T(8,128)(2,1)}, u32[]{:S(2)}) copy-start(bf16[64,3072]{1,0:T(8,128)(2,1)} %get-tuple-element.27) | copy-start | bytes 1179652
  190.3 17.5 %copy-start.35 = (bf16[64,3072]{1,0:T(8,128)(2,1)S(1)}, bf16[64,3072]{1,0:T(8,128)(2,1)}, u32[]{:S(2)}) copy-start(bf16[64,3072]{1,0:T(8,128)(2,1)} %get-tuple-element.30) | copy-start | bytes 1179652
  190.3 21.4 %copy-start.16 = (bf16[64,3072]{1,0:T(8,128)(2,1)S(1)}, bf16[64,3072]{1,0:T(8,128)(2,1)}, u32[]{:S(2)}) copy-start(bf16[64,3072]{1,0:T(8,128)(2,1)} %get-tuple-element.21.refs_6_) | copy-start | bytes 1179652
  190.5 25.7 %copy-start.34 = (bf16[64,3072]{1,0:T(8,128)(2,1)S(1)}, bf16[64,3072]{1,0:T(8,128)(2,1)}, u32[]{:S(2)}) copy-start(bf16[64,3072]{1,0:T(8,128)(2,1)} %get-tuple-element.25) | copy-start | bytes 1179652
  190.5 12.7 %collective-permute-start.28 = (bf16[64,3072]{1,0:T(8,128)(2,1)S(1)}, bf16[64,3072]{1,0:T(8,128)(2,1)S(1)}, u32[]{:S(2)}, u32[]{:S(2)}) collective-permute-start(bf16[64,3072]{1,0:T(8,128)(2,1)S(1)} %get-tuple-element.35), channel_id=1, source_target_pairs={{0,4},{4,8},{1,5},{5,9},{2,6},{6,10},{3,7},{7,11},{16,20},{20,24},... | collective-permute-start | bytes 1179656 | tf_op jit(solution)/shard_map/ppermute | solution.py:431
  193.8 24.0 %copy-start.18 = (bf16[128,512]{1,0:T(8,128)(2,1)S(1)}, bf16[128,512]{1,0:T(8,128)(2,1)}, u32[]{:S(2)}) copy-start(bf16[128,512]{1,0:T(8,128)(2,1)} %copy-done.17) | copy-start | bytes 393220
  193.8 24.2 %copy-start.20 = (bf16[128,512]{1,0:T(8,128)(2,1)S(1)}, bf16[128,512]{1,0:T(8,128)(2,1)}, u32[]{:S(2)}) copy-start(bf16[128,512]{1,0:T(8,128)(2,1)} %copy-done.19) | copy-start | bytes 393220
  193.8 14.0 %collective-permute-start.30 = (bf16[64,3072]{1,0:T(8,128)(2,1)S(1)}, bf16[64,3072]{1,0:T(8,128)(2,1)S(1)}, u32[]{:S(2)}, u32[]{:S(2)}) collective-permute-start(bf16[64,3072]{1,0:T(8,128)(2,1)S(1)} %get-tuple-element.34), channel_id=1, source_target_pairs={{8,4},{12,8},{9,5},{13,9},{10,6},{14,10},{11,7},{15,11},{24,20},{2... | collective-permute-start | bytes 1179656 | tf_op jit(solution)/shard_map/ppermute | solution.py:431
  194.9 16.8 %collective-permute-start.21 = (bf16[64,3072]{1,0:T(8,128)(2,1)S(1)}, bf16[64,3072]{1,0:T(8,128)(2,1)S(1)}, u32[]{:S(2)}, u32[]{:S(2)}) collective-permute-start(bf16[64,3072]{1,0:T(8,128)(2,1)S(1)} %get-tuple-element.33), channel_id=1, source_target_pairs={{0,4},{4,8},{1,5},{5,9},{2,6},{6,10},{3,7},{7,11},{16,20},{20,24},... | collective-permute-start | bytes 1179656 | tf_op jit(solution)/shard_map/ppermute | solution.py:431
  199.4 16.8 %collective-permute-start.24 = (bf16[64,3072]{1,0:T(8,128)(2,1)S(1)}, bf16[64,3072]{1,0:T(8,128)(2,1)S(1)}, u32[]{:S(2)}, u32[]{:S(2)}) collective-permute-start(bf16[64,3072]{1,0:T(8,128)(2,1)S(1)} %get-tuple-element.32), channel_id=1, source_target_pairs={{8,4},{12,8},{9,5},{13,9},{10,6},{14,10},{11,7},{15,11},{24,20},{2... | collective-permute-start | bytes 1179656 | tf_op jit(solution)/shard_map/ppermute | solution.py:431
  203.4 16.8 %collective-permute-start.29 = (bf16[64,3072]{1,0:T(8,128)(2,1)S(1)}, bf16[64,3072]{1,0:T(8,128)(2,1)S(1)}, u32[]{:S(2)}, u32[]{:S(2)}) collective-permute-start(bf16[64,3072]{1,0:T(8,128)(2,1)S(1)} %add_convert_fusion.1), channel_id=1, source_target_pairs={{0,4},{4,8},{8,12},{1,5},{5,9},{9,13},{2,6},{6,10},{10,14},{3,7},{... | collective-permute-start | bytes 1179656 | tf_op jit(solution)/shard_map/ppermute | solution.py:431
  207.9 12.2 %collective-permute-start.31 = (bf16[64,3072]{1,0:T(8,128)(2,1)S(1)}, bf16[64,3072]{1,0:T(8,128)(2,1)S(1)}, u32[]{:S(2)}, u32[]{:S(2)}) collective-permute-start(bf16[64,3072]{1,0:T(8,128)(2,1)S(1)} %add_convert_fusion), channel_id=1, source_target_pairs={{4,0},{8,4},{12,8},{5,1},{9,5},{13,9},{6,2},{10,6},{14,10},{7,3},{... | collective-permute-start | bytes 1179656 | tf_op jit(solution)/shard_map/ppermute | solution.py:431
  211.8 15.9 %collective-permute-start.22 = (bf16[64,3072]{1,0:T(8,128)(2,1)S(1)}, bf16[64,3072]{1,0:T(8,128)(2,1)S(1)}, u32[]{:S(2)}, u32[]{:S(2)}) collective-permute-start(bf16[64,3072]{1,0:T(8,128)(2,1)S(1)} %add_convert_fusion.3), channel_id=1, source_target_pairs={{0,4},{4,8},{8,12},{1,5},{5,9},{9,13},{2,6},{6,10},{10,14},{3,7},{... | collective-permute-start | bytes 1179656 | tf_op jit(solution)/shard_map/ppermute | solution.py:431
  216.2 17.5 %copy-start.28 = (bf16[128,512]{1,0:T(8,128)(2,1)S(1)}, bf16[128,512]{1,0:T(8,128)(2,1)}, u32[]{:S(2)}) copy-start(bf16[128,512]{1,0:T(8,128)(2,1)} %copy-done.27) | copy-start | bytes 393220
  216.4 17.7 %copy-start.3 = (bf16[128,512]{1,0:T(8,128)(2,1)S(1)}, bf16[128,512]{1,0:T(8,128)(2,1)}, u32[]{:S(2)}) copy-start(bf16[128,512]{1,0:T(8,128)(2,1)} %mix.6.refs_15_.mine_ref) | copy-start | bytes 393220
  216.4 11.3 %collective-permute-start.25 = (bf16[64,3072]{1,0:T(8,128)(2,1)S(1)}, bf16[64,3072]{1,0:T(8,128)(2,1)S(1)}, u32[]{:S(2)}, u32[]{:S(2)}) collective-permute-start(bf16[64,3072]{1,0:T(8,128)(2,1)S(1)} %add_convert_fusion.2), channel_id=1, source_target_pairs={{4,0},{8,4},{12,8},{5,1},{9,5},{13,9},{6,2},{10,6},{14,10},{7,3},{... | collective-permute-start | bytes 1179656 | tf_op jit(solution)/shard_map/ppermute | solution.py:431
  224.1 10.9 %collective-permute-start.32 = (bf16[64,3072]{1,0:T(8,128)(2,1)}, bf16[64,3072]{1,0:T(8,128)(2,1)S(1)}, u32[]{:S(2)}, u32[]{:S(2)}) collective-permute-start(bf16[64,3072]{1,0:T(8,128)(2,1)} %finish.3), channel_id=1, source_target_pairs={{0,2},{2,0},{1,3},{3,1},{4,6},{6,4},{5,7},{7,5},{8,10},{10,8},{9,1... | collective-permute-start | bytes 1179656 | tf_op jit(solution)/shard_map/ppermute | solution.py:453
  232.3 10.5 %collective-permute-start.26 = (bf16[64,3072]{1,0:T(8,128)(2,1)}, bf16[64,3072]{1,0:T(8,128)(2,1)S(1)}, u32[]{:S(2)}, u32[]{:S(2)}) collective-permute-start(bf16[64,3072]{1,0:T(8,128)(2,1)} %finish.2), channel_id=1, source_target_pairs={{0,2},{2,0},{1,3},{3,1},{4,6},{6,4},{5,7},{7,5},{8,10},{10,8},{9,1... | collective-permute-start | bytes 1179656 | tf_op jit(solution)/shard_map/ppermute | solution.py:453
  (31 other events, 78.1 us)

commit v3 on v2

v3 whole, which is shorter than its diff:
```python
import functools

import jax
import jax.numpy as jnp
import ml_dtypes
import numpy as np
from jax import lax
from jax.experimental import pallas as pl
from jax.experimental.pallas import tpu as pltpu
from jax.sharding import PartitionSpec as P


norm_eps = 1e-06
lanes = 128
sublanes = 8
stat_rows = 16
halves = 2
mebibyte = 1024 * 1024


def tile_of(extent, most):
    tile = min(extent, most)
    while extent % tile:
        tile //= 2
    return tile


def block_of(slot, z):
    kind, k = slot[:2]
    below = z - k
    return z + k if kind == "d" else jnp.where(z == 0, k, below) if kind == "m" else below


def params(grant=8):
    return pltpu.CompilerParams(vmem_limit_bytes=grant * mebibyte)


def vmem(count):
    return [pl.BlockSpec(memory_space=pltpu.VMEM)] * count


def hbm():
    return [pl.BlockSpec(memory_space=pltpu.HBM)]


def order_only():
    return [pl.BlockSpec(memory_space=pl.ANY)]


def smem():
    return [pl.BlockSpec(memory_space=pltpu.SMEM)]


def first_half_kernel(x_ref, gain_ref, out_ref, squares_ref):
    half = out_ref.shape[1]
    rows = x_ref.shape[0]
    x = x_ref[:, :half].astype(jnp.float32)
    out_ref[...] = (x * gain_ref[:, :half]).astype(jnp.bfloat16)
    other = x_ref[:, half:].astype(jnp.float32)
    total = jnp.sum(x * x, axis=1, keepdims=True) + jnp.sum(other * other, axis=1, keepdims=True)
    squares_ref[...] = jnp.transpose(jnp.broadcast_to(total, (rows, lanes)))[:sublanes, :]


def first_half(x, gain):
    rows, width = x.shape
    return pl.pallas_call(
        first_half_kernel,
        in_specs=vmem(2),
        out_specs=vmem(2),
        out_shape=[
            jax.ShapeDtypeStruct((rows, width // 2), jnp.bfloat16),
            jax.ShapeDtypeStruct((sublanes, rows), jnp.float32),
        ],
        compiler_params=params(),
        name="first_half",
    )(x, gain)


def second_half_kernel(x_ref, gain_ref, mine_ref, theirs_ref, out_ref):
    rows, width = x_ref.shape
    for tile in range(width // 2 // lanes):
        place = slice(width // 2 + tile * lanes, width // 2 + (tile + 1) * lanes)
        x = x_ref[:, place].astype(jnp.float32)
        out_ref[tile * rows : (tile + 1) * rows, :] = (x * gain_ref[:, place]).astype(jnp.bfloat16)
    total = mine_ref[:1, :] + theirs_ref[:1, :]
    high = total.astype(jnp.bfloat16).astype(jnp.float32)
    row = lax.broadcasted_iota(jnp.int32, (stat_rows, rows), 0)
    both = jnp.where(row == 0, high, jnp.where(row == 1, total - high, 0.0))
    out_ref[rows * (width // 2 // lanes) :, :] = both.astype(jnp.bfloat16)


def second_half(x, gain, mine, theirs):
    rows, width = x.shape
    return pl.pallas_call(
        second_half_kernel,
        in_specs=vmem(4),
        out_specs=vmem(1)[0],
        out_shape=jax.ShapeDtypeStruct((rows * (width // 2 // lanes) + stat_rows, lanes), jnp.bfloat16),
        compiler_params=params(),
        name="second_half",
    )(x, gain, mine, theirs)


def project_kernel(layout, which, side, first, info_ref, *refs):
    x_refs = refs[: sum(layout) * len(which)]
    refs = refs[sum(layout) * len(which) :]
    carry_ref = None if first else refs[0]
    w_hbm, _, out_ref, joined, w_ref, arrived = refs if first else refs[1:]
    rows = joined.shape[0] // len(layout)
    depth = joined.shape[1] // len(which)
    streams, _, channels = w_hbm.shape
    half = channels // 2
    source = 0
    deep = slice(which[0] * depth, which[0] * depth + joined.shape[1])
    steps = 1 if side is not None else 2

    def weights(index):
        stream = index if steps == 1 else lax.div(index, 2)
        offset = info_ref[side] * half if steps == 1 else lax.rem(index, 2) * half
        place = pl.ds(pl.multiple_of(offset, half), half)
        return pltpu.make_async_copy(w_hbm.at[stream, deep, place], w_ref.at[index], arrived.at[index])

    @pl.loop(0, streams * steps)
    def _(index):
        weights(index).start()

    def total(group, place):
        x = x_refs[group[0]][place]
        for other in group[1:]:
            x = x + x_refs[other][place]
        return x

    for part, stacked in enumerate(which):
        for index, inputs in enumerate(layout):
            group = range(source, source + inputs)
            source += inputs
            here = slice(index * rows, (index + 1) * rows)
            if stacked:
                for tile in range(depth // lanes):
                    column = part * depth + tile * lanes
                    joined[here, column : column + lanes] = total(
                        group, (slice(tile * rows, (tile + 1) * rows), slice(None))
                    )
            else:
                joined[here, part * depth : (part + 1) * depth] = total(group, (slice(None), slice(None)))

    @pl.loop(0, streams * steps)
    def _(index):
        weights(index).wait()
        value = jnp.dot(joined[...], w_ref[index], preferred_element_type=jnp.float32)
        if not first:
            offset = index * channels + info_ref[side] * half
            value = value + carry_ref[:, pl.ds(pl.multiple_of(offset, half), half)]
        out_ref[:, pl.ds(pl.multiple_of(index * half, half), half)] = value.astype(out_ref.dtype)


def project(pieces, layout, which, rows, w, carry, side, info, after):
    streams, deep, channels = w.shape
    total_rows = rows * len(layout)
    depth = deep // 2 * len(which)
    final = side is not None
    width = streams * channels // (2 if final else 1)
    flat = [piece for group in pieces for piece in group]
    carried = () if carry is None else (carry,)
    return pl.pallas_call(
        functools.partial(project_kernel, layout, which, side, carry is None),
        in_specs=smem() + vmem(len(flat) + len(carried)) + hbm() + order_only(),
        out_specs=vmem(1)[0],
        out_shape=jax.ShapeDtypeStruct((total_rows, width), jnp.bfloat16 if final else jnp.float32),
        scratch_shapes=[
            pltpu.VMEM((total_rows, depth), jnp.bfloat16),
            pltpu.VMEM((width // (channels // 2), depth, channels // 2), jnp.bfloat16),
            pltpu.SemaphoreType.DMA((width // (channels // 2),)),
        ],
        compiler_params=params(46),
        cost_estimate=pl.CostEstimate(
            flops=2 * total_rows * depth * width, bytes_accessed=2 * depth * width, transcendentals=0
        ),
        name="project",
    )(info, *flat, *carried, w, after)


def wave_tables(rows):
    window = 2 * rows
    angle = np.pi / window * (2 * np.arange(rows)[:, None] + 1) * np.arange(window)[None, :]
    forward = np.concatenate([np.cos(angle), np.sin(angle)], axis=0)
    inverse = forward[:, rows:].T * (2.0 / window)

    def pair(matrix):
        exact = jnp.asarray(matrix, jnp.float32)
        high = jnp.asarray(np.asarray(matrix, ml_dtypes.bfloat16))
        low = jnp.asarray(np.asarray(matrix - np.asarray(matrix, ml_dtypes.bfloat16).astype(np.float64), ml_dtypes.bfloat16))
        return high, low

    high, low = pair(forward)
    inverse_high, inverse_low = pair(inverse)
    return jnp.concatenate([high, low], axis=0), jnp.concatenate([inverse_high, inverse_low], axis=0)


def spectrum_kernel(taps_ref, forward_ref, _, out_ref):
    taps = taps_ref.shape[1]
    both = lax.dot_general(
        forward_ref[:, :taps], taps_ref[...], (((1,), (1,)), ((), ())), preferred_element_type=jnp.float32
    )
    half = out_ref.shape[0]
    out_ref[...] = both[:half, :] + both[half:, :]


def spectrum(taps, forward, after):
    return pl.pallas_call(
        spectrum_kernel,
        in_specs=vmem(2) + order_only(),
        out_specs=vmem(1)[0],
        out_shape=jax.ShapeDtypeStruct((forward.shape[1], taps.shape[0]), jnp.float32),
        compiler_params=params(),
        name="spectrum",
    )(taps, forward, after)


def mix_kernel(slot, at, before_at, stats, full_width, info_ref, *refs):
    own, got, own_before, got_before, *refs = refs
    stat_refs = refs[: stats[0]]
    before_refs = refs[stats[0] : stats[0] + stats[1]]
    f_ref, forward_ref, inverse_ref, _, out_ref, window = refs[stats[0] + stats[1] :]
    rows, half = out_ref.shape
    block = block_of(slot, info_ref[2])
    length = info_ref[3]
    work = (block >= 0) & (block < slot[2])
    tile = tile_of(half, 256)

    def scale_of(stat_refs):
        total = jnp.zeros((1, rows), jnp.float32)
        for ref in stat_refs:
            last = ref.shape[0] - stat_rows
            pair = ref[last:, :].astype(jnp.float32)
            total = total + pair[:1, :] + pair[1:2, :]
        total = jnp.transpose(jnp.broadcast_to(total, (lanes, rows)))
        scale = lax.rsqrt(total / full_width + norm_eps)
        return jnp.concatenate([scale] * (tile // lanes), axis=1)

    def joined(a_ref, b_ref, at, stream, column):
        place = (slice(at * rows, (at + 1) * rows), slice(stream * half + column, stream * half + column + tile))
        return a_ref[place].astype(jnp.float32) + b_ref[place].astype(jnp.float32)

    @pl.when(work)
    def _():
        row = lax.broadcasted_iota(jnp.int32, (rows, 1), 0)
        scale = scale_of(stat_refs)
        live = (row + block * rows < length).astype(jnp.float32)
        for column in range(0, half, tile):
            here = joined(own, got, at, 1, column) * scale * (joined(own, got, at, 2, column) * scale) * live
            window[rows:, column : column + tile] = here.astype(jnp.bfloat16)

        @pl.when(block > 0)
        def _():
            scale = scale_of(before_refs)
            live = (row + (block - 1) * rows < length).astype(jnp.float32)
            for column in range(0, half, tile):
                key = joined(own_before, got_before, before_at, 1, column) * scale
                value = joined(own_before, got_before, before_at, 2, column) * scale
                window[:rows, column : column + tile] = (key * value * live).astype(jnp.bfloat16)

        @pl.when(block == 0)
        def _():
            window[:rows, :] = jnp.zeros((rows, half), jnp.bfloat16)

        for column in range(0, half, tile):
            place = slice(column, column + tile)
            both = jnp.dot(forward_ref[...], window[:, place], preferred_element_type=jnp.float32)
            cosine = both[:rows, :] + both[2 * rows : 3 * rows, :]
            sine = both[rows : 2 * rows, :] + both[3 * rows :, :]
            channel = pl.ds(pl.multiple_of(info_ref[0] * half + column, tile), tile)
            f_cosine = f_ref[:rows, channel]
            f_sine = f_ref[rows:, channel]
            product = jnp.concatenate(
                [cosine * f_cosine - sine * f_sine, cosine * f_sine + sine * f_cosine], axis=0
            )
            high = product.astype(jnp.bfloat16)
            low = (product - high.astype(jnp.float32)).astype(jnp.bfloat16)
            back = jnp.dot(inverse_ref[...], high, preferred_element_type=jnp.float32)
            conv = back[:rows, :] + back[rows:, :]
            conv = conv + jnp.dot(inverse_ref[:rows, :], low, preferred_element_type=jnp.float32)
            out_ref[:, place] = (joined(own, got, at, 0, column) * scale * conv * live).astype(jnp.bfloat16)

    @pl.when(jnp.logical_not(work))
    def _():
        out_ref[...] = jnp.zeros_like(out_ref)


def mix(slot, here, before, stats, before_stats, rows, waves, filter_waves, full_width, info, after):
    own, got, at = here
    own_before, got_before, before_at = before
    half = filter_waves.shape[1] // 2
    counts = (len(stats), len(before_stats))
    return pl.pallas_call(
        functools.partial(mix_kernel, slot, at, before_at, counts, full_width),
        in_specs=smem() + vmem(4 + sum(counts) + 3) + order_only(),
        out_specs=vmem(1)[0],
        out_shape=jax.ShapeDtypeStruct((rows, half), jnp.bfloat16),
        scratch_shapes=[pltpu.VMEM((2 * rows, half), jnp.bfloat16)],
        compiler_params=params(),
        cost_estimate=pl.CostEstimate(
            flops=16 * rows * rows * half, bytes_accessed=32 * rows * half, transcendentals=0
        ),
        name="mix",
    )(info, own, got, own_before, got_before, *stats, *before_stats, filter_waves, *waves, after)


def emit_kernel(slot, info_ref, mine_ref, theirs_ref, w_hbm, _, *refs):
    *out_refs, w_ref, arrived = refs
    block = block_of(slot, info_ref[2])
    work = (block >= 0) & (block < slot[2])
    chunk, width = out_refs[0].shape
    half = mine_ref.shape[1]
    tile = tile_of(width, 512)

    @pl.when(work)
    def _():
        mine = pl.ds(pl.multiple_of(info_ref[0] * half, half), half)
        theirs = pl.ds(pl.multiple_of(info_ref[1] * half, half), half)

        def weights(index):
            place = pl.ds(pl.multiple_of(index * tile, tile), tile)
            return pltpu.make_async_copy(w_hbm.at[:, place], w_ref.at[index], arrived.at[index])

        @pl.loop(0, width // tile)
        def _(index):
            weights(index).start()

        @pl.loop(0, width // tile)
        def _(index):
            weights(index).wait()
            product = jnp.dot(mine_ref[...], w_ref[index, mine, :], preferred_element_type=jnp.float32)
            product = product + jnp.dot(theirs_ref[...], w_ref[index, theirs, :], preferred_element_type=jnp.float32)
            product = product.astype(jnp.bfloat16)
            place = pl.ds(pl.multiple_of(index * tile, tile), tile)
            for part, out_ref in enumerate(out_refs):
                out_ref[:, place] = product[part * chunk : (part + 1) * chunk, :]

    @pl.when(jnp.logical_not(work))
    def _():
        for out_ref in out_refs:
            out_ref[...] = jnp.zeros_like(out_ref)


def emit(slot, mine, theirs, w, info, after):
    rows, half = mine.shape
    width = w.shape[1]
    chunk = rows // halves
    return pl.pallas_call(
        functools.partial(emit_kernel, slot),
        in_specs=smem() + vmem(2) + hbm() + order_only(),
        out_specs=vmem(halves),
        out_shape=[jax.ShapeDtypeStruct((chunk, width), jnp.bfloat16)] * halves,
        scratch_shapes=[
            pltpu.VMEM((width // tile_of(width, 512), w.shape[0], tile_of(width, 512)), jnp.bfloat16),
            pltpu.SemaphoreType.DMA((width // tile_of(width, 512),)),
        ],
        compiler_params=params(50),
        cost_estimate=pl.CostEstimate(
            flops=4 * rows * half * width, bytes_accessed=4 * half * width, transcendentals=0
        ),
        name="emit",
    )(info, mine, theirs, w, after)


def finish_kernel(index, x_ref, *refs):
    chunk = refs[-1].shape[0]
    total = x_ref[index * chunk : (index + 1) * chunk, :].astype(jnp.float32)
    for ref in refs[:-1]:
        total = total + ref[...].astype(jnp.float32)
    refs[-1][...] = total.astype(jnp.bfloat16)


def finish(x, index, terms):
    chunk, width = terms[0].shape
    return pl.pallas_call(
        functools.partial(finish_kernel, index),
        in_specs=vmem(1 + len(terms)),
        out_specs=vmem(1)[0],
        out_shape=jax.ShapeDtypeStruct((chunk, width), jnp.bfloat16),
        compiler_params=params(),
        cost_estimate=pl.CostEstimate(
            flops=chunk * width * len(terms), bytes_accessed=2 * chunk * width * (len(terms) + 2), transcendentals=0
        ),
        name="finish",
    )(x, *terms)


def added(*terms):
    total = terms[0].astype(jnp.float32)
    for term in terms[1:]:
        total = total + term.astype(jnp.float32)
    return total.astype(jnp.bfloat16)


def layer(spans, norm_gain, w_in, filters, w_out, prompt_len, needles):
    count = lax.axis_size("ctx")
    place = lax.axis_index("ctx")
    x_local = spans[0]
    rows, half_width = x_local.shape
    full_width = half_width * lax.axis_size("mp")
    weights = jnp.swapaxes(w_in[0], 0, 1)
    up = [(source, source + 1) for source in range(count - 1)]
    down = [(source + 1, source) for source in range(count - 1)]
    partner = [(0, 1), (1, 0)] if lax.axis_size("mp") == 2 else None

    far = count - 1
    order = [("d", 0)] + [(kind, k) for k in range(1, far) for kind in "du"] + [("m", far)]
    z = place.astype(jnp.int32)

    core = lax.axis_index("mp").astype(jnp.int32)
    info = jnp.concatenate([jnp.stack([core, 1 - core, z]), prompt_len])
    waves = wave_tables(rows)
    leading, squares = first_half(x_local, norm_gain)
    other_squares = lax.ppermute(squares, "mp", partner)
    pieces = [leading, second_half(x_local, norm_gain, squares, other_squares)]
    gathered = {("d", 0): pieces, ("u", 0): pieces}
    for k in range(1, count):
        gathered["u", k] = []
        gathered["d", k] = []
        for i in range(halves):
            value = lax.ppermute(gathered["u", k - 1][i], "ctx", [(a, b) for a, b in up if a >= k - 1])
            gathered["u", k].append(value)
            value = lax.ppermute(gathered["d", k - 1][i], "ctx", [(a, b) for a, b in down if a <= count - k])
            gathered["d", k].append(value)

    held = {}
    gated = {}
    sums = {}

    def stats_of(kind, k):
        if 2 * k >= count:
            return [gathered["u", k][-1], gathered["d", k][-1]]
        return [gathered["d" if kind == "m" else kind, k][-1]]

    def combine(kind, k, after):
        before = ("u", k + 1) if kind == "u" or k == 0 else ("d", k - 1)
        mine = mix(
            (kind, k, count), held["d" if kind == "m" else kind, k], held[before],
            stats_of(kind, k), stats_of(*before), rows, waves, filter_waves, full_width, info, after,
        )
        gated[kind, k] = (mine, lax.ppermute(mine, "mp", partner))
        return mine

    def spread(kind, k, after):
        sums[kind, k] = emit((kind, k, count), *gated[kind, k], w_out[0], info, after)
        return sums[kind, k][0]

    filter_waves = spectrum(filters[0], waves[0], pieces[1])
    after = filter_waves
    for group in groups_of(count):
        name = group[0]
        layout = []
        inputs = [[] for _ in range(halves)]
        for k in group:
            merged = 2 * k >= count
            for kind in ("d",) if k == 0 else ("ud",) if merged else ("u", "d"):
                for way in kind:
                    held[way, k] = len(layout)
                    for i in range(halves):
                        inputs[i].append(gathered[way, k][i])
                layout.append(len(kind))
        carry = None
        for i in range(halves - 1 if name else 0):
            carry = project(inputs[i : i + 1], layout, (i,), rows, weights, carry, None, info, after)
            after = carry
        inputs, which = (inputs[-1:], (1,)) if name else (inputs, (0, 1))
        theirs = project(inputs, layout, which, rows, weights, carry, 1, info, after)
        got = lax.ppermute(theirs, "mp", partner)
        mine = project(inputs, layout, which, rows, weights, carry, 0, info, theirs)
        after = mine
        for k in group:
            for way in "d" if k == 0 else "ud":
                held[way, k] = (mine, got, held[way, k])
        for kind, k in early_slots(count) if name == 1 else ():
            after = combine(kind, k, after)
        for kind, k in early_slots(count) if name == 1 else ():
            after = spread(kind, k, after)
    rest = [slot for slot in [("m", far)] + [(kind, k) for k in range(far - 1, 0, -1) for kind in "ud"] + [("d", 0)]]
    rest = [slot for slot in rest if slot not in sums]
    after = combine(*rest[0], after)
    for index, slot in enumerate(rest):
        if index + 1 < len(rest):
            after = combine(*rest[index + 1], after)
        after = spread(*slot, after)

    def reduce_step(values, pairs):
        moved = []
        for value in values:
            moved.append(lax.ppermute(value, "ctx", pairs))
        return moved

    terms = [sums["d", 0]]
    for k in range(far, 0, -1):
        to_up = [(a, b) for a, b in up if a + k <= far]
        to_down = [(a, b) for a, b in down if a >= k]
        if k == far and far != 2:
            arrived = [reduce_step(sums["m", far], to_up + to_down)] * 2
        else:
            from_up, from_down = ("m", "m") if k == far else ("d", "u")
            arrived = [reduce_step(sums[from_up, k], to_up), reduce_step(sums[from_down, k], to_down)]
        if k > 1:
            for kind, moved in zip("du", arrived):
                sums[kind, k - 1] = [added(a, b) for a, b in zip(sums[kind, k - 1], moved)]
        else:
            terms += arrived if far > 1 else arrived[:1]
    sections = lax.axis_size("section")
    turn = [(source, (source + 1) % sections) for source in range(sections)]
    advanced = []
    for i in range(halves):
        final = finish(x_local, i, [term[i] for term in terms])
        advanced.append(lax.ppermute(final, "section", turn))
    advanced = jnp.concatenate(advanced, axis=0)[None]

    row = jnp.arange(rows, dtype=jnp.int32)
    picked = [0.0, 0.0]
    for slot in order:
        one_hot = (needles[0][:, None] == (row + block_of(slot, z) * rows)[None, :]).astype(jnp.bfloat16)
        for index, part in enumerate(gated[slot]):
            picked[index] += jnp.dot(one_hot, part, preferred_element_type=jnp.float32)
    mine, theirs = [value.astype(jnp.bfloat16) for value in picked]
    lower = jnp.where(core == 0, mine, theirs)
    upper = jnp.where(core == 0, theirs, mine)
    return (advanced, jnp.concatenate([lower, upper], axis=1)[None])


def groups_of(count):
    return [[0], [1]] + [list(range(k, min(k + 2, count))) for k in range(2, count, 2)]


def early_slots(count):
    return [("d", 0), ("d", 1)] if count > 2 else []


def solution(mesh):
    return jax.shard_map(
        layer,
        mesh=mesh,
        in_specs=(
            P("section", ("groups", "ctx"), "mp"),
            P("section", "mp"),
            P("section", "mp", None, "ctx"),
            P("section", "ctx", None),
            P("section", "ctx", "mp"),
            P(("groups", "section")),
            P("section", "groups"),
        ),
        out_specs=(P("section", ("groups", "ctx"), "mp"), P("section", "groups", "ctx")),
        check_vma=False,
    )
```

time: 248 us -> 181 us (0.73); the launches traced: 244 us -> 179 us
  Pallas kernels: 125 us -> 72 us
  blocking collectives: 20.6 us -> 0 us
  starting transfers between devices: 50.2 us -> 63.4 us
  local copies, waits for them, and re-layouts: 15.1 us -> 10.3 us
    pallas_call x24 -> x25, Pallas kernels: 125 us -> 72 us  [the longest x8 41 us: project(): pl.pallas_call(functools.partial(project_kernel, layout, which, side, car...]
    psum x1 -> x0, blocking collectives: 20.6 us -> none  [layer(): total = lax.psum(mine.reshape(-1), ('ctx', 'mp'))]
    ppermute x10, starting transfers between devices: 25.3 us -> 33.8 us  [reduce_step(): moved.append(lax.ppermute(value, 'ctx', pairs))]
    ppermute x6, starting transfers between devices: 12.3 us -> 16.6 us  [layer(): lax.ppermute(gathered['u', k - 1][i], 'ctx', [(a, b) for a, b in up if a...]
    ppermute x6, waiting for transfers between devices: 5.39 us -> 2.16 us  [layer(): lax.ppermute(gathered['d', k - 1][i], 'ctx', [(a, b) for a, b in down if...]
    unnamed x92 -> x50, local copies, waits for them, and re-layouts: 13.3 us -> 10.3 us
    ppermute x10, waiting for transfers between devices: 9.7 us -> 12.5 us  [reduce_step(): moved.append(lax.ppermute(value, 'ctx', pairs))]
    add x6, other arithmetic: 0.02 us -> 2.68 us  [layer(): row + block_of(slot, z) * rows]
  transfers between devices with their start and end apart: 33 -> 34, of which waited for: 7 -> 9; matrix products, arithmetic and copies ran while one was open for 3% -> 5% of each run, Pallas kernels for 44% -> 33%
where the time goes in v3:
time: 181 us; the launch traced here: 179 us
  Pallas kernels  72 us (40%)
  starting transfers between devices  63.4 us (35%)
  waiting for transfers between devices  22.3 us (12%)
  local copies, waits for them, and re-layouts  10.3 us (6%)
  other arithmetic  5.06 us (3%)
  matrix products  4.29 us (2%)
  between operations  2.02 us (1%)
    pallas_call x8, Pallas kernels, project(): pl.pallas_call(functools.partial(project_kernel, layout, which, side, car...  41 us
    ppermute x10, starting transfers between devices, reduce_step(): moved.append(lax.ppermute(value, 'ctx', pairs))  33.8 us
    pallas_call x6, Pallas kernels, emit(): pl.pallas_call(functools.partial(emit_kernel, slot), in_specs=smem() + vm...  17.1 us
    ppermute x6, starting transfers between devices, layer(): lax.ppermute(gathered['u', k - 1][i], 'ctx', [(a, b) for a, b in up if a...  16.6 us
    pallas_call x6, Pallas kernels, mix(): pl.pallas_call(functools.partial(mix_kernel, slot, at, before_at, counts,...  12.7 us
    ppermute x10, waiting for transfers between devices, reduce_step(): moved.append(lax.ppermute(value, 'ctx', pairs))  12.5 us
    unnamed x50, local copies, waits for them, and re-layouts  10.3 us
    ppermute x6, starting transfers between devices, layer(): lax.ppermute(gathered['d', k - 1][i], 'ctx', [(a, b) for a, b in down if...  7.72 us
  transfers between devices with their start and end apart: 34, of which 9 were waited for; matrix products, arithmetic and copies ran while one was open for 5% of the time, Pallas kernels for 33%

profile of v3, /device:TPU:0, one launch (start us, length us, event | category | flops | bytes accessed | tf_op | source)
XLA Modules:
  0.0 179.4 jit_solution(17769843255936489272)
XLA Ops:
  2.8 1.3 collective-permute-start.5
  4.1 6.4 %collective-permute-start.4 = (bf16[128,1536]{1,0:T(8,128)(2,1)S(1)}, bf16[128,1536]{1,0:T(8,128)(2,1)}, u32[]{:S(2)}, u32[]{:S(2)}) collective-permute-start(bf16[128,1536]{1,0:T(8,128)(2,1)S(1)} %get-tuple-element.16.refs_0_), channel_id=1, source_target_pairs={{0,4},{4,8},{8,12},{1,5},{5,9},{9,13},{2,6},{6,10},{10,14},{3,7},{... | collective-permute-start | bytes 1179656 | tf_op jit(solution)/shard_map/ppermute | solution.py:423
  11.6 1.1 copy-done.5
  13.5 1.3 collective-permute-start.3
  14.8 5.3 %collective-permute-start.2 = (bf16[1552,128]{1,0:T(8,128)(2,1)S(1)}, bf16[1552,128]{1,0:T(8,128)(2,1)}, u32[]{:S(2)}, u32[]{:S(2)}) collective-permute-start(bf16[1552,128]{1,0:T(8,128)(2,1)S(1)} %second_half.1._.refs_1_.refs_4_.refs_5_), channel_id=1, source_target_pairs={{0,4},{4,8},{8,12},{1,5},{5,9},{9,13},{2,6},{6,10},{10,14},{3,7},{... | collective-permute-start | bytes 1191944 | tf_op jit(solution)/shard_map/ppermute | solution.py:423
  22.4 4.9 %project.8.refs_3_ = bf16[128,1536]{1,0:T(8,128)(2,1)S(1)} custom-call(s32[4]{0:T(128)S(1)} %pad_add_fusion.info_ref, bf16[128,1536]{1,0:T(8,128)(2,1)S(1)} %get-tuple-element.16.refs_0_, bf16[1552,128]{1,0:T(8,128)(2,1)S(1)} %second_half.1._.refs_1_.refs_4_.refs_5_, bf16[3,3072,1024]{2,1,0:T(8,128)(2,1)} %bitcast.31, ...), custom_call_target="tpu_custom_call" | custom-call | flops 1207959552 | bytes 9437184 | tf_op jit(solution)/shard_map/project/pallas_call | solution.py:165
  27.4 4.9 %project.9.refs_3_.refs_0_.refs_2_ = bf16[128,1536]{1,0:T(8,128)(2,1)S(1)} custom-call(s32[4]{0:T(128)S(1)} %pad_add_fusion.info_ref, bf16[128,1536]{1,0:T(8,128)(2,1)S(1)} %get-tuple-element.16.refs_0_, bf16[1552,128]{1,0:T(8,128)(2,1)S(1)} %second_half.1._.refs_1_.refs_4_.refs_5_, bf16[3,3072,1024]{2,1,0:T(8,128)(2,1)} %bitcast.32, ...), custom_call_target="tpu_custom_call" | custom-call | flops 1207959552 | bytes 9437184 | tf_op jit(solution)/shard_map/project/pallas_call | solution.py:165
  32.3 6.2 %project.10.refs_2_.refs_4_ = f32[256,3072]{1,0:T(8,128)S(1)} custom-call(s32[4]{0:T(128)S(1)} %pad_add_fusion.info_ref, bf16[128,1536]{1,0:T(8,128)(2,1)} %collective-permute-done.4.refs_0_, bf16[128,1536]{1,0:T(8,128)(2,1)} %collective-permute-done.5.refs_1_, bf16[3,3072,1024]{2,1,0:T(8,128)(2,1)} %bitcast.33, ...), custom_call_target="tpu_custom_call" | custom-call | flops 2415919104 | bytes 9437184 | tf_op jit(solution)/shard_map/project/pallas_call | solution.py:165
  38.5 5.8 %project.11.refs_4_ = bf16[256,1536]{1,0:T(8,128)(2,1)} custom-call(s32[4]{0:T(128)S(1)} %pad_add_fusion.info_ref, bf16[1552,128]{1,0:T(8,128)(2,1)} %collective-permute-done.2.refs_0_.refs_5_.refs_4_, bf16[1552,128]{1,0:T(8,128)(2,1)} %collective-permute-done.3.refs_1_.refs_4_.refs_6_, f32[256,3072]{1,0:T(8,128)S(1)} %project.10.refs_2_.refs_4_, ...), custom_call_target="tpu_custom_call" | custom-call | flops 1207959552 | bytes 4718592 | tf_op jit(solution)/shard_map/project/pallas_call | solution.py:165
  44.9 1.3 collective-permute-start.14
  46.1 1.4 collective-permute-start.13
  48.7 1.3 collective-permute-start.10
  52.0 1.9 %copy-done.1 = f32[256,3072]{1,0:T(8,128)S(1)} copy-done((f32[256,3072]{1,0:T(8,128)S(1)}, f32[256,3072]{1,0:T(8,128)}, u32[]{:S(2)}) %copy-start.1) | copy-done | bytes 3145752
  53.9 4.4 %project.12.refs_2_.refs_9_.refs_0_ = bf16[256,1536]{1,0:T(8,128)(2,1)S(1)} custom-call(s32[4]{0:T(128)S(1)} %pad_add_fusion.info_ref, bf16[1552,128]{1,0:T(8,128)(2,1)} %collective-permute-done.2.refs_0_.refs_5_.refs_4_, bf16[1552,128]{1,0:T(8,128)(2,1)} %collective-permute-done.3.refs_1_.refs_4_.refs_6_, f32[256,3072]{1,0:T(8,128)S(1)} %copy-done.1, ...), custom_call_target="tpu_custom_call" | custom-call | flops 1207959552 | bytes 4718592 | tf_op jit(solution)/shard_map/project/pallas_call | solution.py:165
  59.0 1.3 collective-permute-start.16
  60.3 1.4 collective-permute-start.15
  61.8 2.3 %mix.6.refs_9_.mine_ref = bf16[128,512]{1,0:T(8,128)(2,1)S(1)} custom-call(s32[4]{0:T(128)S(1)} %pad_add_fusion.info_ref, bf16[128,1536]{1,0:T(8,128)(2,1)S(1)} %copy-done.8, bf16[128,1536]{1,0:T(8,128)(2,1)S(1)} %copy-done.12, bf16[256,1536]{1,0:T(8,128)(2,1)S(1)} %project.12.refs_2_.refs_9_.refs_0_, ...), custom_call_target="tpu_custom_call" | custom-call | flops 134217728 | bytes 2097152 | tf_op jit(solution)/shard_map/mix/pallas_call | solution.py:295
  65.2 1.3 collective-permute-done.10.refs_1_.refs_7_.refs_5_.refs_6_
  66.6 1.3 collective-permute-start.12
  67.9 1.4 collective-permute-start.11
  71.3 3.1 %mix.7._.mine_ref = bf16[128,512]{1,0:T(8,128)(2,1)} custom-call(s32[4]{0:T(128)S(1)} %pad_add_fusion.info_ref, bf16[256,1536]{1,0:T(8,128)(2,1)S(1)} %project.12.refs_2_.refs_9_.refs_0_, bf16[256,1536]{1,0:T(8,128)(2,1)} %collective-permute-done.6.refs_3_.refs_1_, bf16[128,1536]{1,0:T(8,128)(2,1)S(1)} %copy-done.9, bf16[128,1536]{1,0:T(8,128)(2,1)S(1)} %copy-done.13, ...), custom_call_target="tpu_custom_call" | custom-call | flops 134217728 | bytes 2097152 | tf_op jit(solution)/shard_map/mix/pallas_call | solution.py:295
  74.4 4.1 %emit.6 = (bf16[64,3072]{1,0:T(8,128)(2,1)S(1)}, bf16[64,3072]{1,0:T(8,128)(2,1)S(1)}) custom-call(s32[4]{0:T(128)S(1)} %pad_add_fusion.info_ref, bf16[128,512]{1,0:T(8,128)(2,1)S(1)} %mix.6.refs_9_.mine_ref, bf16[128,512]{1,0:T(8,128)(2,1)} %collective-permute-done.7.theirs_ref, bf16[1024,3072]{1,0:T(8,128)(2,1)} %bitcast.39, bf16[128,512]{1,0:T(8,128)(2,1)} %mix.7._.mine_ref), custom_call_target="tpu_custom_call" | custom-call | flops 805306368 | bytes 6291456 | tf_op jit(solution)/shard_map/emit/pallas_call | solution.py:350
  78.6 4.1 %emit.7 = (bf16[64,3072]{1,0:T(8,128)(2,1)S(1)}, bf16[64,3072]{1,0:T(8,128)(2,1)S(1)}) custom-call(s32[4]{0:T(128)S(1)} %pad_add_fusion.info_ref, bf16[128,512]{1,0:T(8,128)(2,1)} %mix.7._.mine_ref, bf16[128,512]{1,0:T(8,128)(2,1)S(1)} %collective-permute-done.8.theirs_ref, bf16[1024,3072]{1,0:T(8,128)(2,1)} %bitcast.40, ...), custom_call_target="tpu_custom_call" | custom-call | flops 805306368 | bytes 6291456 | tf_op jit(solution)/shard_map/emit/pallas_call | solution.py:350
  82.7 6.3 %project.13.refs_4_.refs_6_ = f32[256,3072]{1,0:T(8,128)S(1)} custom-call(s32[4]{0:T(128)S(1)} %pad_add_fusion.info_ref, bf16[128,1536]{1,0:T(8,128)(2,1)} %collective-permute-done.13.refs_0_, bf16[128,1536]{1,0:T(8,128)(2,1)} %collective-permute-done.14.refs_1_, bf16[128,1536]{1,0:T(8,128)(2,1)} %collective-permute-done.15.refs_2_, ...), custom_call_target="tpu_custom_call" | custom-call | flops 2415919104 | bytes 9437184 | tf_op jit(solution)/shard_map/project/pallas_call | solution.py:165
  89.1 4.3 %project.14.refs_6_ = bf16[256,1536]{1,0:T(8,128)(2,1)S(1)} custom-call(s32[4]{0:T(128)S(1)} %pad_add_fusion.info_ref, bf16[1552,128]{1,0:T(8,128)(2,1)S(1)} %collective-permute-done.9.refs_0_.refs_6_.refs_4_.refs_5_, bf16[1552,128]{1,0:T(8,128)(2,1)S(1)} %collective-permute-done.10.refs_1_.refs_7_.refs_5_.refs_6_, ...), custom_call_target="tpu_custom_call" | custom-call | flops 1207959552 | bytes 4718592 | tf_op jit(solution)/shard_map/project/pallas_call | solution.py:165
  95.2 4.3 %project.15.refs_0_.refs_2_.refs_11_ = bf16[256,1536]{1,0:T(8,128)(2,1)S(1)} custom-call(s32[4]{0:T(128)S(1)} %pad_add_fusion.info_ref, bf16[1552,128]{1,0:T(8,128)(2,1)S(1)} %collective-permute-done.9.refs_0_.refs_6_.refs_4_.refs_5_, bf16[1552,128]{1,0:T(8,128)(2,1)S(1)} %collective-permute-done.10.refs_1_.refs_7_.refs_5_.refs_6_, ...), custom_call_target="tpu_custom_call" | custom-call | flops 1207959552 | bytes 4718592 | tf_op jit(solution)/shard_map/project/pallas_call | solution.py:165
  99.8 2.3 %mix.8.refs_11_.mine_ref = bf16[128,512]{1,0:T(8,128)(2,1)S(1)} custom-call(s32[4]{0:T(128)S(1)} %pad_add_fusion.info_ref, bf16[256,1536]{1,0:T(8,128)(2,1)S(1)} %project.15.refs_0_.refs_2_.refs_11_, bf16[256,1536]{1,0:T(8,128)(2,1)S(1)} %collective-permute-done.17.refs_1_.refs_3_, bf16[256,1536]{1,0:T(8,128)(2,1)S(1)} %project.15.refs_0_.refs_2_.refs_11_, ...), custom_call_target="tpu_custom_call" | custom-call | flops 134217728 | bytes 2097152 | tf_op jit(solution)/shard_map/mix/pallas_call | solution.py:295
  102.2 1.1 mix.9._.mine_ref
  104.1 3.8 %emit.8 = (bf16[64,3072]{1,0:T(8,128)(2,1)S(1)}, bf16[64,3072]{1,0:T(8,128)(2,1)S(1)}) custom-call(s32[4]{0:T(128)S(1)} %pad_add_fusion.info_ref, bf16[128,512]{1,0:T(8,128)(2,1)S(1)} %mix.8.refs_11_.mine_ref, bf16[128,512]{1,0:T(8,128)(2,1)S(1)} %collective-permute-done.18.theirs_ref, bf16[1024,3072]{1,0:T(8,128)(2,1)} %bitcast.41, ...), custom_call_target="tpu_custom_call" | custom-call | flops 805306368 | bytes 6291456 | tf_op jit(solution)/shard_map/emit/pallas_call | solution.py:350
  107.9 6.6 %collective-permute-start.21 = (bf16[64,3072]{1,0:T(8,128)(2,1)S(1)}, bf16[64,3072]{1,0:T(8,128)(2,1)S(1)}, u32[]{:S(2)}, u32[]{:S(2)}) collective-permute-start(bf16[64,3072]{1,0:T(8,128)(2,1)S(1)} %get-tuple-element.20.refs_10_), channel_id=1, source_target_pairs={{0,4},{12,8},{1,5},{13,9},{2,6},{14,10},{3,7},{15,11},{16,20},{28,... | collective-permute-start | bytes 1179656 | tf_op jit(solution)/shard_map/ppermute | solution.py:491
  114.5 2.4 %mix.10._.mine_ref = bf16[128,512]{1,0:T(8,128)(2,1)S(1)} custom-call(s32[4]{0:T(128)S(1)} %pad_add_fusion.info_ref, bf16[256,1536]{1,0:T(8,128)(2,1)S(1)} %project.15.refs_0_.refs_2_.refs_11_, bf16[256,1536]{1,0:T(8,128)(2,1)S(1)} %collective-permute-done.17.refs_1_.refs_3_, bf16[256,1536]{1,0:T(8,128)(2,1)S(1)} %project.12.refs_2_.refs_9_.refs_0_, ...), custom_call_target="tpu_custom_call" | custom-call | flops 134217728 | bytes 2097152 | tf_op jit(solution)/shard_map/mix/pallas_call | solution.py:295
  117.2 1.6 collective-permute-start.28
  119.7 1.4 mix.11._.mine_ref
  121.9 3.8 %emit.10 = (bf16[64,3072]{1,0:T(8,128)(2,1)S(1)}, bf16[64,3072]{1,0:T(8,128)(2,1)S(1)}) custom-call(s32[4]{0:T(128)S(1)} %pad_add_fusion.info_ref, bf16[128,512]{1,0:T(8,128)(2,1)S(1)} %mix.10._.mine_ref, bf16[128,512]{1,0:T(8,128)(2,1)S(1)} %collective-permute-done.19.theirs_ref, bf16[1024,3072]{1,0:T(8,128)(2,1)} %bitcast.43, ...), custom_call_target="tpu_custom_call" | custom-call | flops 805306368 | bytes 6291456 | tf_op jit(solution)/shard_map/emit/pallas_call | solution.py:350
  127.2 6.0 %collective-permute-start.22 = (bf16[64,3072]{1,0:T(8,128)(2,1)S(1)}, bf16[64,3072]{1,0:T(8,128)(2,1)S(1)}, u32[]{:S(2)}, u32[]{:S(2)}) collective-permute-start(bf16[64,3072]{1,0:T(8,128)(2,1)S(1)} %get-tuple-element.31), channel_id=1, source_target_pairs={{0,4},{4,8},{1,5},{5,9},{2,6},{6,10},{3,7},{7,11},{16,20},{20,24},... | collective-permute-start | bytes 1179656 | tf_op jit(solution)/shard_map/ppermute | solution.py:491
  134.3 5.2 %collective-permute-start.29 = (bf16[64,3072]{1,0:T(8,128)(2,1)S(1)}, bf16[64,3072]{1,0:T(8,128)(2,1)S(1)}, u32[]{:S(2)}, u32[]{:S(2)}) collective-permute-start(bf16[64,3072]{1,0:T(8,128)(2,1)S(1)} %get-tuple-element.33), channel_id=1, source_target_pairs={{0,4},{4,8},{1,5},{5,9},{2,6},{6,10},{3,7},{7,11},{16,20},{20,24},... | collective-permute-start | bytes 1179656 | tf_op jit(solution)/shard_map/ppermute | solution.py:491
  139.6 1.3 collective-permute-start.26
  140.9 1.9 %collective-permute-done.22 = bf16[64,3072]{1,0:T(8,128)(2,1)S(1)} collective-permute-done((bf16[64,3072]{1,0:T(8,128)(2,1)S(1)}, bf16[64,3072]{1,0:T(8,128)(2,1)S(1)}, u32[]{:S(2)}, u32[]{:S(2)}) %collective-permute-start.22) | collective-permute-done | bytes 393248 | tf_op jit(solution)/shard_map/ppermute | solution.py:491
  142.8 5.2 %collective-permute-start.23 = (bf16[64,3072]{1,0:T(8,128)(2,1)S(1)}, bf16[64,3072]{1,0:T(8,128)(2,1)S(1)}, u32[]{:S(2)}, u32[]{:S(2)}) collective-permute-start(bf16[64,3072]{1,0:T(8,128)(2,1)S(1)} %add_convert_fusion.3), channel_id=1, source_target_pairs={{0,4},{4,8},{8,12},{1,5},{5,9},{9,13},{2,6},{6,10},{10,14},{3,7},{... | collective-permute-start | bytes 1179656 | tf_op jit(solution)/shard_map/ppermute | solution.py:491
  148.1 1.3 collective-permute-start.32
  149.4 1.8 collective-permute-done.29
  151.3 5.2 %collective-permute-start.30 = (bf16[64,3072]{1,0:T(8,128)(2,1)S(1)}, bf16[64,3072]{1,0:T(8,128)(2,1)S(1)}, u32[]{:S(2)}, u32[]{:S(2)}) collective-permute-start(bf16[64,3072]{1,0:T(8,128)(2,1)S(1)} %add_convert_fusion.1), channel_id=1, source_target_pairs={{0,4},{4,8},{8,12},{1,5},{5,9},{9,13},{2,6},{6,10},{10,14},{3,7},{... | collective-permute-start | bytes 1179656 | tf_op jit(solution)/shard_map/ppermute | solution.py:491
  156.8 2.7 %collective-permute-done.23.refs_1_ = bf16[64,3072]{1,0:T(8,128)(2,1)S(1)} collective-permute-done((bf16[64,3072]{1,0:T(8,128)(2,1)S(1)}, bf16[64,3072]{1,0:T(8,128)(2,1)S(1)}, u32[]{:S(2)}, u32[]{:S(2)}) %collective-permute-start.23) | collective-permute-done | bytes 393248 | tf_op jit(solution)/shard_map/ppermute | solution.py:491
  159.8 1.6 collective-permute-start.27
  161.4 1.4 collective-permute-done.32.refs_2_
  162.7 4.8 %collective-permute-done.30.refs_1_ = bf16[64,3072]{1,0:T(8,128)(2,1)S(1)} collective-permute-done((bf16[64,3072]{1,0:T(8,128)(2,1)S(1)}, bf16[64,3072]{1,0:T(8,128)(2,1)S(1)}, u32[]{:S(2)}, u32[]{:S(2)}) %collective-permute-start.30) | collective-permute-done | bytes 393248 | tf_op jit(solution)/shard_map/ppermute | solution.py:491
  167.7 1.6 collective-permute-start.33
  171.3 7.1 %collective-permute-done.33 = bf16[64,3072]{1,0:T(8,128)(2,1)S(1)} collective-permute-done((bf16[64,3072]{1,0:T(8,128)(2,1)S(1)}, bf16[64,3072]{1,0:T(8,128)(2,1)S(1)}, u32[]{:S(2)}, u32[]{:S(2)}) %collective-permute-start.33) | collective-permute-done | bytes 393248 | tf_op jit(solution)/shard_map/ppermute | solution.py:513
  (122 shorter events, 24.8 us)
Async XLA Ops:
  2.8 29.5 %collective-permute-start.5 = (bf16[128,1536]{1,0:T(8,128)(2,1)S(1)}, bf16[128,1536]{1,0:T(8,128)(2,1)}, u32[]{:S(2)}, u32[]{:S(2)}) collective-permute-start(bf16[128,1536]{1,0:T(8,128)(2,1)S(1)} %get-tuple-element.16.refs_0_), channel_id=1, source_target_pairs={{4,0},{8,4},{12,8},{5,1},{9,5},{13,9},{6,2},{10,6},{14,10},{7,3},{... | collective-permute-start | bytes 1179656 | tf_op jit(solution)/shard_map/ppermute | solution.py:425
  4.1 28.2 %collective-permute-start.4 = (bf16[128,1536]{1,0:T(8,128)(2,1)S(1)}, bf16[128,1536]{1,0:T(8,128)(2,1)}, u32[]{:S(2)}, u32[]{:S(2)}) collective-permute-start(bf16[128,1536]{1,0:T(8,128)(2,1)S(1)} %get-tuple-element.16.refs_0_), channel_id=1, source_target_pairs={{0,4},{4,8},{8,12},{1,5},{5,9},{9,13},{2,6},{6,10},{10,14},{3,7},{... | collective-permute-start | bytes 1179656 | tf_op jit(solution)/shard_map/ppermute | solution.py:423
  10.4 1.2 collective-permute-start
  13.5 25.0 %collective-permute-start.3 = (bf16[1552,128]{1,0:T(8,128)(2,1)S(1)}, bf16[1552,128]{1,0:T(8,128)(2,1)}, u32[]{:S(2)}, u32[]{:S(2)}) collective-permute-start(bf16[1552,128]{1,0:T(8,128)(2,1)S(1)} %second_half.1._.refs_1_.refs_4_.refs_5_), channel_id=1, source_target_pairs={{4,0},{8,4},{12,8},{5,1},{9,5},{13,9},{6,2},{10,6},{14,10},{7,3},{... | collective-permute-start | bytes 1191944 | tf_op jit(solution)/shard_map/ppermute | solution.py:425
  14.8 23.7 %collective-permute-start.2 = (bf16[1552,128]{1,0:T(8,128)(2,1)S(1)}, bf16[1552,128]{1,0:T(8,128)(2,1)}, u32[]{:S(2)}, u32[]{:S(2)}) collective-permute-start(bf16[1552,128]{1,0:T(8,128)(2,1)S(1)} %second_half.1._.refs_1_.refs_4_.refs_5_), channel_id=1, source_target_pairs={{0,4},{4,8},{8,12},{1,5},{5,9},{9,13},{2,6},{6,10},{10,14},{3,7},{... | collective-permute-start | bytes 1191944 | tf_op jit(solution)/shard_map/ppermute | solution.py:423
  32.3 6.2 %copy-start.7 = (bf16[128,1536]{1,0:T(8,128)(2,1)}, bf16[128,1536]{1,0:T(8,128)(2,1)S(1)}, u32[]{:S(2)}) copy-start(bf16[128,1536]{1,0:T(8,128)(2,1)S(1)} %project.9.refs_3_.refs_0_.refs_2_) | copy-start | bytes 1179652
  38.5 5.8 %copy-start = (f32[256,3072]{1,0:T(8,128)}, f32[256,3072]{1,0:T(8,128)S(1)}, u32[]{:S(2)}) copy-start(f32[256,3072]{1,0:T(8,128)S(1)} %project.10.refs_2_.refs_4_) | copy-start | bytes 9437188
  44.3 17.5 %collective-permute-start.6 = (bf16[256,1536]{1,0:T(8,128)(2,1)}, bf16[256,1536]{1,0:T(8,128)(2,1)}, u32[]{:S(2)}, u32[]{:S(2)}) collective-permute-start(bf16[256,1536]{1,0:T(8,128)(2,1)} %project.11.refs_4_), channel_id=1, source_target_pairs={{0,1},{1,0},{2,3},{3,2},{4,5},{5,4},{6,7},{7,6},{8,9},{9,8},{10,11... | collective-permute-start | bytes 2359304 | tf_op jit(solution)/shard_map/ppermute | solution.py:470
  44.4 5.7 %collective-permute-start.1 = (bf16[128,1536]{1,0:T(8,128)(2,1)S(1)}, bf16[128,1536]{1,0:T(8,128)(2,1)S(1)}, u32[]{:S(2)}, u32[]{:S(2)}) collective-permute-start(bf16[128,1536]{1,0:T(8,128)(2,1)S(1)} %project.8.refs_3_), channel_id=1, source_target_pairs={{0,1},{1,0},{2,3},{3,2},{4,5},{5,4},{6,7},{7,6},{8,9},{9,8},{10,11... | collective-permute-start | bytes 1179656 | tf_op jit(solution)/shard_map/ppermute | solution.py:470
  44.9 14.2 %collective-permute-start.14 = (bf16[128,1536]{1,0:T(8,128)(2,1)}, bf16[128,1536]{1,0:T(8,128)(2,1)}, u32[]{:S(2)}, u32[]{:S(2)}) collective-permute-start(bf16[128,1536]{1,0:T(8,128)(2,1)} %collective-permute-done.5.refs_1_), channel_id=1, source_target_pairs={{4,0},{8,4},{5,1},{9,5},{6,2},{10,6},{7,3},{11,7},{20,16},{24,20},... | collective-permute-start | bytes 1179656 | tf_op jit(solution)/shard_map/ppermute | solution.py:425
  46.1 14.2 %collective-permute-start.13 = (bf16[128,1536]{1,0:T(8,128)(2,1)}, bf16[128,1536]{1,0:T(8,128)(2,1)}, u32[]{:S(2)}, u32[]{:S(2)}) collective-permute-start(bf16[128,1536]{1,0:T(8,128)(2,1)} %collective-permute-done.4.refs_0_), channel_id=1, source_target_pairs={{4,8},{8,12},{5,9},{9,13},{6,10},{10,14},{7,11},{11,15},{20,24},{2... | collective-permute-start | bytes 1179656 | tf_op jit(solution)/shard_map/ppermute | solution.py:423
  48.7 17.8 %collective-permute-start.10 = (bf16[1552,128]{1,0:T(8,128)(2,1)}, bf16[1552,128]{1,0:T(8,128)(2,1)S(1)}, u32[]{:S(2)}, u32[]{:S(2)}) collective-permute-start(bf16[1552,128]{1,0:T(8,128)(2,1)} %collective-permute-done.3.refs_1_.refs_4_.refs_6_), channel_id=1, source_target_pairs={{4,0},{8,4},{5,1},{9,5},{6,2},{10,6},{7,3},{11,7},{20,16},{24,20},... | collective-permute-start | bytes 1191944 | tf_op jit(solution)/shard_map/ppermute | solution.py:425
  50.8 17.1 %collective-permute-start.9 = (bf16[1552,128]{1,0:T(8,128)(2,1)}, bf16[1552,128]{1,0:T(8,128)(2,1)S(1)}, u32[]{:S(2)}, u32[]{:S(2)}) collective-permute-start(bf16[1552,128]{1,0:T(8,128)(2,1)} %collective-permute-done.2.refs_0_.refs_5_.refs_4_), channel_id=1, source_target_pairs={{4,8},{8,12},{5,9},{9,13},{6,10},{10,14},{7,11},{11,15},{20,24},{2... | collective-permute-start | bytes 1191944 | tf_op jit(solution)/shard_map/ppermute | solution.py:423
  51.9 1.9 %copy-start.1 = (f32[256,3072]{1,0:T(8,128)S(1)}, f32[256,3072]{1,0:T(8,128)}, u32[]{:S(2)}) copy-start(f32[256,3072]{1,0:T(8,128)} %copy-done) | copy-start | bytes 9437188
  53.8 7.9 %copy-start.3 = (bf16[512,256]{1,0:T(8,128)(2,1)S(1)}, bf16[512,256]{1,0:T(8,128)(2,1)}, u32[]{:S(2)}) copy-start(bf16[512,256]{1,0:T(8,128)(2,1)} %constant.44.forward_ref.refs_7_.refs_9_.refs_8_) | copy-start | bytes 786436
  53.8 7.9 %copy-start.8 = (bf16[128,1536]{1,0:T(8,128)(2,1)S(1)}, bf16[128,1536]{1,0:T(8,128)(2,1)}, u32[]{:S(2)}) copy-start(bf16[128,1536]{1,0:T(8,128)(2,1)} %copy-done.7) | copy-start | bytes 1179652
  53.8 7.9 %copy-start.10 = (bf16[256,256]{1,0:T(8,128)(2,1)S(1)}, bf16[256,256]{1,0:T(8,128)(2,1)}, u32[]{:S(2)}) copy-start(bf16[256,256]{1,0:T(8,128)(2,1)} %constant.45.refs_8_.refs_10_.refs_9_) | copy-start | bytes 393220
  53.8 7.9 %copy-start.12 = (bf16[128,1536]{1,0:T(8,128)(2,1)S(1)}, bf16[128,1536]{1,0:T(8,128)(2,1)}, u32[]{:S(2)}) copy-start(bf16[128,1536]{1,0:T(8,128)(2,1)} %copy-done.11) | copy-start | bytes 1179652
  59.0 23.7 %collective-permute-start.16 = (bf16[128,1536]{1,0:T(8,128)(2,1)}, bf16[128,1536]{1,0:T(8,128)(2,1)}, u32[]{:S(2)}, u32[]{:S(2)}) collective-permute-start(bf16[128,1536]{1,0:T(8,128)(2,1)} %collective-permute-done.14.refs_1_), channel_id=1, source_target_pairs={{4,0},{5,1},{6,2},{7,3},{20,16},{21,17},{22,18},{23,19}} | collective-permute-start | bytes 1179656 | tf_op jit(solution)/shard_map/ppermute | solution.py:425
  60.3 22.4 %collective-permute-start.15 = (bf16[128,1536]{1,0:T(8,128)(2,1)}, bf16[128,1536]{1,0:T(8,128)(2,1)}, u32[]{:S(2)}, u32[]{:S(2)}) collective-permute-start(bf16[128,1536]{1,0:T(8,128)(2,1)} %collective-permute-done.13.refs_0_), channel_id=1, source_target_pairs={{8,12},{9,13},{10,14},{11,15},{24,28},{25,29},{26,30},{27,31}} | collective-permute-start | bytes 1179656 | tf_op jit(solution)/shard_map/ppermute | solution.py:423
  64.1 10.3 %collective-permute-start.7 = (bf16[128,512]{1,0:T(8,128)(2,1)S(1)}, bf16[128,512]{1,0:T(8,128)(2,1)}, u32[]{:S(2)}, u32[]{:S(2)}) collective-permute-start(bf16[128,512]{1,0:T(8,128)(2,1)S(1)} %mix.6.refs_9_.mine_ref), channel_id=1, source_target_pairs={{0,1},{1,0},{2,3},{3,2},{4,5},{5,4},{6,7},{7,6},{8,9},{9,8},{10,11... | collective-permute-start | bytes 393224 | tf_op jit(solution)/shard_map/ppermute | solution.py:443
  66.6 22.5 %collective-permute-start.12 = (bf16[1552,128]{1,0:T(8,128)(2,1)S(1)}, bf16[1552,128]{1,0:T(8,128)(2,1)}, u32[]{:S(2)}, u32[]{:S(2)}) collective-permute-start(bf16[1552,128]{1,0:T(8,128)(2,1)S(1)} %collective-permute-done.10.refs_1_.refs_7_.refs_5_.refs_6_), channel_id=1, source_target_pairs={{4,0},{5,1},{6,2},{7,3},{20,16},{21,17},{22,18},{23,19}} | collective-permute-start | bytes 1191944 | tf_op jit(solution)/shard_map/ppermute | solution.py:425
  67.9 21.2 %collective-permute-start.11 = (bf16[1552,128]{1,0:T(8,128)(2,1)S(1)}, bf16[1552,128]{1,0:T(8,128)(2,1)}, u32[]{:S(2)}, u32[]{:S(2)}) collective-permute-start(bf16[1552,128]{1,0:T(8,128)(2,1)S(1)} %collective-permute-done.9.refs_0_.refs_6_.refs_4_.refs_5_), channel_id=1, source_target_pairs={{8,12},{9,13},{10,14},{11,15},{24,28},{25,29},{26,30},{27,31}} | collective-permute-start | bytes 1191944 | tf_op jit(solution)/shard_map/ppermute | solution.py:423
  74.4 4.2 %collective-permute-start.8 = (bf16[128,512]{1,0:T(8,128)(2,1)}, bf16[128,512]{1,0:T(8,128)(2,1)S(1)}, u32[]{:S(2)}, u32[]{:S(2)}) collective-permute-start(bf16[128,512]{1,0:T(8,128)(2,1)} %mix.7._.mine_ref), channel_id=1, source_target_pairs={{0,1},{1,0},{2,3},{3,2},{4,5},{5,4},{6,7},{7,6},{8,9},{9,8},{10,11... | collective-permute-start | bytes 393224 | tf_op jit(solution)/shard_map/ppermute | solution.py:443
  74.4 29.5 %copy-start.20 = (s32[128]{0:T(128)}, s32[128]{0:T(128)S(1)}, u32[]{:S(2)}) copy-start(s32[128]{0:T(128)S(1)} %iota_add_fusion) | copy-start | bytes 1540
  89.0 4.9 %copy-start.17 = (s32[1,64]{1,0:T(1,128)S(1)}, s32[1,64]{1,0:T(1,128)}, u32[]{:S(2)}) copy-start(s32[1,64]{1,0:T(1,128)} %param.17) | copy-start | bytes 772
  89.0 4.9 %copy-start.19 = (s32[128]{0:T(128)S(1)}, s32[128]{0:T(128)}, u32[]{:S(2)}) copy-start(s32[128]{0:T(128)} %iota_add_fusion.4) | copy-start | bytes 1540
  89.0 6.0 %copy-start.22 = (s32[128]{0:T(128)S(1)}, s32[128]{0:T(128)}, u32[]{:S(2)}) copy-start(s32[128]{0:T(128)} %iota_add_fusion.5) | copy-start | bytes 1540
  93.4 6.4 %collective-permute-start.17 = (bf16[256,1536]{1,0:T(8,128)(2,1)S(1)}, bf16[256,1536]{1,0:T(8,128)(2,1)S(1)}, u32[]{:S(2)}, u32[]{:S(2)}) collective-permute-start(bf16[256,1536]{1,0:T(8,128)(2,1)S(1)} %project.14.refs_6_), channel_id=1, source_target_pairs={{0,1},{1,0},{2,3},{3,2},{4,5},{5,4},{6,7},{7,6},{8,9},{9,8},{10,11... | collective-permute-start | bytes 2359304 | tf_op jit(solution)/shard_map/ppermute | solution.py:470
  102.1 2.0 %collective-permute-start.18 = (bf16[128,512]{1,0:T(8,128)(2,1)S(1)}, bf16[128,512]{1,0:T(8,128)(2,1)S(1)}, u32[]{:S(2)}, u32[]{:S(2)}) collective-permute-start(bf16[128,512]{1,0:T(8,128)(2,1)S(1)} %mix.8.refs_11_.mine_ref), channel_id=1, source_target_pairs={{0,1},{1,0},{2,3},{3,2},{4,5},{5,4},{6,7},{7,6},{8,9},{9,8},{10,11... | collective-permute-start | bytes 393224 | tf_op jit(solution)/shard_map/ppermute | solution.py:443
  103.3 15.7 %collective-permute-start.20 = (bf16[128,512]{1,0:T(8,128)(2,1)S(1)}, bf16[128,512]{1,0:T(8,128)(2,1)S(1)}, u32[]{:S(2)}, u32[]{:S(2)}) collective-permute-start(bf16[128,512]{1,0:T(8,128)(2,1)S(1)} %mix.9._.mine_ref), channel_id=1, source_target_pairs={{0,1},{1,0},{2,3},{3,2},{4,5},{5,4},{6,7},{7,6},{8,9},{9,8},{10,11... | collective-permute-start | bytes 393224 | tf_op jit(solution)/shard_map/ppermute | solution.py:443
  107.9 10.9 %copy-start.18 = (s32[128]{0:T(128)S(1)}, s32[128]{0:T(128)}, u32[]{:S(2)}) copy-start(s32[128]{0:T(128)} %iota_add_fusion.2) | copy-start | bytes 1540
  107.9 18.5 %collective-permute-start.21 = (bf16[64,3072]{1,0:T(8,128)(2,1)S(1)}, bf16[64,3072]{1,0:T(8,128)(2,1)S(1)}, u32[]{:S(2)}, u32[]{:S(2)}) collective-permute-start(bf16[64,3072]{1,0:T(8,128)(2,1)S(1)} %get-tuple-element.20.refs_10_), channel_id=1, source_target_pairs={{0,4},{12,8},{1,5},{13,9},{2,6},{14,10},{3,7},{15,11},{16,20},{28,... | collective-permute-start | bytes 1179656 | tf_op jit(solution)/shard_map/ppermute | solution.py:491
  116.9 5.0 %collective-permute-start.19 = (bf16[128,512]{1,0:T(8,128)(2,1)S(1)}, bf16[128,512]{1,0:T(8,128)(2,1)S(1)}, u32[]{:S(2)}, u32[]{:S(2)}) collective-permute-start(bf16[128,512]{1,0:T(8,128)(2,1)S(1)} %mix.10._.mine_ref), channel_id=1, source_target_pairs={{0,1},{1,0},{2,3},{3,2},{4,5},{5,4},{6,7},{7,6},{8,9},{9,8},{10,11... | collective-permute-start | bytes 393224 | tf_op jit(solution)/shard_map/ppermute | solution.py:443
  117.2 16.1 %collective-permute-start.28 = (bf16[64,3072]{1,0:T(8,128)(2,1)S(1)}, bf16[64,3072]{1,0:T(8,128)(2,1)S(1)}, u32[]{:S(2)}, u32[]{:S(2)}) collective-permute-start(bf16[64,3072]{1,0:T(8,128)(2,1)S(1)} %get-tuple-element.27), channel_id=1, source_target_pairs={{0,4},{12,8},{1,5},{13,9},{2,6},{14,10},{3,7},{15,11},{16,20},{28,... | collective-permute-start | bytes 1179656 | tf_op jit(solution)/shard_map/ppermute | solution.py:491
  119.7 2.0 %copy-start.24 = (s32[128]{0:T(128)S(1)}, s32[128]{0:T(128)}, u32[]{:S(2)}) copy-start(s32[128]{0:T(128)} %iota_add_fusion.1) | copy-start | bytes 1540
  121.2 4.5 %collective-permute-start.24 = (bf16[128,512]{1,0:T(8,128)(2,1)S(1)}, bf16[128,512]{1,0:T(8,128)(2,1)S(1)}, u32[]{:S(2)}, u32[]{:S(2)}) collective-permute-start(bf16[128,512]{1,0:T(8,128)(2,1)S(1)} %mix.11._.mine_ref), channel_id=1, source_target_pairs={{0,1},{1,0},{2,3},{3,2},{4,5},{5,4},{6,7},{7,6},{8,9},{9,8},{10,11... | collective-permute-start | bytes 393224 | tf_op jit(solution)/shard_map/ppermute | solution.py:443
  126.5 12.9 %collective-permute-start.25 = (bf16[64,3072]{1,0:T(8,128)(2,1)S(1)}, bf16[64,3072]{1,0:T(8,128)(2,1)S(1)}, u32[]{:S(2)}, u32[]{:S(2)}) collective-permute-start(bf16[64,3072]{1,0:T(8,128)(2,1)S(1)} %get-tuple-element.30), channel_id=1, source_target_pairs={{8,4},{12,8},{9,5},{13,9},{10,6},{14,10},{11,7},{15,11},{24,20},{2... | collective-permute-start | bytes 1179656 | tf_op jit(solution)/shard_map/ppermute | solution.py:491
  127.2 15.5 %collective-permute-start.22 = (bf16[64,3072]{1,0:T(8,128)(2,1)S(1)}, bf16[64,3072]{1,0:T(8,128)(2,1)S(1)}, u32[]{:S(2)}, u32[]{:S(2)}) collective-permute-start(bf16[64,3072]{1,0:T(8,128)(2,1)S(1)} %get-tuple-element.31), channel_id=1, source_target_pairs={{0,4},{4,8},{1,5},{5,9},{2,6},{6,10},{3,7},{7,11},{16,20},{20,24},... | collective-permute-start | bytes 1179656 | tf_op jit(solution)/shard_map/ppermute | solution.py:491
  133.3 26.3 %copy-start.6 = (bf16[1,128,3072]{2,1,0:T(8,128)(2,1)S(1)}, bf16[1,128,3072]{2,1,0:T(8,128)(2,1)}, u32[]{:S(2)}) copy-start(bf16[1,128,3072]{2,1,0:T(8,128)(2,1)} %param.11) | copy-start | bytes 2359300
  133.5 14.5 %collective-permute-start.31 = (bf16[64,3072]{1,0:T(8,128)(2,1)S(1)}, bf16[64,3072]{1,0:T(8,128)(2,1)S(1)}, u32[]{:S(2)}, u32[]{:S(2)}) collective-permute-start(bf16[64,3072]{1,0:T(8,128)(2,1)S(1)} %get-tuple-element.32), channel_id=1, source_target_pairs={{8,4},{12,8},{9,5},{13,9},{10,6},{14,10},{11,7},{15,11},{24,20},{2... | collective-permute-start | bytes 1179656 | tf_op jit(solution)/shard_map/ppermute | solution.py:491
  134.3 16.9 %collective-permute-start.29 = (bf16[64,3072]{1,0:T(8,128)(2,1)S(1)}, bf16[64,3072]{1,0:T(8,128)(2,1)S(1)}, u32[]{:S(2)}, u32[]{:S(2)}) collective-permute-start(bf16[64,3072]{1,0:T(8,128)(2,1)S(1)} %get-tuple-element.33), channel_id=1, source_target_pairs={{0,4},{4,8},{1,5},{5,9},{2,6},{6,10},{3,7},{7,11},{16,20},{20,24},... | collective-permute-start | bytes 1179656 | tf_op jit(solution)/shard_map/ppermute | solution.py:491
  139.6 17.3 %collective-permute-start.26 = (bf16[64,3072]{1,0:T(8,128)(2,1)S(1)}, bf16[64,3072]{1,0:T(8,128)(2,1)S(1)}, u32[]{:S(2)}, u32[]{:S(2)}) collective-permute-start(bf16[64,3072]{1,0:T(8,128)(2,1)S(1)} %add_convert_fusion.2), channel_id=1, source_target_pairs={{4,0},{8,4},{12,8},{5,1},{9,5},{13,9},{6,2},{10,6},{14,10},{7,3},{... | collective-permute-start | bytes 1179656 | tf_op jit(solution)/shard_map/ppermute | solution.py:491
  142.8 16.8 %collective-permute-start.23 = (bf16[64,3072]{1,0:T(8,128)(2,1)S(1)}, bf16[64,3072]{1,0:T(8,128)(2,1)S(1)}, u32[]{:S(2)}, u32[]{:S(2)}) collective-permute-start(bf16[64,3072]{1,0:T(8,128)(2,1)S(1)} %add_convert_fusion.3), channel_id=1, source_target_pairs={{0,4},{4,8},{8,12},{1,5},{5,9},{9,13},{2,6},{6,10},{10,14},{3,7},{... | collective-permute-start | bytes 1179656 | tf_op jit(solution)/shard_map/ppermute | solution.py:491
  148.1 14.6 %collective-permute-start.32 = (bf16[64,3072]{1,0:T(8,128)(2,1)S(1)}, bf16[64,3072]{1,0:T(8,128)(2,1)S(1)}, u32[]{:S(2)}, u32[]{:S(2)}) collective-permute-start(bf16[64,3072]{1,0:T(8,128)(2,1)S(1)} %add_convert_fusion), channel_id=1, source_target_pairs={{4,0},{8,4},{12,8},{5,1},{9,5},{13,9},{6,2},{10,6},{14,10},{7,3},{... | collective-permute-start | bytes 1179656 | tf_op jit(solution)/shard_map/ppermute | solution.py:491
  151.3 16.3 %collective-permute-start.30 = (bf16[64,3072]{1,0:T(8,128)(2,1)S(1)}, bf16[64,3072]{1,0:T(8,128)(2,1)S(1)}, u32[]{:S(2)}, u32[]{:S(2)}) collective-permute-start(bf16[64,3072]{1,0:T(8,128)(2,1)S(1)} %add_convert_fusion.1), channel_id=1, source_target_pairs={{0,4},{4,8},{8,12},{1,5},{5,9},{9,13},{2,6},{6,10},{10,14},{3,7},{... | collective-permute-start | bytes 1179656 | tf_op jit(solution)/shard_map/ppermute | solution.py:491
  159.8 11.5 %collective-permute-start.27 = (bf16[64,3072]{1,0:T(8,128)(2,1)S(1)}, bf16[64,3072]{1,0:T(8,128)(2,1)S(1)}, u32[]{:S(2)}, u32[]{:S(2)}) collective-permute-start(bf16[64,3072]{1,0:T(8,128)(2,1)S(1)} %finish.2), channel_id=1, source_target_pairs={{0,2},{2,0},{1,3},{3,1},{4,6},{6,4},{5,7},{7,5},{8,10},{10,8},{9,1... | collective-permute-start | bytes 1179656 | tf_op jit(solution)/shard_map/ppermute | solution.py:513
  167.7 10.7 %collective-permute-start.33 = (bf16[64,3072]{1,0:T(8,128)(2,1)S(1)}, bf16[64,3072]{1,0:T(8,128)(2,1)S(1)}, u32[]{:S(2)}, u32[]{:S(2)}) collective-permute-start(bf16[64,3072]{1,0:T(8,128)(2,1)S(1)} %finish.3), channel_id=1, source_target_pairs={{0,2},{2,0},{1,3},{3,1},{4,6},{6,4},{5,7},{7,5},{8,10},{10,8},{9,1... | collective-permute-start | bytes 1179656 | tf_op jit(solution)/shard_map/ppermute | solution.py:513
  (11 other events, 11.7 us)

commit v4 on v3

v4 whole, which is shorter than its diff:
```python
import functools

import jax
import jax.numpy as jnp
import ml_dtypes
import numpy as np
from jax import lax
from jax.experimental import pallas as pl
from jax.experimental.pallas import tpu as pltpu
from jax.sharding import PartitionSpec as P


norm_eps = 1e-06
lanes = 128
stat_rows = 16
halves = 2
mebibyte = 1024 * 1024


def tile_of(extent, most):
    tile = min(extent, most)
    while extent % tile:
        tile //= 2
    return tile


def block_of(slot, z):
    kind, k = slot[:2]
    below = z - k
    return z + k if kind == "d" else jnp.where(z == 0, k, below) if kind == "m" else below


def params(grant=8):
    return pltpu.CompilerParams(vmem_limit_bytes=grant * mebibyte)


def vmem(count):
    return [pl.BlockSpec(memory_space=pltpu.VMEM)] * count


def hbm():
    return [pl.BlockSpec(memory_space=pltpu.HBM)]


def order_only():
    return [pl.BlockSpec(memory_space=pl.ANY)]


def smem():
    return [pl.BlockSpec(memory_space=pltpu.SMEM)]


def prepare_kernel(x_hbm, gain_hbm, out_ref, x_ref, gain_ref, arrived):
    copies = [
        pltpu.make_async_copy(x_hbm, x_ref, arrived.at[0]),
        pltpu.make_async_copy(gain_hbm, gain_ref, arrived.at[1]),
    ]
    for copy in copies:
        copy.start()
    for copy in copies:
        copy.wait()
    rows, width = x_ref.shape
    total = jnp.zeros((rows, lanes), jnp.float32)
    for tile in range(width // lanes):
        place = slice(tile * lanes, (tile + 1) * lanes)
        x = x_ref[:, place].astype(jnp.float32)
        out_ref[tile * rows : (tile + 1) * rows, :] = (x * gain_ref[:, place]).astype(jnp.bfloat16)
        total = total + x * x
    total = jnp.transpose(jnp.broadcast_to(jnp.sum(total, axis=1, keepdims=True), (rows, lanes)))
    total = jnp.broadcast_to(total[:1, :], (stat_rows, rows))
    high = total.astype(jnp.bfloat16).astype(jnp.float32)
    row = lax.broadcasted_iota(jnp.int32, (stat_rows, rows), 0)
    both = jnp.where(row == 0, high, jnp.where(row == 1, total - high, 0.0))
    out_ref[rows * (width // lanes) :, :] = both.astype(jnp.bfloat16)


def prepare(x, gain):
    rows, width = x.shape
    return pl.pallas_call(
        prepare_kernel,
        in_specs=hbm() * 2,
        out_specs=vmem(1)[0],
        out_shape=jax.ShapeDtypeStruct((rows * (width // lanes) + stat_rows, lanes), jnp.bfloat16),
        scratch_shapes=[
            pltpu.VMEM(x.shape, x.dtype),
            pltpu.VMEM(gain.shape, gain.dtype),
            pltpu.SemaphoreType.DMA((2,)),
        ],
        compiler_params=params(),
        name="prepare",
    )(x, gain)


def project_kernel(layout, side, info_ref, *refs):
    x_refs = refs[: sum(layout)]
    w_hbm, _, out_ref, joined, w_ref, arrived = refs[sum(layout) :]
    depth = joined.shape[1]
    rows = joined.shape[0] // len(layout)
    streams, _, channels = w_hbm.shape
    half = channels // 2

    def weights(stream):
        place = pl.ds(pl.multiple_of(info_ref[side] * half, half), half)
        return pltpu.make_async_copy(w_hbm.at[stream, :, place], w_ref.at[stream], arrived.at[stream])

    @pl.loop(0, streams)
    def _(stream):
        weights(stream).start()

    source = 0
    for index, inputs in enumerate(layout):
        group = x_refs[source : source + inputs]
        source += inputs

        def total(place):
            x = group[0][place, :]
            for other in group[1:]:
                x = x + other[place, :]
            return x

        here = slice(index * rows, (index + 1) * rows)
        for tile in range(depth // lanes):
            joined[here, tile * lanes : (tile + 1) * lanes] = total(slice(tile * rows, (tile + 1) * rows))
        below = joined.shape[0] + index * stat_rows
        last = rows * (depth // lanes)
        out_ref[below : below + stat_rows, :lanes] = total(slice(last, last + stat_rows))

    @pl.loop(0, streams)
    def _(stream):
        weights(stream).wait()
        value = jnp.dot(joined[...], w_ref[stream], preferred_element_type=jnp.float32)
        place = pl.ds(pl.multiple_of(stream * half, half), half)
        out_ref[: joined.shape[0], place] = value.astype(out_ref.dtype)


def project(pieces, layout, rows, w, side, info, after):
    streams, depth, channels = w.shape
    total_rows = rows * len(layout)
    half = channels // 2
    return pl.pallas_call(
        functools.partial(project_kernel, layout, side),
        in_specs=smem() + vmem(len(pieces)) + hbm() + order_only(),
        out_specs=vmem(1)[0],
        out_shape=jax.ShapeDtypeStruct((total_rows + stat_rows * len(layout), streams * half), jnp.bfloat16),
        scratch_shapes=[
            pltpu.VMEM((total_rows, depth), jnp.bfloat16),
            pltpu.VMEM((streams, depth, half), jnp.bfloat16),
            pltpu.SemaphoreType.DMA((streams,)),
        ],
        compiler_params=params(46),
        cost_estimate=pl.CostEstimate(
            flops=2 * total_rows * depth * streams * half,
            bytes_accessed=2 * depth * streams * half,
            transcendentals=0,
        ),
        name="project",
    )(info, *pieces, w, after)


def wave_tables(rows):
    window = 2 * rows
    angle = np.pi / window * (2 * np.arange(rows)[:, None] + 1) * np.arange(window)[None, :]
    forward = np.concatenate([np.cos(angle), np.sin(angle)], axis=0)
    inverse = forward[:, rows:].T * (2.0 / window)

    def pair(matrix):
        exact = jnp.asarray(matrix, jnp.float32)
        high = jnp.asarray(np.asarray(matrix, ml_dtypes.bfloat16))
        low = jnp.asarray(np.asarray(matrix - np.asarray(matrix, ml_dtypes.bfloat16).astype(np.float64), ml_dtypes.bfloat16))
        return high, low

    high, low = pair(forward)
    inverse_high, inverse_low = pair(inverse)
    return jnp.concatenate([high, low], axis=0), jnp.concatenate([inverse_high, inverse_low], axis=0)


def spectrum_kernel(taps_ref, forward_ref, _, out_ref):
    taps = taps_ref.shape[1]
    both = lax.dot_general(
        forward_ref[:, :taps], taps_ref[...], (((1,), (1,)), ((), ())), preferred_element_type=jnp.float32
    )
    half = out_ref.shape[0]
    out_ref[...] = both[:half, :] + both[half:, :]


def spectrum(taps, forward, after):
    return pl.pallas_call(
        spectrum_kernel,
        in_specs=vmem(2) + order_only(),
        out_specs=vmem(1)[0],
        out_shape=jax.ShapeDtypeStruct((forward.shape[1], taps.shape[0]), jnp.float32),
        compiler_params=params(),
        name="spectrum",
    )(taps, forward, after)


def mix_kernel(slot, at, before_at, full_width, info_ref, *refs):
    own, got, own_before, got_before, f_ref, forward_ref, inverse_ref, _, out_ref, window = refs
    rows, half = out_ref.shape
    block = block_of(slot, info_ref[2])
    length = info_ref[3]
    work = (block >= 0) & (block < slot[2])
    tile = tile_of(half, 256)

    def scale_of(own_ref, got_ref, at):
        blocks = own_ref.shape[0] // (rows + stat_rows)
        below = blocks * rows + at * stat_rows
        total = jnp.zeros((1, rows), jnp.float32)
        for ref in (own_ref, got_ref):
            pair = ref[below : below + stat_rows, :lanes].astype(jnp.float32)
            total = total + (pair[:1, :] + pair[1:2, :])
        total = jnp.transpose(jnp.broadcast_to(total, (lanes, rows)))
        scale = lax.rsqrt(total / full_width + norm_eps)
        return jnp.concatenate([scale] * (tile // lanes), axis=1)

    def joined(a_ref, b_ref, at, stream, column):
        place = (slice(at * rows, (at + 1) * rows), slice(stream * half + column, stream * half + column + tile))
        return a_ref[place].astype(jnp.float32) + b_ref[place].astype(jnp.float32)

    @pl.when(work)
    def _():
        row = lax.broadcasted_iota(jnp.int32, (rows, 1), 0)
        scale = scale_of(own, got, at)
        live = (row + block * rows < length).astype(jnp.float32)
        for column in range(0, half, tile):
            here = joined(own, got, at, 1, column) * scale * (joined(own, got, at, 2, column) * scale) * live
            window[rows:, column : column + tile] = here.astype(jnp.bfloat16)

        @pl.when(block > 0)
        def _():
            scale = scale_of(own_before, got_before, before_at)
            live = (row + (block - 1) * rows < length).astype(jnp.float32)
            for column in range(0, half, tile):
                key = joined(own_before, got_before, before_at, 1, column) * scale
                value = joined(own_before, got_before, before_at, 2, column) * scale
                window[:rows, column : column + tile] = (key * value * live).astype(jnp.bfloat16)

        @pl.when(block == 0)
        def _():
            window[:rows, :] = jnp.zeros((rows, half), jnp.bfloat16)

        for column in range(0, half, tile):
            place = slice(column, column + tile)
            both = jnp.dot(forward_ref[...], window[:, place], preferred_element_type=jnp.float32)
            cosine = both[:rows, :] + both[2 * rows : 3 * rows, :]
            sine = both[rows : 2 * rows, :] + both[3 * rows :, :]
            channel = pl.ds(pl.multiple_of(info_ref[0] * half + column, tile), tile)
            f_cosine = f_ref[:rows, channel]
            f_sine = f_ref[rows:, channel]
            product = jnp.concatenate(
                [cosine * f_cosine - sine * f_sine, cosine * f_sine + sine * f_cosine], axis=0
            )
            high = product.astype(jnp.bfloat16)
            low = (product - high.astype(jnp.float32)).astype(jnp.bfloat16)
            back = jnp.dot(inverse_ref[...], high, preferred_element_type=jnp.float32)
            conv = back[:rows, :] + back[rows:, :]
            conv = conv + jnp.dot(inverse_ref[:rows, :], low, preferred_element_type=jnp.float32)
            out_ref[:, place] = (joined(own, got, at, 0, column) * scale * conv * live).astype(jnp.bfloat16)

    @pl.when(jnp.logical_not(work))
    def _():
        out_ref[...] = jnp.zeros_like(out_ref)


def mix(slot, here, before, rows, waves, filter_waves, full_width, info, after):
    own, got, at = here
    own_before, got_before, before_at = before
    half = filter_waves.shape[1] // 2
    return pl.pallas_call(
        functools.partial(mix_kernel, slot, at, before_at, full_width),
        in_specs=smem() + vmem(7) + order_only(),
        out_specs=vmem(1)[0],
        out_shape=jax.ShapeDtypeStruct((rows, half), jnp.bfloat16),
        scratch_shapes=[pltpu.VMEM((2 * rows, half), jnp.bfloat16)],
        compiler_params=params(),
        cost_estimate=pl.CostEstimate(
            flops=16 * rows * rows * half, bytes_accessed=32 * rows * half, transcendentals=0
        ),
        name="mix",
    )(info, own, got, own_before, got_before, filter_waves, *waves, after)


def emit_kernel(slot, info_ref, mine_ref, theirs_ref, w_hbm, _, *refs):
    *out_refs, w_ref, arrived = refs
    block = block_of(slot, info_ref[2])
    work = (block >= 0) & (block < slot[2])
    chunk, width = out_refs[0].shape
    half = mine_ref.shape[1]
    tile = tile_of(width, 512)

    @pl.when(work)
    def _():
        mine = pl.ds(pl.multiple_of(info_ref[0] * half, half), half)
        theirs = pl.ds(pl.multiple_of(info_ref[1] * half, half), half)

        def weights(index):
            place = pl.ds(pl.multiple_of(index * tile, tile), tile)
            return pltpu.make_async_copy(w_hbm.at[:, place], w_ref.at[index], arrived.at[index])

        @pl.loop(0, width // tile)
        def _(index):
            weights(index).start()

        @pl.loop(0, width // tile)
        def _(index):
            weights(index).wait()
            product = jnp.dot(mine_ref[...], w_ref[index, mine, :], preferred_element_type=jnp.float32)
            product = product + jnp.dot(theirs_ref[...], w_ref[index, theirs, :], preferred_element_type=jnp.float32)
            product = product.astype(jnp.bfloat16)
            place = pl.ds(pl.multiple_of(index * tile, tile), tile)
            for part, out_ref in enumerate(out_refs):
                out_ref[:, place] = product[part * chunk : (part + 1) * chunk, :]

    @pl.when(jnp.logical_not(work))
    def _():
        for out_ref in out_refs:
            out_ref[...] = jnp.zeros_like(out_ref)


def emit(slot, mine, theirs, w, info, after):
    rows, half = mine.shape
    width = w.shape[1]
    chunk = rows // halves
    return pl.pallas_call(
        functools.partial(emit_kernel, slot),
        in_specs=smem() + vmem(2) + hbm() + order_only(),
        out_specs=vmem(halves),
        out_shape=[jax.ShapeDtypeStruct((chunk, width), jnp.bfloat16)] * halves,
        scratch_shapes=[
            pltpu.VMEM((width // tile_of(width, 512), w.shape[0], tile_of(width, 512)), jnp.bfloat16),
            pltpu.SemaphoreType.DMA((width // tile_of(width, 512),)),
        ],
        compiler_params=params(50),
        cost_estimate=pl.CostEstimate(
            flops=4 * rows * half * width, bytes_accessed=4 * half * width, transcendentals=0
        ),
        name="emit",
    )(info, mine, theirs, w, after)


def finish_kernel(index, x_ref, *refs):
    chunk = refs[-1].shape[0]
    total = x_ref[index * chunk : (index + 1) * chunk, :].astype(jnp.float32)
    for ref in refs[:-1]:
        total = total + ref[...].astype(jnp.float32)
    refs[-1][...] = total.astype(jnp.bfloat16)


def finish(x, index, terms):
    chunk, width = terms[0].shape
    return pl.pallas_call(
        functools.partial(finish_kernel, index),
        in_specs=vmem(1 + len(terms)),
        out_specs=vmem(1)[0],
        out_shape=jax.ShapeDtypeStruct((chunk, width), jnp.bfloat16),
        compiler_params=params(),
        cost_estimate=pl.CostEstimate(
            flops=chunk * width * len(terms), bytes_accessed=2 * chunk * width * (len(terms) + 2), transcendentals=0
        ),
        name="finish",
    )(x, *terms)


def readout_kernel(slots, info_ref, needle_ref, *refs):
    *refs, _, out_ref = refs
    rows, half = refs[0].shape
    row = lax.broadcasted_iota(jnp.int32, (rows, needle_ref.shape[1]), 0)
    totals = [jnp.zeros((needle_ref.shape[1], half), jnp.float32)] * 2
    for index, slot in enumerate(slots):
        chosen = row + block_of(slot, info_ref[2]) * rows == needle_ref[...]
        chosen = jnp.transpose(chosen.astype(jnp.float32)).astype(jnp.bfloat16)
        for side in range(2):
            part = refs[2 * index + side][...]
            totals[side] += jnp.dot(chosen, part, preferred_element_type=jnp.float32)
    for side in range(2):
        place = pl.ds(pl.multiple_of(info_ref[side] * half, half), half)
        out_ref[:, place] = totals[side].astype(jnp.bfloat16)


def readout(gated, needles, info, after):
    slots = list(gated)
    parts = [part for slot in slots for part in gated[slot]]
    half = parts[0].shape[1]
    return pl.pallas_call(
        functools.partial(readout_kernel, slots),
        in_specs=smem() + vmem(1 + len(parts)) + order_only(),
        out_specs=vmem(1)[0],
        out_shape=jax.ShapeDtypeStruct((needles.shape[1], 2 * half), jnp.bfloat16),
        compiler_params=params(),
        cost_estimate=pl.CostEstimate(
            flops=2 * needles.shape[1] * parts[0].shape[0] * half * len(parts), bytes_accessed=0, transcendentals=0
        ),
        name="readout",
    )(info, needles, *parts, after)


def added(*terms):
    total = terms[0].astype(jnp.float32)
    for term in terms[1:]:
        total = total + term.astype(jnp.float32)
    return total.astype(jnp.bfloat16)


def layer(spans, norm_gain, w_in, filters, w_out, prompt_len, needles):
    count = lax.axis_size("ctx")
    place = lax.axis_index("ctx")
    x_local = spans[0]
    rows, half_width = x_local.shape
    full_width = half_width * lax.axis_size("mp")
    weights = jnp.swapaxes(w_in[0], 0, 1)
    up = [(source, source + 1) for source in range(count - 1)]
    down = [(source + 1, source) for source in range(count - 1)]
    partner = [(0, 1), (1, 0)] if lax.axis_size("mp") == 2 else None

    far = count - 1
    z = place.astype(jnp.int32)

    core = lax.axis_index("mp").astype(jnp.int32)
    info = jnp.concatenate([jnp.stack([core, 1 - core, z]), prompt_len])
    waves = wave_tables(rows)
    piece = prepare(x_local, norm_gain)
    gathered = {("d", 0): piece, ("u", 0): piece}
    for k in range(1, count):
        to_up = [(a, b) for a, b in up if a >= k - 1]
        gathered["u", k] = lax.ppermute(gathered["u", k - 1], "ctx", to_up)
        to_down = [(a, b) for a, b in down if a <= count - k]
        gathered["d", k] = lax.ppermute(gathered["d", k - 1], "ctx", to_down)

    held = {}
    gated = {}
    sums = {}

    def combine(kind, k, after):
        before = ("u", k + 1) if kind == "u" or k == 0 else ("d", k - 1)
        mine = mix(
            (kind, k, count), held["d" if kind == "m" else kind, k], held[before],
            rows, waves, filter_waves, full_width, info, after,
        )
        gated[kind, k] = (mine, lax.ppermute(mine, "mp", partner))
        return mine

    def spread(kind, k, after):
        sums[kind, k] = emit((kind, k, count), *gated[kind, k], w_out[0], info, after)
        return sums[kind, k][0]

    filter_waves = spectrum(filters[0], waves[0], piece)
    after = filter_waves
    for k in range(count):
        kinds = ("d",) if k == 0 else ("ud",) if 2 * k >= count else ("u", "d")
        layout = [len(kind) for kind in kinds]
        inputs = [gathered[way, k] for kind in kinds for way in kind]
        theirs = project(inputs, layout, rows, weights, 1, info, after)
        got = lax.ppermute(theirs, "mp", partner)
        after = project(inputs, layout, rows, weights, 0, info, theirs)
        for index, kind in enumerate(kinds):
            for way in kind:
                held[way, k] = (after, got, index)
        if k == 0:
            held["u", 0] = held["d", 0]
        if count > 2 and k == 1:
            for slot in (("d", 0), ("d", 1)):
                after = combine(*slot, after)
        if count > 2 and k == 2:
            for slot in (("d", 0), ("d", 1)):
                after = spread(*slot, after)
    rest = [slot for slot in [("m", far)] + [(kind, k) for k in range(far - 1, 0, -1) for kind in "ud"] + [("d", 0)]]
    rest = [slot for slot in rest if slot not in sums]
    after = combine(*rest[0], after)
    for index, slot in enumerate(rest):
        if index + 1 < len(rest):
            after = combine(*rest[index + 1], after)
        after = spread(*slot, after)

    def reduce_step(values, pairs):
        moved = []
        for value in values:
            moved.append(lax.ppermute(value, "ctx", pairs))
        return moved

    terms = [sums["d", 0]]
    for k in range(far, 0, -1):
        to_up = [(a, b) for a, b in up if a + k <= far]
        to_down = [(a, b) for a, b in down if a >= k]
        if k == far and far != 2:
            arrived = [reduce_step(sums["m", far], to_up + to_down)] * 2
        else:
            from_up, from_down = ("m", "m") if k == far else ("d", "u")
            arrived = [reduce_step(sums[from_up, k], to_up), reduce_step(sums[from_down, k], to_down)]
        if k > 1:
            for kind, moved in zip("du", arrived):
                sums[kind, k - 1] = [added(a, b) for a, b in zip(sums[kind, k - 1], moved)]
        else:
            terms += arrived if far > 1 else arrived[:1]
    sections = lax.axis_size("section")
    turn = [(source, (source + 1) % sections) for source in range(sections)]
    advanced = []
    for i in range(halves):
        final = finish(x_local, i, [term[i] for term in terms])
        advanced.append(lax.ppermute(final, "section", turn))
    advanced = jnp.concatenate(advanced, axis=0)[None]

    picked = readout(gated, needles, info, after)
    return (advanced, picked[None])


def solution(mesh):
    return jax.shard_map(
        layer,
        mesh=mesh,
        in_specs=(
            P("section", ("groups", "ctx"), "mp"),
            P("section", "mp"),
            P("section", "mp", None, "ctx"),
            P("section", "ctx", None),
            P("section", "ctx", "mp"),
            P(("groups", "section")),
            P("section", "groups"),
        ),
        out_specs=(P("section", ("groups", "ctx"), "mp"), P("section", "groups", "ctx")),
        check_vma=False,
    )
```

time: 181 us -> 160 us (0.88)
  waiting for transfers between devices: 22.3 us -> 44.9 us
  starting transfers between devices: 63.4 us -> 41 us
  local copies, waits for them, and re-layouts: 10.3 us -> 1.91 us
  Pallas kernels: 72 us -> 67.7 us
  matrix products: 4.29 us -> 0 us
  other arithmetic: 5.06 us -> 1.73 us
    ppermute x13 -> x6, waiting for transfers between devices: 2.61 us -> 20.1 us  [the longest x3 10.7 us: layer(): gathered['d', k] = lax.ppermute(gathered['d', k - 1], 'ctx', to_down)]
    ppermute x13 -> x6, starting transfers between devices: 24.3 us -> 10.3 us  [the longest x3 6.41 us: layer(): gathered['u', k] = lax.ppermute(gathered['u', k - 1], 'ctx', to_up)]
    ppermute x10, starting transfers between devices: 33.8 us -> 24.5 us  [reduce_step(): moved.append(lax.ppermute(value, 'ctx', pairs))]
    unnamed x50 -> x14, local copies, waits for them, and re-layouts: 10.3 us -> 1.91 us
    ppermute x10, waiting for transfers between devices: 12.5 us -> 17.1 us  [reduce_step(): moved.append(lax.ppermute(value, 'ctx', pairs))]
    dot_general x12 -> x0, matrix products: 4.29 us -> none  [layer(): picked[index] += jnp.dot(one_hot, part, preferred_element_type=jnp.float32)]
    pallas_call x16, Pallas kernels: 54 us -> 50.4 us  [the longest x8 40.3 us: project(): pl.pallas_call(functools.partial(project_kernel, layout, side), in_specs=...]
    add x6 -> x0, other arithmetic: 2.68 us -> none  [layer(): row + block_of(slot, z) * rows]
  transfers between devices with their start and end apart: 34 -> 28, of which waited for: 9 -> 11; matrix products, arithmetic and copies ran while one was open for 5% -> 0% of each run, Pallas kernels for 33% -> 41%
where the time goes in v4:
time: 160 us; the launch traced here: 159 us
  Pallas kernels  67.7 us (42%)
  waiting for transfers between devices  44.9 us (28%)
  starting transfers between devices  41 us (26%)
  local copies, waits for them, and re-layouts  1.91 us (1%)
  between operations  1.82 us (1%)
  other arithmetic  1.73 us (1%)
    pallas_call x8, Pallas kernels, project(): pl.pallas_call(functools.partial(project_kernel, layout, side), in_specs=...  40.3 us
    ppermute x10, starting transfers between devices, reduce_step(): moved.append(lax.ppermute(value, 'ctx', pairs))  24.5 us
    ppermute x10, waiting for transfers between devices, reduce_step(): moved.append(lax.ppermute(value, 'ctx', pairs))  17.1 us
    pallas_call x6, Pallas kernels, emit(): pl.pallas_call(functools.partial(emit_kernel, slot), in_specs=smem() + vm...  16.4 us
    ppermute x3, waiting for transfers between devices, layer(): gathered['d', k] = lax.ppermute(gathered['d', k - 1], 'ctx', to_down)  10.7 us
    ppermute x3, waiting for transfers between devices, layer(): gathered['u', k] = lax.ppermute(gathered['u', k - 1], 'ctx', to_up)  9.42 us
    pallas_call x6, Pallas kernels, mix(): pl.pallas_call(functools.partial(mix_kernel, slot, at, before_at, full_wi...  8.07 us
    ppermute x2, waiting for transfers between devices, layer(): advanced.append(lax.ppermute(final, 'section', turn))  7.37 us
  transfers between devices with their start and end apart: 28, of which 11 were waited for; matrix products, arithmetic and copies ran while one was open for 0% of the time, Pallas kernels for 41%

profile of v4, /device:TPU:0, one launch (start us, length us, event | category | flops | bytes accessed | tf_op | source)
XLA Modules:
  0.0 159.0 jit_solution(14191670828358402892)
XLA Ops:
  0.7 1.2 copy-done.1
  1.8 0.7 copy-done.5
  3.0 5.0 %collective-permute-start.1 = (bf16[3088,128]{1,0:T(8,128)(2,1)S(1)}, bf16[3088,128]{1,0:T(8,128)(2,1)S(1)}, u32[]{:S(2)}, u32[]{:S(2)}) collective-permute-start(bf16[3088,128]{1,0:T(8,128)(2,1)S(1)} %prepare.1._.refs_0_), channel_id=1, source_target_pairs={{0,4},{4,8},{8,12},{1,5},{5,9},{9,13},{2,6},{6,10},{10,14},{3,7},{... | collective-permute-start | bytes 2371592 | tf_op jit(solution)/shard_map/ppermute | solution.py:425
  8.0 1.3 collective-permute-start.2
  10.5 4.9 %project.8.refs_2_ = bf16[144,1536]{1,0:T(8,128)(2,1)S(1)} custom-call(s32[4]{0:T(128)S(1)} %pad_add_fusion.info_ref, bf16[3088,128]{1,0:T(8,128)(2,1)S(1)} %prepare.1._.refs_0_, bf16[3,3072,1024]{2,1,0:T(8,128)(2,1)} %bitcast.16, f32[256,1024]{1,0:T(8,128)S(1)} %spectrum.1.refs_2_.refs_4_), custom_call_target="tpu_custom_call" | custom-call | flops 1207959552 | bytes 9437184 | tf_op jit(solution)/shard_map/project/pallas_call | solution.py:140
  15.4 9.4 %collective-permute-done.1.refs_0_ = bf16[3088,128]{1,0:T(8,128)(2,1)S(1)} collective-permute-done((bf16[3088,128]{1,0:T(8,128)(2,1)S(1)}, bf16[3088,128]{1,0:T(8,128)(2,1)S(1)}, u32[]{:S(2)}, u32[]{:S(2)}) %collective-permute-start.1) | collective-permute-done | bytes 790560 | tf_op jit(solution)/shard_map/ppermute | solution.py:425
  24.8 0.7 collective-permute-start.5
  25.5 3.5 %collective-permute-done.2.refs_1_ = bf16[3088,128]{1,0:T(8,128)(2,1)S(1)} collective-permute-done((bf16[3088,128]{1,0:T(8,128)(2,1)S(1)}, bf16[3088,128]{1,0:T(8,128)(2,1)S(1)}, u32[]{:S(2)}, u32[]{:S(2)}) %collective-permute-start.2) | collective-permute-done | bytes 790560 | tf_op jit(solution)/shard_map/ppermute | solution.py:427
  29.0 1.3 collective-permute-start.6
  30.3 4.9 %project.9.refs_3_.refs_0_.refs_2_ = bf16[144,1536]{1,0:T(8,128)(2,1)S(1)} custom-call(s32[4]{0:T(128)S(1)} %pad_add_fusion.info_ref, bf16[3088,128]{1,0:T(8,128)(2,1)S(1)} %prepare.1._.refs_0_, bf16[3,3072,1024]{2,1,0:T(8,128)(2,1)} %bitcast.17, bf16[144,1536]{1,0:T(8,128)(2,1)S(1)} %project.8.refs_2_), custom_call_target="tpu_custom_call" | custom-call | flops 1207959552 | bytes 9437184 | tf_op jit(solution)/shard_map/project/pallas_call | solution.py:140
  35.2 5.5 %project.10.refs_3_ = bf16[288,1536]{1,0:T(8,128)(2,1)S(1)} custom-call(s32[4]{0:T(128)S(1)} %pad_add_fusion.info_ref, bf16[3088,128]{1,0:T(8,128)(2,1)S(1)} %collective-permute-done.1.refs_0_, bf16[3088,128]{1,0:T(8,128)(2,1)S(1)} %collective-permute-done.2.refs_1_, bf16[3,3072,1024]{2,1,0:T(8,128)(2,1)} %bitcast.18, ...), custom_call_target="tpu_custom_call" | custom-call | flops 2415919104 | bytes 9437184 | tf_op jit(solution)/shard_map/project/pallas_call | solution.py:140
  41.2 0.7 collective-permute-start.9
  42.0 7.3 %collective-permute-done.6.refs_1_ = bf16[3088,128]{1,0:T(8,128)(2,1)S(1)} collective-permute-done((bf16[3088,128]{1,0:T(8,128)(2,1)S(1)}, bf16[3088,128]{1,0:T(8,128)(2,1)S(1)}, u32[]{:S(2)}, u32[]{:S(2)}) %collective-permute-start.6) | collective-permute-done | bytes 790560 | tf_op jit(solution)/shard_map/ppermute | solution.py:427
  49.2 1.3 collective-permute-start.10
  50.5 5.4 %project.11.refs_2_.refs_7_.refs_0_ = bf16[288,1536]{1,0:T(8,128)(2,1)S(1)} custom-call(s32[4]{0:T(128)S(1)} %pad_add_fusion.info_ref, bf16[3088,128]{1,0:T(8,128)(2,1)S(1)} %collective-permute-done.1.refs_0_, bf16[3088,128]{1,0:T(8,128)(2,1)S(1)} %collective-permute-done.2.refs_1_, bf16[3,3072,1024]{2,1,0:T(8,128)(2,1)} %bitcast.19, ...), custom_call_target="tpu_custom_call" | custom-call | flops 2415919104 | bytes 9437184 | tf_op jit(solution)/shard_map/project/pallas_call | solution.py:140
  56.0 1.6 %mix.6.refs_7_.mine_ref.refs_0_ = bf16[128,512]{1,0:T(8,128)(2,1)S(1)} custom-call(s32[4]{0:T(128)S(1)} %pad_add_fusion.info_ref, bf16[144,1536]{1,0:T(8,128)(2,1)S(1)} %project.9.refs_3_.refs_0_.refs_2_, bf16[144,1536]{1,0:T(8,128)(2,1)S(1)} %collective-permute-done.refs_1_.refs_3_, bf16[288,1536]{1,0:T(8,128)(2,1)S(1)} %project.11.refs_2_.refs_7_.refs_0_, ...), custom_call_target="tpu_custom_call" | custom-call | flops 134217728 | bytes 2097152 | tf_op jit(solution)/shard_map/mix/pallas_call | solution.py:269
  57.7 1.7 %mix.7.refs_3_.mine_ref.refs_2_ = bf16[128,512]{1,0:T(8,128)(2,1)S(1)} custom-call(s32[4]{0:T(128)S(1)} %pad_add_fusion.info_ref, bf16[288,1536]{1,0:T(8,128)(2,1)S(1)} %project.11.refs_2_.refs_7_.refs_0_, bf16[288,1536]{1,0:T(8,128)(2,1)S(1)} %collective-permute-done.3.refs_3_.refs_1_, bf16[144,1536]{1,0:T(8,128)(2,1)S(1)} %project.9.refs_3_.refs_0_.refs_2_, ...), custom_call_target="tpu_custom_call" | custom-call | flops 134217728 | bytes 2097152 | tf_op jit(solution)/shard_map/mix/pallas_call | solution.py:269
  60.0 4.9 %project.12.refs_3_ = bf16[144,1536]{1,0:T(8,128)(2,1)S(1)} custom-call(s32[4]{0:T(128)S(1)} %pad_add_fusion.info_ref, bf16[3088,128]{1,0:T(8,128)(2,1)S(1)} %collective-permute-done.5.refs_0_, bf16[3088,128]{1,0:T(8,128)(2,1)S(1)} %collective-permute-done.6.refs_1_, bf16[3,3072,1024]{2,1,0:T(8,128)(2,1)} %bitcast.20, ...), custom_call_target="tpu_custom_call" | custom-call | flops 1207959552 | bytes 9437184 | tf_op jit(solution)/shard_map/project/pallas_call | solution.py:140
  65.0 4.9 %project.13._.refs_2_.refs_0_ = bf16[144,1536]{1,0:T(8,128)(2,1)S(1)} custom-call(s32[4]{0:T(128)S(1)} %pad_add_fusion.info_ref, bf16[3088,128]{1,0:T(8,128)(2,1)S(1)} %collective-permute-done.5.refs_0_, bf16[3088,128]{1,0:T(8,128)(2,1)S(1)} %collective-permute-done.6.refs_1_, bf16[3,3072,1024]{2,1,0:T(8,128)(2,1)} %bitcast.21, ...), custom_call_target="tpu_custom_call" | custom-call | flops 1207959552 | bytes 9437184 | tf_op jit(solution)/shard_map/project/pallas_call | solution.py:140
  69.9 3.8 %emit.6 = (bf16[64,3072]{1,0:T(8,128)(2,1)S(1)}, bf16[64,3072]{1,0:T(8,128)(2,1)S(1)}) custom-call(s32[4]{0:T(128)S(1)} %pad_add_fusion.info_ref, bf16[128,512]{1,0:T(8,128)(2,1)S(1)} %mix.6.refs_7_.mine_ref.refs_0_, bf16[128,512]{1,0:T(8,128)(2,1)S(1)} %collective-permute-done.4.theirs_ref.refs_1_, bf16[1024,3072]{1,0:T(8,128)(2,1)} %bitcast.24, ...), custom_call_target="tpu_custom_call" | custom-call | flops 805306368 | bytes 6291456 | tf_op jit(solution)/shard_map/emit/pallas_call | solution.py:324
  73.7 3.8 %emit.7 = (bf16[64,3072]{1,0:T(8,128)(2,1)S(1)}, bf16[64,3072]{1,0:T(8,128)(2,1)S(1)}) custom-call(s32[4]{0:T(128)S(1)} %pad_add_fusion.info_ref, bf16[128,512]{1,0:T(8,128)(2,1)S(1)} %mix.7.refs_3_.mine_ref.refs_2_, bf16[128,512]{1,0:T(8,128)(2,1)S(1)} %collective-permute-done.7.theirs_ref.refs_3_, bf16[1024,3072]{1,0:T(8,128)(2,1)} %bitcast.25, ...), custom_call_target="tpu_custom_call" | custom-call | flops 805306368 | bytes 6291456 | tf_op jit(solution)/shard_map/emit/pallas_call | solution.py:324
  77.5 4.9 %project.14.refs_3_ = bf16[144,1536]{1,0:T(8,128)(2,1)S(1)} custom-call(s32[4]{0:T(128)S(1)} %pad_add_fusion.info_ref, bf16[3088,128]{1,0:T(8,128)(2,1)S(1)} %collective-permute-done.9.refs_0_, bf16[3088,128]{1,0:T(8,128)(2,1)S(1)} %collective-permute-done.10.refs_1_, bf16[3,3072,1024]{2,1,0:T(8,128)(2,1)} %bitcast.22, ...), custom_call_target="tpu_custom_call" | custom-call | flops 1207959552 | bytes 9437184 | tf_op jit(solution)/shard_map/project/pallas_call | solution.py:140
  82.9 4.9 %project.15.refs_0_.refs_7_.refs_2_ = bf16[144,1536]{1,0:T(8,128)(2,1)S(1)} custom-call(s32[4]{0:T(128)S(1)} %pad_add_fusion.info_ref, bf16[3088,128]{1,0:T(8,128)(2,1)S(1)} %collective-permute-done.9.refs_0_, bf16[3088,128]{1,0:T(8,128)(2,1)S(1)} %collective-permute-done.10.refs_1_, bf16[3,3072,1024]{2,1,0:T(8,128)(2,1)} %bitcast.23, ...), custom_call_target="tpu_custom_call" | custom-call | flops 1207959552 | bytes 9437184 | tf_op jit(solution)/shard_map/project/pallas_call | solution.py:140
  87.9 1.7 %mix.8.refs_7_.mine_ref.refs_4_ = bf16[128,512]{1,0:T(8,128)(2,1)S(1)} custom-call(s32[4]{0:T(128)S(1)} %pad_add_fusion.info_ref, bf16[144,1536]{1,0:T(8,128)(2,1)S(1)} %project.15.refs_0_.refs_7_.refs_2_, bf16[144,1536]{1,0:T(8,128)(2,1)S(1)} %collective-permute-done.11.refs_1_.refs_3_, bf16[144,1536]{1,0:T(8,128)(2,1)S(1)} %project.13._.refs_2_.refs_0_, ...), custom_call_target="tpu_custom_call" | custom-call | flops 134217728 | bytes 2097152 | tf_op jit(solution)/shard_map/mix/pallas_call | solution.py:269
  91.0 3.8 %emit.8 = (bf16[64,3072]{1,0:T(8,128)(2,1)S(1)}, bf16[64,3072]{1,0:T(8,128)(2,1)S(1)}) custom-call(s32[4]{0:T(128)S(1)} %pad_add_fusion.info_ref, bf16[128,512]{1,0:T(8,128)(2,1)S(1)} %mix.8.refs_7_.mine_ref.refs_4_, bf16[128,512]{1,0:T(8,128)(2,1)S(1)} %collective-permute-done.12.theirs_ref.refs_5_, bf16[1024,3072]{1,0:T(8,128)(2,1)} %bitcast.26, ...), custom_call_target="tpu_custom_call" | custom-call | flops 805306368 | bytes 6291456 | tf_op jit(solution)/shard_map/emit/pallas_call | solution.py:324
  94.8 1.3 collective-permute-start.22
  96.1 1.9 %mix.10._.mine_ref.refs_8_ = bf16[128,512]{1,0:T(8,128)(2,1)S(1)} custom-call(s32[4]{0:T(128)S(1)} %pad_add_fusion.info_ref, bf16[144,1536]{1,0:T(8,128)(2,1)S(1)} %project.13._.refs_2_.refs_0_, bf16[144,1536]{1,0:T(8,128)(2,1)S(1)} %collective-permute-done.8.refs_3_.refs_1_, bf16[288,1536]{1,0:T(8,128)(2,1)S(1)} %project.11.refs_2_.refs_7_.refs_0_, ...), custom_call_target="tpu_custom_call" | custom-call | flops 134217728 | bytes 2097152 | tf_op jit(solution)/shard_map/mix/pallas_call | solution.py:269
  99.9 1.5 collective-permute-start.15
  101.4 3.8 %emit.10 = (bf16[64,3072]{1,0:T(8,128)(2,1)S(1)}, bf16[64,3072]{1,0:T(8,128)(2,1)S(1)}) custom-call(s32[4]{0:T(128)S(1)} %pad_add_fusion.info_ref, bf16[128,512]{1,0:T(8,128)(2,1)S(1)} %mix.10._.mine_ref.refs_8_, bf16[128,512]{1,0:T(8,128)(2,1)S(1)} %collective-permute-done.13.theirs_ref.refs_9_, bf16[1024,3072]{1,0:T(8,128)(2,1)} %bitcast.28, ...), custom_call_target="tpu_custom_call" | custom-call | flops 805306368 | bytes 6291456 | tf_op jit(solution)/shard_map/emit/pallas_call | solution.py:324
  105.2 0.7 emit.11
  106.0 4.4 %collective-permute-start.23 = (bf16[64,3072]{1,0:T(8,128)(2,1)S(1)}, bf16[64,3072]{1,0:T(8,128)(2,1)S(1)}, u32[]{:S(2)}, u32[]{:S(2)}) collective-permute-start(bf16[64,3072]{1,0:T(8,128)(2,1)S(1)} %get-tuple-element.29), channel_id=1, source_target_pairs={{0,4},{4,8},{1,5},{5,9},{2,6},{6,10},{3,7},{7,11},{16,20},{20,24},... | collective-permute-start | bytes 1179656 | tf_op jit(solution)/shard_map/ppermute | solution.py:477
  110.4 0.7 collective-permute-start.25
  111.1 2.9 %collective-permute-done.15 = bf16[64,3072]{1,0:T(8,128)(2,1)S(1)} collective-permute-done((bf16[64,3072]{1,0:T(8,128)(2,1)S(1)}, bf16[64,3072]{1,0:T(8,128)(2,1)S(1)}, u32[]{:S(2)}, u32[]{:S(2)}) %collective-permute-start.15) | collective-permute-done | bytes 393248 | tf_op jit(solution)/shard_map/ppermute | solution.py:477
  114.2 4.4 %collective-permute-start.16 = (bf16[64,3072]{1,0:T(8,128)(2,1)S(1)}, bf16[64,3072]{1,0:T(8,128)(2,1)S(1)}, u32[]{:S(2)}, u32[]{:S(2)}) collective-permute-start(bf16[64,3072]{1,0:T(8,128)(2,1)S(1)} %get-tuple-element.27), channel_id=1, source_target_pairs={{0,4},{4,8},{1,5},{5,9},{2,6},{6,10},{3,7},{7,11},{16,20},{20,24},... | collective-permute-start | bytes 1179656 | tf_op jit(solution)/shard_map/ppermute | solution.py:477
  118.6 0.7 collective-permute-start.19
  119.3 3.1 %collective-permute-done.23 = bf16[64,3072]{1,0:T(8,128)(2,1)S(1)} collective-permute-done((bf16[64,3072]{1,0:T(8,128)(2,1)S(1)}, bf16[64,3072]{1,0:T(8,128)(2,1)S(1)}, u32[]{:S(2)}, u32[]{:S(2)}) %collective-permute-start.23) | collective-permute-done | bytes 393248 | tf_op jit(solution)/shard_map/ppermute | solution.py:477
  122.5 4.4 %collective-permute-start.24 = (bf16[64,3072]{1,0:T(8,128)(2,1)S(1)}, bf16[64,3072]{1,0:T(8,128)(2,1)S(1)}, u32[]{:S(2)}, u32[]{:S(2)}) collective-permute-start(bf16[64,3072]{1,0:T(8,128)(2,1)S(1)} %add_convert_fusion.1), channel_id=1, source_target_pairs={{0,4},{4,8},{8,12},{1,5},{5,9},{9,13},{2,6},{6,10},{10,14},{3,7},{... | collective-permute-start | bytes 1179656 | tf_op jit(solution)/shard_map/ppermute | solution.py:477
  127.1 1.4 collective-permute-start.26
  128.5 2.4 %collective-permute-done.16 = bf16[64,3072]{1,0:T(8,128)(2,1)S(1)} collective-permute-done((bf16[64,3072]{1,0:T(8,128)(2,1)S(1)}, bf16[64,3072]{1,0:T(8,128)(2,1)S(1)}, u32[]{:S(2)}, u32[]{:S(2)}) %collective-permute-start.16) | collective-permute-done | bytes 393248 | tf_op jit(solution)/shard_map/ppermute | solution.py:477
  130.9 4.4 %collective-permute-start.17 = (bf16[64,3072]{1,0:T(8,128)(2,1)S(1)}, bf16[64,3072]{1,0:T(8,128)(2,1)S(1)}, u32[]{:S(2)}, u32[]{:S(2)}) collective-permute-start(bf16[64,3072]{1,0:T(8,128)(2,1)S(1)} %add_convert_fusion.3), channel_id=1, source_target_pairs={{0,4},{4,8},{8,12},{1,5},{5,9},{9,13},{2,6},{6,10},{10,14},{3,7},{... | collective-permute-start | bytes 1179656 | tf_op jit(solution)/shard_map/ppermute | solution.py:477
  135.5 1.3 collective-permute-start.20
  136.8 2.5 %collective-permute-done.24.refs_1_ = bf16[64,3072]{1,0:T(8,128)(2,1)S(1)} collective-permute-done((bf16[64,3072]{1,0:T(8,128)(2,1)S(1)}, bf16[64,3072]{1,0:T(8,128)(2,1)S(1)}, u32[]{:S(2)}, u32[]{:S(2)}) %collective-permute-start.24) | collective-permute-done | bytes 393248 | tf_op jit(solution)/shard_map/ppermute | solution.py:477
  139.5 1.6 collective-permute-start.27
  141.0 6.1 %collective-permute-done.17.refs_1_ = bf16[64,3072]{1,0:T(8,128)(2,1)S(1)} collective-permute-done((bf16[64,3072]{1,0:T(8,128)(2,1)S(1)}, bf16[64,3072]{1,0:T(8,128)(2,1)S(1)}, u32[]{:S(2)}, u32[]{:S(2)}) %collective-permute-start.17) | collective-permute-done | bytes 393248 | tf_op jit(solution)/shard_map/ppermute | solution.py:477
  147.5 1.6 collective-permute-start.21
  149.0 1.6 %readout.1 = bf16[64,1024]{1,0:T(8,128)(2,1)} custom-call(s32[4]{0:T(128)S(1)} %pad_add_fusion.info_ref, s32[1,64]{1,0:T(1,128)S(1)} %copy-done.6, bf16[128,512]{1,0:T(8,128)(2,1)S(1)} %mix.6.refs_7_.mine_ref.refs_0_, bf16[128,512]{1,0:T(8,128)(2,1)S(1)} %collective-permute-done.4.theirs_ref.refs_1_, bf16[128,512]{1,0:T(8,128)(2,1)S(1)} %mix.7.refs_3_.mine_ref.refs_2_, ...), custom_call_target="tpu_custom_call" | custom-call | flops 100663296 | tf_op jit(solution)/shard_map/readout/pallas_call | solution.py:384
  150.7 7.4 %collective-permute-done.21 = bf16[64,3072]{1,0:T(8,128)(2,1)S(1)} collective-permute-done((bf16[64,3072]{1,0:T(8,128)(2,1)S(1)}, bf16[64,3072]{1,0:T(8,128)(2,1)S(1)}, u32[]{:S(2)}, u32[]{:S(2)}) %collective-permute-start.21) | collective-permute-done | bytes 393248 | tf_op jit(solution)/shard_map/ppermute | solution.py:499
  158.0 0.9 maximum_bitcast_fusion
  (55 shorter events, 7.4 us)
Async XLA Ops:
  0.6 9.3 %copy-start = (bf16[512,256]{1,0:T(8,128)(2,1)S(1)}, bf16[512,256]{1,0:T(8,128)(2,1)}, u32[]{:S(2)}) copy-start(bf16[512,256]{1,0:T(8,128)(2,1)} %constant.30.forward_ref.refs_5_) | copy-start | bytes 786436
  0.6 1.2 copy-start.1
  1.8 0.7 copy-start.5
  2.5 7.4 %copy-start.4 = (bf16[1,1024,128]{2,1,0:T(8,128)(2,1)S(1)}, bf16[1,1024,128]{2,1,0:T(8,128)(2,1)}, u32[]{:S(2)}) copy-start(bf16[1,1024,128]{2,1,0:T(8,128)(2,1)} %param.14) | copy-start | bytes 786436
  3.0 21.8 %collective-permute-start.1 = (bf16[3088,128]{1,0:T(8,128)(2,1)S(1)}, bf16[3088,128]{1,0:T(8,128)(2,1)S(1)}, u32[]{:S(2)}, u32[]{:S(2)}) collective-permute-start(bf16[3088,128]{1,0:T(8,128)(2,1)S(1)} %prepare.1._.refs_0_), channel_id=1, source_target_pairs={{0,4},{4,8},{8,12},{1,5},{5,9},{9,13},{2,6},{6,10},{10,14},{3,7},{... | collective-permute-start | bytes 2371592 | tf_op jit(solution)/shard_map/ppermute | solution.py:425
  8.0 21.0 %collective-permute-start.2 = (bf16[3088,128]{1,0:T(8,128)(2,1)S(1)}, bf16[3088,128]{1,0:T(8,128)(2,1)S(1)}, u32[]{:S(2)}, u32[]{:S(2)}) collective-permute-start(bf16[3088,128]{1,0:T(8,128)(2,1)S(1)} %prepare.1._.refs_0_), channel_id=1, source_target_pairs={{4,0},{8,4},{12,8},{5,1},{9,5},{13,9},{6,2},{10,6},{14,10},{7,3},{... | collective-permute-start | bytes 2371592 | tf_op jit(solution)/shard_map/ppermute | solution.py:427
  24.8 16.4 %collective-permute-start.5 = (bf16[3088,128]{1,0:T(8,128)(2,1)S(1)}, bf16[3088,128]{1,0:T(8,128)(2,1)S(1)}, u32[]{:S(2)}, u32[]{:S(2)}) collective-permute-start(bf16[3088,128]{1,0:T(8,128)(2,1)S(1)} %collective-permute-done.1.refs_0_), channel_id=1, source_target_pairs={{4,8},{8,12},{5,9},{9,13},{6,10},{10,14},{7,11},{11,15},{20,24},{2... | collective-permute-start | bytes 2371592 | tf_op jit(solution)/shard_map/ppermute | solution.py:425
  29.0 20.2 %collective-permute-start.6 = (bf16[3088,128]{1,0:T(8,128)(2,1)S(1)}, bf16[3088,128]{1,0:T(8,128)(2,1)S(1)}, u32[]{:S(2)}, u32[]{:S(2)}) collective-permute-start(bf16[3088,128]{1,0:T(8,128)(2,1)S(1)} %collective-permute-done.2.refs_1_), channel_id=1, source_target_pairs={{4,0},{8,4},{5,1},{9,5},{6,2},{10,6},{7,3},{11,7},{20,16},{24,20},... | collective-permute-start | bytes 2371592 | tf_op jit(solution)/shard_map/ppermute | solution.py:427
  40.7 15.3 %copy-start.3 = (bf16[256,256]{1,0:T(8,128)(2,1)S(1)}, bf16[256,256]{1,0:T(8,128)(2,1)}, u32[]{:S(2)}) copy-start(bf16[256,256]{1,0:T(8,128)(2,1)} %constant.31.refs_6_) | copy-start | bytes 393220
  40.7 15.3 %collective-permute-start.3 = (bf16[288,1536]{1,0:T(8,128)(2,1)S(1)}, bf16[288,1536]{1,0:T(8,128)(2,1)S(1)}, u32[]{:S(2)}, u32[]{:S(2)}) collective-permute-start(bf16[288,1536]{1,0:T(8,128)(2,1)S(1)} %project.10.refs_3_), channel_id=1, source_target_pairs={{0,1},{1,0},{2,3},{3,2},{4,5},{5,4},{6,7},{7,6},{8,9},{9,8},{10,11... | collective-permute-start | bytes 2654216 | tf_op jit(solution)/shard_map/ppermute | solution.py:453
  40.7 15.2 %collective-permute-start = (bf16[144,1536]{1,0:T(8,128)(2,1)S(1)}, bf16[144,1536]{1,0:T(8,128)(2,1)S(1)}, u32[]{:S(2)}, u32[]{:S(2)}) collective-permute-start(bf16[144,1536]{1,0:T(8,128)(2,1)S(1)} %project.8.refs_2_), channel_id=1, source_target_pairs={{0,1},{1,0},{2,3},{3,2},{4,5},{5,4},{6,7},{7,6},{8,9},{9,8},{10,11... | collective-permute-start | bytes 1327112 | tf_op jit(solution)/shard_map/ppermute | solution.py:453
  41.2 36.2 %collective-permute-start.9 = (bf16[3088,128]{1,0:T(8,128)(2,1)S(1)}, bf16[3088,128]{1,0:T(8,128)(2,1)S(1)}, u32[]{:S(2)}, u32[]{:S(2)}) collective-permute-start(bf16[3088,128]{1,0:T(8,128)(2,1)S(1)} %collective-permute-done.5.refs_0_), channel_id=1, source_target_pairs={{8,12},{9,13},{10,14},{11,15},{24,28},{25,29},{26,30},{27,31}} | collective-permute-start | bytes 2371592 | tf_op jit(solution)/shard_map/ppermute | solution.py:425
  49.2 28.2 %collective-permute-start.10 = (bf16[3088,128]{1,0:T(8,128)(2,1)S(1)}, bf16[3088,128]{1,0:T(8,128)(2,1)S(1)}, u32[]{:S(2)}, u32[]{:S(2)}) collective-permute-start(bf16[3088,128]{1,0:T(8,128)(2,1)S(1)} %collective-permute-done.6.refs_1_), channel_id=1, source_target_pairs={{4,0},{5,1},{6,2},{7,3},{20,16},{21,17},{22,18},{23,19}} | collective-permute-start | bytes 2371592 | tf_op jit(solution)/shard_map/ppermute | solution.py:427
  57.6 12.3 %collective-permute-start.4 = (bf16[128,512]{1,0:T(8,128)(2,1)S(1)}, bf16[128,512]{1,0:T(8,128)(2,1)S(1)}, u32[]{:S(2)}, u32[]{:S(2)}) collective-permute-start(bf16[128,512]{1,0:T(8,128)(2,1)S(1)} %mix.6.refs_7_.mine_ref.refs_0_), channel_id=1, source_target_pairs={{0,1},{1,0},{2,3},{3,2},{4,5},{5,4},{6,7},{7,6},{8,9},{9,8},{10,11... | collective-permute-start | bytes 393224 | tf_op jit(solution)/shard_map/ppermute | solution.py:439
  59.4 14.3 %collective-permute-start.7 = (bf16[128,512]{1,0:T(8,128)(2,1)S(1)}, bf16[128,512]{1,0:T(8,128)(2,1)S(1)}, u32[]{:S(2)}, u32[]{:S(2)}) collective-permute-start(bf16[128,512]{1,0:T(8,128)(2,1)S(1)} %mix.7.refs_3_.mine_ref.refs_2_), channel_id=1, source_target_pairs={{0,1},{1,0},{2,3},{3,2},{4,5},{5,4},{6,7},{7,6},{8,9},{9,8},{10,11... | collective-permute-start | bytes 393224 | tf_op jit(solution)/shard_map/ppermute | solution.py:439
  64.9 23.0 %collective-permute-start.8 = (bf16[144,1536]{1,0:T(8,128)(2,1)S(1)}, bf16[144,1536]{1,0:T(8,128)(2,1)S(1)}, u32[]{:S(2)}, u32[]{:S(2)}) collective-permute-start(bf16[144,1536]{1,0:T(8,128)(2,1)S(1)} %project.12.refs_3_), channel_id=1, source_target_pairs={{0,1},{1,0},{2,3},{3,2},{4,5},{5,4},{6,7},{7,6},{8,9},{9,8},{10,11... | collective-permute-start | bytes 1327112 | tf_op jit(solution)/shard_map/ppermute | solution.py:453
  82.4 5.5 %collective-permute-start.11 = (bf16[144,1536]{1,0:T(8,128)(2,1)S(1)}, bf16[144,1536]{1,0:T(8,128)(2,1)S(1)}, u32[]{:S(2)}, u32[]{:S(2)}) collective-permute-start(bf16[144,1536]{1,0:T(8,128)(2,1)S(1)} %project.14.refs_3_), channel_id=1, source_target_pairs={{0,1},{1,0},{2,3},{3,2},{4,5},{5,4},{6,7},{7,6},{8,9},{9,8},{10,11... | collective-permute-start | bytes 1327112 | tf_op jit(solution)/shard_map/ppermute | solution.py:453
  89.6 1.4 collective-permute-start.12
  90.2 8.0 %collective-permute-start.14 = (bf16[128,512]{1,0:T(8,128)(2,1)S(1)}, bf16[128,512]{1,0:T(8,128)(2,1)S(1)}, u32[]{:S(2)}, u32[]{:S(2)}) collective-permute-start(bf16[128,512]{1,0:T(8,128)(2,1)S(1)} %mix.9._.mine_ref.refs_6_), channel_id=1, source_target_pairs={{0,1},{1,0},{2,3},{3,2},{4,5},{5,4},{6,7},{7,6},{8,9},{9,8},{10,11... | collective-permute-start | bytes 393224 | tf_op jit(solution)/shard_map/ppermute | solution.py:439
  94.8 11.1 %collective-permute-start.22 = (bf16[64,3072]{1,0:T(8,128)(2,1)S(1)}, bf16[64,3072]{1,0:T(8,128)(2,1)S(1)}, u32[]{:S(2)}, u32[]{:S(2)}) collective-permute-start(bf16[64,3072]{1,0:T(8,128)(2,1)S(1)} %get-tuple-element.23), channel_id=1, source_target_pairs={{0,4},{12,8},{1,5},{13,9},{2,6},{14,10},{3,7},{15,11},{16,20},{28,... | collective-permute-start | bytes 1179656 | tf_op jit(solution)/shard_map/ppermute | solution.py:477
  98.0 3.4 %collective-permute-start.13 = (bf16[128,512]{1,0:T(8,128)(2,1)S(1)}, bf16[128,512]{1,0:T(8,128)(2,1)S(1)}, u32[]{:S(2)}, u32[]{:S(2)}) collective-permute-start(bf16[128,512]{1,0:T(8,128)(2,1)S(1)} %mix.10._.mine_ref.refs_8_), channel_id=1, source_target_pairs={{0,1},{1,0},{2,3},{3,2},{4,5},{5,4},{6,7},{7,6},{8,9},{9,8},{10,11... | collective-permute-start | bytes 393224 | tf_op jit(solution)/shard_map/ppermute | solution.py:439
  99.5 5.7 %collective-permute-start.18 = (bf16[128,512]{1,0:T(8,128)(2,1)S(1)}, bf16[128,512]{1,0:T(8,128)(2,1)S(1)}, u32[]{:S(2)}, u32[]{:S(2)}) collective-permute-start(bf16[128,512]{1,0:T(8,128)(2,1)S(1)} %mix.11._.mine_ref.refs_10_), channel_id=1, source_target_pairs={{0,1},{1,0},{2,3},{3,2},{4,5},{5,4},{6,7},{7,6},{8,9},{9,8},{10,11... | collective-permute-start | bytes 393224 | tf_op jit(solution)/shard_map/ppermute | solution.py:439
  99.9 14.1 %collective-permute-start.15 = (bf16[64,3072]{1,0:T(8,128)(2,1)S(1)}, bf16[64,3072]{1,0:T(8,128)(2,1)S(1)}, u32[]{:S(2)}, u32[]{:S(2)}) collective-permute-start(bf16[64,3072]{1,0:T(8,128)(2,1)S(1)} %get-tuple-element.16.refs_7_), channel_id=1, source_target_pairs={{0,4},{12,8},{1,5},{13,9},{2,6},{14,10},{3,7},{15,11},{16,20},{28,... | collective-permute-start | bytes 1179656 | tf_op jit(solution)/shard_map/ppermute | solution.py:477
  106.0 16.4 %collective-permute-start.23 = (bf16[64,3072]{1,0:T(8,128)(2,1)S(1)}, bf16[64,3072]{1,0:T(8,128)(2,1)S(1)}, u32[]{:S(2)}, u32[]{:S(2)}) collective-permute-start(bf16[64,3072]{1,0:T(8,128)(2,1)S(1)} %get-tuple-element.29), channel_id=1, source_target_pairs={{0,4},{4,8},{1,5},{5,9},{2,6},{6,10},{3,7},{7,11},{16,20},{20,24},... | collective-permute-start | bytes 1179656 | tf_op jit(solution)/shard_map/ppermute | solution.py:477
  110.4 16.5 %collective-permute-start.25 = (bf16[64,3072]{1,0:T(8,128)(2,1)S(1)}, bf16[64,3072]{1,0:T(8,128)(2,1)S(1)}, u32[]{:S(2)}, u32[]{:S(2)}) collective-permute-start(bf16[64,3072]{1,0:T(8,128)(2,1)S(1)} %get-tuple-element.28), channel_id=1, source_target_pairs={{8,4},{12,8},{9,5},{13,9},{10,6},{14,10},{11,7},{15,11},{24,20},{2... | collective-permute-start | bytes 1179656 | tf_op jit(solution)/shard_map/ppermute | solution.py:477
  114.2 16.7 %collective-permute-start.16 = (bf16[64,3072]{1,0:T(8,128)(2,1)S(1)}, bf16[64,3072]{1,0:T(8,128)(2,1)S(1)}, u32[]{:S(2)}, u32[]{:S(2)}) collective-permute-start(bf16[64,3072]{1,0:T(8,128)(2,1)S(1)} %get-tuple-element.27), channel_id=1, source_target_pairs={{0,4},{4,8},{1,5},{5,9},{2,6},{6,10},{3,7},{7,11},{16,20},{20,24},... | collective-permute-start | bytes 1179656 | tf_op jit(solution)/shard_map/ppermute | solution.py:477
  118.6 16.8 %collective-permute-start.19 = (bf16[64,3072]{1,0:T(8,128)(2,1)S(1)}, bf16[64,3072]{1,0:T(8,128)(2,1)S(1)}, u32[]{:S(2)}, u32[]{:S(2)}) collective-permute-start(bf16[64,3072]{1,0:T(8,128)(2,1)S(1)} %get-tuple-element.26), channel_id=1, source_target_pairs={{8,4},{12,8},{9,5},{13,9},{10,6},{14,10},{11,7},{15,11},{24,20},{2... | collective-permute-start | bytes 1179656 | tf_op jit(solution)/shard_map/ppermute | solution.py:477
  122.5 16.8 %collective-permute-start.24 = (bf16[64,3072]{1,0:T(8,128)(2,1)S(1)}, bf16[64,3072]{1,0:T(8,128)(2,1)S(1)}, u32[]{:S(2)}, u32[]{:S(2)}) collective-permute-start(bf16[64,3072]{1,0:T(8,128)(2,1)S(1)} %add_convert_fusion.1), channel_id=1, source_target_pairs={{0,4},{4,8},{8,12},{1,5},{5,9},{9,13},{2,6},{6,10},{10,14},{3,7},{... | collective-permute-start | bytes 1179656 | tf_op jit(solution)/shard_map/ppermute | solution.py:477
  126.9 12.3 %copy-start.2 = (bf16[1,128,3072]{2,1,0:T(8,128)(2,1)S(1)}, bf16[1,128,3072]{2,1,0:T(8,128)(2,1)}, u32[]{:S(2)}) copy-start(bf16[1,128,3072]{2,1,0:T(8,128)(2,1)} %param.11) | copy-start | bytes 2359300
  127.1 12.2 %collective-permute-start.26 = (bf16[64,3072]{1,0:T(8,128)(2,1)S(1)}, bf16[64,3072]{1,0:T(8,128)(2,1)S(1)}, u32[]{:S(2)}, u32[]{:S(2)}) collective-permute-start(bf16[64,3072]{1,0:T(8,128)(2,1)S(1)} %add_convert_fusion), channel_id=1, source_target_pairs={{4,0},{8,4},{12,8},{5,1},{9,5},{13,9},{6,2},{10,6},{14,10},{7,3},{... | collective-permute-start | bytes 1179656 | tf_op jit(solution)/shard_map/ppermute | solution.py:477
  130.9 16.2 %collective-permute-start.17 = (bf16[64,3072]{1,0:T(8,128)(2,1)S(1)}, bf16[64,3072]{1,0:T(8,128)(2,1)S(1)}, u32[]{:S(2)}, u32[]{:S(2)}) collective-permute-start(bf16[64,3072]{1,0:T(8,128)(2,1)S(1)} %add_convert_fusion.3), channel_id=1, source_target_pairs={{0,4},{4,8},{8,12},{1,5},{5,9},{9,13},{2,6},{6,10},{10,14},{3,7},{... | collective-permute-start | bytes 1179656 | tf_op jit(solution)/shard_map/ppermute | solution.py:477
  135.5 11.8 %collective-permute-start.20 = (bf16[64,3072]{1,0:T(8,128)(2,1)S(1)}, bf16[64,3072]{1,0:T(8,128)(2,1)S(1)}, u32[]{:S(2)}, u32[]{:S(2)}) collective-permute-start(bf16[64,3072]{1,0:T(8,128)(2,1)S(1)} %add_convert_fusion.2), channel_id=1, source_target_pairs={{4,0},{8,4},{12,8},{5,1},{9,5},{13,9},{6,2},{10,6},{14,10},{7,3},{... | collective-permute-start | bytes 1179656 | tf_op jit(solution)/shard_map/ppermute | solution.py:477
  139.5 9.6 %copy-start.6 = (s32[1,64]{1,0:T(1,128)S(1)}, s32[1,64]{1,0:T(1,128)}, u32[]{:S(2)}) copy-start(s32[1,64]{1,0:T(1,128)} %needle_ref.1) | copy-start | bytes 772
  139.5 11.2 %collective-permute-start.27 = (bf16[64,3072]{1,0:T(8,128)(2,1)S(1)}, bf16[64,3072]{1,0:T(8,128)(2,1)S(1)}, u32[]{:S(2)}, u32[]{:S(2)}) collective-permute-start(bf16[64,3072]{1,0:T(8,128)(2,1)S(1)} %finish.3), channel_id=1, source_target_pairs={{0,2},{2,0},{1,3},{3,1},{4,6},{6,4},{5,7},{7,5},{8,10},{10,8},{9,1... | collective-permute-start | bytes 1179656 | tf_op jit(solution)/shard_map/ppermute | solution.py:499
  147.5 10.5 %collective-permute-start.21 = (bf16[64,3072]{1,0:T(8,128)(2,1)S(1)}, bf16[64,3072]{1,0:T(8,128)(2,1)S(1)}, u32[]{:S(2)}, u32[]{:S(2)}) collective-permute-start(bf16[64,3072]{1,0:T(8,128)(2,1)S(1)} %finish.2), channel_id=1, source_target_pairs={{0,2},{2,0},{1,3},{3,1},{4,6},{6,4},{5,7},{7,5},{8,10},{10,8},{9,1... | collective-permute-start | bytes 1179656 | tf_op jit(solution)/shard_map/ppermute | solution.py:499
